TPU v7x, 32 devices: a whole 2x2x4 slice. The times are simulated.
32 devices in a mesh: dp: 4 (over z), expert: 8 (over y, x, core).
Axes of the slice: x: 2, y: 2, z: 4, core: 2. Of those that a mesh axis runs over, the one named last changes fastest.
Arguments:
- tokens: bfloat16 [2, 8, 1024, 1024], P(None, 'expert', 'dp'), may hold values from -6 to 6
- cotangent: float32 [2, 8, 1024, 1024], P(None, 'expert', 'dp'), may hold values from -6 to 6
- routes: int32 [2, 8, 1024, 1], P(None, 'expert', 'dp'), may hold values from 0 to 7; in each aligned block of 256 rows (0 to 255, 256 to 511, ..., all dimensions but the last counted through in order) at most 40 rows name the same one
- prefix: int32 [2, 8], P(None, 'expert'), may hold values from 0 to 1024
- qkv_weight: bfloat16 [1024, 3072], P(('dp', 'expert')), may hold values from -0.25 to 0.25
- mix_weight: bfloat16 [1024, 1024], P(('dp', 'expert')), may hold values from -0.75 to 0.75
- up_weight: bfloat16 [1024, 4096], P(('dp', 'expert')), may hold values from -0.1875 to 0.1875
- down_weight: bfloat16 [4096, 1024], P(('dp', 'expert')), may hold values from -0.09375 to 0.09375
- dense_gain: bfloat16 [2, 1024], P(None, ('dp', 'expert')), may hold values from 0.5 to 1.5
- expert_up: bfloat16 [8, 2, 1024, 4096], P('expert', None, None, 'dp'), may hold values from -0.1875 to 0.1875
- expert_down: bfloat16 [8, 2, 4096, 1024], P('expert', None, 'dp'), may hold values from -0.09375 to 0.09375
- expert_gain: bfloat16 [8, 2, 1024], P('expert'), may hold values from 0.5 to 1.5
- centroids: bfloat16 [8, 1024], P('expert'), may hold values from -0.13085938 to 0.13085938
Outputs:
- outputs: bfloat16 [2, 8, 1024, 1024], P(None, 'expert', 'dp')
- input_grad: float32 [2, 8, 1024, 1024], P(None, 'expert', 'dp')
- qkv_grad: float32 [1024, 3072], P(('dp', 'expert'))
- mix_grad: float32 [1024, 1024], P(('dp', 'expert'))
- up_grad: float32 [1024, 4096], P(('dp', 'expert'))
- down_grad: float32 [4096, 1024], P(('dp', 'expert'))
- dense_gain_grad: float32 [2, 1024], P(None, ('dp', 'expert'))
- expert_up_grad: float32 [8, 2, 1024, 4096], P('expert', None, None, 'dp')
- expert_down_grad: float32 [8, 2, 4096, 1024], P('expert', None, 'dp')
- expert_gain_grad: float32 [8, 2, 1024], P('expert')
- centroid_grad: float32 [8, 1024], P('expert')
- branch_rms: float32 [4, 2, 8], P(None, None, 'expert')
Inputs may be any that keep to these rules, and one draw needn't show every extreme that they name: `routes`: in each aligned block of 256 rows (one sequence's tokens on one index of dp) no expert is named by more than 40 rows, a bound that some block reaches.
All inputs are finite; a program needn't handle non-finite values.
Results may differ from a plain program's by a relative error of at most 0.018.
Values may be sent and summed in bfloat16 or wider, within the bound.
No kernel may reach another device: no remote copies, remote signals or barrier semaphores. Data moves between devices by JAX's collectives and lax.ppermute only.
A program may use at most 384 MiB of HBM per device.

v0:
```python
import jax
import jax.numpy as jnp
from jax import lax
from jax.sharding import PartitionSpec as P

HEAD_DIM = 64


eps = 1e-05


def layer_norm(values, gain):
    centred = values - jnp.mean(values, -1, keepdims=True)
    spread = jnp.mean(centred * centred, -1, keepdims=True)
    return centred * lax.rsqrt(spread + eps) * gain


def norm_back(values, gain, grads):
    _, pullback = jax.vjp(layer_norm, values, gain)
    return pullback(grads)


def gelu(values):
    return jax.nn.gelu(values, approximate=True)


def gelu_back(values, grads):
    _, pullback = jax.vjp(gelu, values)
    return pullback(grads)[0]


def contract_rows(left, right):
    return lax.dot_general(
        left, right, (((0,), (0,)), ((), ())), preferred_element_type=jnp.float32
    )


def contract_cols(left, right):
    return lax.dot_general(
        left, right, (((1,), (1,)), ((), ())), preferred_element_type=jnp.float32
    )


def expert_forward(rows, gain, w_first, w_second, centroid):
    state = rows.astype(jnp.float32)
    score = jnp.dot(rows, centroid, preferred_element_type=jnp.float32)
    kept = []
    for layer in range(2):
        normed = layer_norm(state, gain[layer].astype(jnp.float32)).astype(jnp.bfloat16)
        gathered = lax.all_gather(normed, "dp", axis=0, tiled=True)
        pre = jnp.dot(gathered, w_first[layer], preferred_element_type=jnp.float32)
        hidden = gelu(pre).astype(jnp.bfloat16)
        partial_out = jnp.dot(hidden, w_second[layer], preferred_element_type=jnp.float32)
        added = lax.psum_scatter(
            partial_out.astype(jnp.bfloat16), "dp", scatter_dimension=0, tiled=True
        ).astype(jnp.float32)
        kept.append((state, gathered, pre, hidden))
        state = state + added
    gated = (jax.nn.sigmoid(score)[:, None] * state).astype(jnp.bfloat16)
    return (gated, (kept, state, score))


def expert_backward(grad_rows, rows, gain, w_first, w_second, centroid, saved):
    kept, state, score = saved
    incoming = grad_rows.astype(jnp.float32)
    sig = jax.nn.sigmoid(score)
    score_grad = jnp.sum(incoming * state, 1) * sig * (1.0 - sig)
    carried = incoming * sig[:, None]
    up_grads = [None, None]
    down_grads = [None, None]
    gain_grads = [None, None]
    for layer in (1, 0):
        before, gathered, pre, hidden = kept[layer]
        out_grad = lax.all_gather(carried.astype(jnp.bfloat16), "dp", axis=0, tiled=True)
        down_grads[layer] = contract_rows(hidden, out_grad)
        hidden_grad = contract_cols(out_grad, w_second[layer])
        pre_grad = gelu_back(pre, hidden_grad).astype(jnp.bfloat16)
        up_grads[layer] = contract_rows(gathered, pre_grad)
        normed_part = contract_cols(pre_grad, w_first[layer])
        normed_grad = lax.psum_scatter(
            normed_part.astype(jnp.bfloat16), "dp", scatter_dimension=0, tiled=True
        ).astype(jnp.float32)
        state_grad, gain_grad = norm_back(before, gain[layer].astype(jnp.float32), normed_grad)
        gain_grads[layer] = gain_grad
        carried = carried + state_grad
    input_grad = carried + score_grad[:, None] * centroid.astype(jnp.float32)[None, :]
    centroid_grad = jnp.sum(score_grad[:, None] * rows.astype(jnp.float32), 0)
    return (
        input_grad.astype(jnp.bfloat16),
        jnp.stack(up_grads),
        jnp.stack(down_grads),
        jnp.stack(gain_grads),
        centroid_grad,
    )


def shards(
    tokens,
    cotangent,
    routes,
    prefix,
    qkv_weight,
    mix_weight,
    up_weight,
    down_weight,
    dense_gain,
    expert_up,
    expert_down,
    expert_gain,
    centroids,
):
    micro_count, _, rows_dev, width = tokens.shape
    dp_count = lax.axis_size("dp")
    experts = lax.axis_size("expert")
    capacity = max(2, 5 * rows_dev // (4 * experts))
    length = rows_dev * dp_count
    heads = width // HEAD_DIM
    scale = HEAD_DIM ** (-0.5)
    query_pos = lax.axis_index("dp") * rows_dev + jnp.arange(rows_dev, dtype=jnp.int32)
    key_pos = jnp.arange(length, dtype=jnp.int32)
    slot_ids = jnp.arange(experts * capacity, dtype=jnp.int32)
    expert_ids = jnp.arange(experts, dtype=jnp.int32)
    full_qkv, full_mix, full_up, full_down, full_gain = (
        lax.all_gather(qkv_weight, ("dp", "expert"), axis=0, tiled=True),
        lax.all_gather(mix_weight, ("dp", "expert"), axis=0, tiled=True),
        lax.all_gather(up_weight, ("dp", "expert"), axis=0, tiled=True),
        lax.all_gather(down_weight, ("dp", "expert"), axis=0, tiled=True),
        lax.all_gather(dense_gain, ("dp", "expert"), axis=1, tiled=True),
    )
    gains = full_gain.astype(jnp.float32)

    def scores_of(query, keys, allowed):
        raw = jnp.einsum("thd,lhd->htl", query, keys, preferred_element_type=jnp.float32) * scale
        return jnp.where(allowed[None], raw, -1e30)

    stash = []
    stat_list = []
    output_list = []
    for micro in range(micro_count):
        inputs = tokens[micro, 0].astype(jnp.float32)
        normed = layer_norm(inputs, gains[0]).astype(jnp.bfloat16)
        qkv = jnp.dot(normed, full_qkv, preferred_element_type=jnp.float32).astype(jnp.bfloat16)
        query = qkv[:, :width].reshape(rows_dev, heads, HEAD_DIM)
        key_value = lax.all_gather(qkv[:, width:], "dp", axis=0, tiled=True)
        keys = key_value[:, :width].reshape(length, heads, HEAD_DIM)
        values = key_value[:, width:].reshape(length, heads, HEAD_DIM)
        allowed = (key_pos[None, :] <= query_pos[:, None]) | (key_pos[None, :] < prefix[micro, 0])
        scores = scores_of(query, keys, allowed)
        row_max = jnp.max(scores, -1, keepdims=True)
        log_total = jnp.log(jnp.sum(jnp.exp(scores - row_max), -1, keepdims=True)) + row_max
        probs_low = jnp.exp(scores - log_total).astype(jnp.bfloat16)
        mixed = jnp.einsum("htl,lhd->thd", probs_low, values, preferred_element_type=jnp.float32)
        mixed = mixed.reshape(rows_dev, width).astype(jnp.bfloat16)
        attn = jnp.dot(mixed, full_mix, preferred_element_type=jnp.float32)
        resid = inputs + attn
        normed2 = layer_norm(resid, gains[1]).astype(jnp.bfloat16)
        pre = jnp.dot(normed2, full_up, preferred_element_type=jnp.float32)
        hidden = gelu(pre).astype(jnp.bfloat16)
        ffn = jnp.dot(hidden, full_down, preferred_element_type=jnp.float32)
        after = resid + ffn
        route = routes[micro, 0, :, 0]
        onehot = (route[:, None] == expert_ids[None, :]).astype(jnp.int32)
        rank = jnp.sum((jnp.cumsum(onehot, 0) - 1) * onehot, 1)
        slot = route * capacity + rank
        place = (slot[None, :] == slot_ids[:, None]).astype(jnp.bfloat16)
        sent = jnp.dot(
            place, after.astype(jnp.bfloat16), preferred_element_type=jnp.float32
        ).astype(jnp.bfloat16)
        rows = lax.all_to_all(
            sent.reshape(experts, capacity, width),
            "expert",
            split_axis=0,
            concat_axis=0,
            tiled=True,
        ).reshape(experts * capacity, width)
        gated, saved = expert_forward(
            rows, expert_gain[0], expert_up[0], expert_down[0], centroids[0]
        )
        returned = lax.all_to_all(
            gated.reshape(experts, capacity, width),
            "expert",
            split_axis=0,
            concat_axis=0,
            tiled=True,
        ).reshape(experts * capacity, width)
        branch = contract_rows(place, returned)
        final = after + branch
        output_list.append(final.astype(jnp.bfloat16))
        stat_list.append(
            jnp.stack(
                [
                    jnp.sum(final * final),
                    jnp.sum(attn * attn),
                    jnp.sum(ffn * ffn),
                    jnp.sum(branch * branch),
                ]
            )
        )
        stash.append(
            (
                inputs,
                normed,
                query,
                keys,
                values,
                allowed,
                log_total,
                mixed,
                resid,
                normed2,
                pre,
                hidden,
                place,
                rows,
                saved,
            )
        )
    back_qkv, back_mix, back_up, back_down, back_gain = (
        lax.all_gather(qkv_weight, ("dp", "expert"), axis=0, tiled=True),
        lax.all_gather(mix_weight, ("dp", "expert"), axis=0, tiled=True),
        lax.all_gather(up_weight, ("dp", "expert"), axis=0, tiled=True),
        lax.all_gather(down_weight, ("dp", "expert"), axis=0, tiled=True),
        lax.all_gather(dense_gain, ("dp", "expert"), axis=1, tiled=True),
    )
    back_gains = back_gain.astype(jnp.float32)
    ex_up_acc = jnp.zeros(expert_up.shape[1:], jnp.float32)
    ex_down_acc = jnp.zeros(expert_down.shape[1:], jnp.float32)
    ex_gain_acc = jnp.zeros((2, width), jnp.float32)
    cent_acc = jnp.zeros((width,), jnp.float32)
    gain_acc = jnp.zeros((2, width), jnp.float32)
    input_grads = []
    (
        normed_rows,
        qkv_grad_rows,
        mixed_rows,
        attn_rows,
        normed2_rows,
        pre_grad_rows,
        hidden_rows,
        ffn_rows,
    ) = ([], [], [], [], [], [], [], [])
    for micro in range(micro_count):
        (
            inputs,
            normed,
            query,
            keys,
            values,
            allowed,
            log_total,
            mixed,
            resid,
            normed2,
            pre,
            hidden,
            place,
            rows,
            saved,
        ) = stash[micro]
        upstream = cotangent[micro, 0]
        upstream_low = upstream.astype(jnp.bfloat16)
        grad_sent = jnp.dot(place, upstream_low, preferred_element_type=jnp.float32).astype(
            jnp.bfloat16
        )
        grad_rows = lax.all_to_all(
            grad_sent.reshape(experts, capacity, width),
            "expert",
            split_axis=0,
            concat_axis=0,
            tiled=True,
        ).reshape(experts * capacity, width)
        row_grad, up_part, down_part, gain_part, cent_part = expert_backward(
            grad_rows, rows, expert_gain[0], expert_up[0], expert_down[0], centroids[0], saved
        )
        ex_up_acc = ex_up_acc + up_part
        ex_down_acc = ex_down_acc + down_part
        ex_gain_acc = ex_gain_acc + gain_part
        cent_acc = cent_acc + cent_part
        grad_back = lax.all_to_all(
            row_grad.reshape(experts, capacity, width),
            "expert",
            split_axis=0,
            concat_axis=0,
            tiled=True,
        ).reshape(experts * capacity, width)
        after_grad = upstream + contract_rows(place, grad_back)
        ffn_low = after_grad.astype(jnp.bfloat16)
        hidden_grad = contract_cols(ffn_low, back_down)
        pre_grad = gelu_back(pre, hidden_grad).astype(jnp.bfloat16)
        normed2_grad = contract_cols(pre_grad, back_up)
        resid_part, gain2_grad = norm_back(resid, back_gains[1], normed2_grad)
        resid_grad = after_grad + resid_part
        attn_low = resid_grad.astype(jnp.bfloat16)
        mixed_grad = (
            contract_cols(attn_low, back_mix)
            .astype(jnp.bfloat16)
            .reshape(rows_dev, heads, HEAD_DIM)
        )
        probs = jnp.exp(scores_of(query, keys, allowed) - log_total)
        probs_back = probs.astype(jnp.bfloat16)
        prob_grad = jnp.einsum(
            "thd,lhd->htl", mixed_grad, values, preferred_element_type=jnp.float32
        )
        inner = jnp.sum(probs * prob_grad, -1, keepdims=True)
        score_grad = (probs * (prob_grad - inner)).astype(jnp.bfloat16)
        query_grad = (
            jnp.einsum("htl,lhd->thd", score_grad, keys, preferred_element_type=jnp.float32) * scale
        )
        key_grad = (
            jnp.einsum("htl,thd->lhd", score_grad, query, preferred_element_type=jnp.float32)
            * scale
        )
        value_grad = jnp.einsum(
            "htl,thd->lhd", probs_back, mixed_grad, preferred_element_type=jnp.float32
        )
        both_grads = jnp.concatenate(
            [key_grad.reshape(length, width), value_grad.reshape(length, width)], 1
        )
        own_grads = lax.psum_scatter(
            both_grads.astype(jnp.bfloat16), "dp", scatter_dimension=0, tiled=True
        ).astype(jnp.float32)
        qkv_grad = jnp.concatenate([query_grad.reshape(rows_dev, width), own_grads], 1).astype(
            jnp.bfloat16
        )
        normed_grad = contract_cols(qkv_grad, back_qkv)
        input_part, gain1_grad = norm_back(inputs, back_gains[0], normed_grad)
        input_grads.append(resid_grad + input_part)
        gain_acc = gain_acc + jnp.stack([gain1_grad, gain2_grad])
        normed_rows.append(normed)
        qkv_grad_rows.append(qkv_grad)
        mixed_rows.append(mixed)
        attn_rows.append(attn_low)
        normed2_rows.append(normed2)
        pre_grad_rows.append(pre_grad)
        hidden_rows.append(hidden)
        ffn_rows.append(ffn_low)
    qkv_acc = contract_rows(jnp.concatenate(normed_rows, 0), jnp.concatenate(qkv_grad_rows, 0))
    mix_acc = contract_rows(jnp.concatenate(mixed_rows, 0), jnp.concatenate(attn_rows, 0))
    up_acc = contract_rows(jnp.concatenate(normed2_rows, 0), jnp.concatenate(pre_grad_rows, 0))
    down_acc = contract_rows(jnp.concatenate(hidden_rows, 0), jnp.concatenate(ffn_rows, 0))
    qkv_out, mix_out, up_out, down_out, gain_out = (
        lax.psum_scatter(qkv_acc, ("dp", "expert"), scatter_dimension=0, tiled=True),
        lax.psum_scatter(mix_acc, ("dp", "expert"), scatter_dimension=0, tiled=True),
        lax.psum_scatter(up_acc, ("dp", "expert"), scatter_dimension=0, tiled=True),
        lax.psum_scatter(down_acc, ("dp", "expert"), scatter_dimension=0, tiled=True),
        lax.psum_scatter(gain_acc, ("dp", "expert"), scatter_dimension=1, tiled=True),
    )
    stat_sums, ex_gain_sum, cent_sum = lax.psum(
        (jnp.stack(stat_list, 1), ex_gain_acc, cent_acc), "dp"
    )
    branch_rms = jnp.sqrt(stat_sums / (length * width)).reshape(4, micro_count, 1)
    outputs = jnp.stack(output_list)[:, None]
    input_grad = jnp.stack(input_grads)[:, None]
    return (
        outputs,
        input_grad,
        qkv_out,
        mix_out,
        up_out,
        down_out,
        gain_out,
        ex_up_acc[None],
        ex_down_acc[None],
        ex_gain_sum[None],
        cent_sum[None],
        branch_rms,
    )


def solution(mesh):
    return jax.shard_map(
        shards,
        mesh=mesh,
        in_specs=(
            P(None, "expert", "dp", None),
            P(None, "expert", "dp", None),
            P(None, "expert", "dp", None),
            P(None, "expert"),
            P(("dp", "expert"), None),
            P(("dp", "expert"), None),
            P(("dp", "expert"), None),
            P(("dp", "expert"), None),
            P(None, ("dp", "expert")),
            P("expert", None, None, "dp"),
            P("expert", None, "dp", None),
            P("expert", None, None),
            P("expert", None),
        ),
        out_specs=(
            P(None, "expert", "dp", None),
            P(None, "expert", "dp", None),
            P(("dp", "expert"), None),
            P(("dp", "expert"), None),
            P(("dp", "expert"), None),
            P(("dp", "expert"), None),
            P(None, ("dp", "expert")),
            P("expert", None, None, "dp"),
            P("expert", None, "dp", None),
            P("expert", None, None),
            P("expert", None),
            P(None, None, "expert"),
        ),
        check_vma=False,
    )
```

profile of v0, /device:TPU:0, one launch (start us, length us, event | category | flops | bytes accessed | tf_op | source)
XLA Modules:
  0.0 2484.2 jit_solution(7647835267204220900)
XLA Ops:
  8.0 43.5 %all-gather = bf16[32,32,2]{1,2,0:T(2,128)(2,1)S(1)} all-gather(bf16[1,32,2]{1,2,0:T(2,128)(2,1)} %bitcast.443), channel_id=1, replica_groups=mesh['dp'=4,'expert'=8] {'dp','expert'}, dimensions={0}, use_global_device_ids=true | all-gather | bytes 4224 | tf_op jit(solution)/shard_map/all_gather | solution.py:128
  56.9 25.9 %all-gather.16.cloned.1.call-done = bf16[1024,3072]{1,0:T(8,128)(2,1)} async-done(((bf16[32,3072]{1,0:T(8,128)(2,1)}), bf16[1024,3072]{1,0:T(8,128)(2,1)}) %all-gather.16.cloned.1.call-update) | async-done | bytes 6291472 | tf_op jit(solution)/shard_map/all_gather | solution.py:124
  103.7 64.2 %all-gather.18.cloned.1.call-done = bf16[1024,2048]{1,0:T(8,128)(2,1)} async-done(((bf16[256,2048]{1,0:T(8,128)(2,1)}), bf16[1024,2048]{1,0:T(8,128)(2,1)}) %all-gather.18.cloned.1.call-update) | async-done | bytes 4194320 | tf_op jit(solution)/shard_map/all_gather | solution.py:144
  175.5 73.8 %all-gather.30.cloned.1.call-done = bf16[1024,2048]{1,0:T(8,128)(2,1)} async-done(((bf16[256,2048]{1,0:T(8,128)(2,1)}), bf16[1024,2048]{1,0:T(8,128)(2,1)}) %all-gather.30.cloned.1.call-update) | async-done | bytes 4194320 | tf_op jit(solution)/shard_map/all_gather | solution.py:144
  320.1 65.3 %all-gather.22.cloned.1.call-done = bf16[1024,4096]{1,0:T(8,128)(2,1)} async-done(((bf16[32,4096]{1,0:T(8,128)(2,1)}), bf16[1024,4096]{1,0:T(8,128)(2,1)}) %all-gather.22.cloned.1.call-update) | async-done | bytes 8388624 | tf_op jit(solution)/shard_map/all_gather | solution.py:126
  394.6 69.2 %all-gather.24.cloned.1.call-done = bf16[4096,1024]{1,0:T(8,128)(2,1)} async-done(((bf16[128,1024]{1,0:T(8,128)(2,1)}), bf16[4096,1024]{1,0:T(8,128)(2,1)}) %all-gather.24.cloned.1.call-update) | async-done | bytes 8388624 | tf_op jit(solution)/shard_map/all_gather | solution.py:127
  513.1 51.8 %all-gather.32.cloned.1.call-done = bf16[1280,1024]{1,0:T(8,128)(2,1)} async-done(((bf16[320,1024]{1,0:T(8,128)(2,1)}), bf16[1280,1024]{1,0:T(8,128)(2,1)}) %all-gather.32.cloned.1.call-update) | async-done | bytes 2621456 | tf_op jit(solution)/shard_map/all_gather | solution.py:50
  577.5 42.5 %all-gather.26.cloned.1.call-done = bf16[1280,1024]{1,0:T(8,128)(2,1)} async-done(((bf16[320,1024]{1,0:T(8,128)(2,1)}), bf16[1280,1024]{1,0:T(8,128)(2,1)}) %all-gather.26.cloned.1.call-update) | async-done | bytes 2621456 | tf_op jit(solution)/shard_map/all_gather | solution.py:50
  632.4 41.0 %reduce-scatter.22.cloned.1.call-done = bf16[320,1024]{1,0:T(8,128)(2,1)} async-done(((bf16[1280,1024]{1,0:T(8,128)(2,1)}), bf16[320,1024]{1,0:T(8,128)(2,1)}) %reduce-scatter.22.cloned.1.call-update) | async-done | bytes 655376 | tf_op jit(solution)/shard_map/reduce_scatter | solution.py:54
  676.2 51.1 %reduce-scatter.18.cloned.1.call-done = bf16[320,1024]{1,0:T(8,128)(2,1)} async-done(((bf16[1280,1024]{1,0:T(8,128)(2,1)}), bf16[320,1024]{1,0:T(8,128)(2,1)}) %reduce-scatter.18.cloned.1.call-update) | async-done | bytes 655376 | tf_op jit(solution)/shard_map/reduce_scatter | solution.py:54
  770.1 17.3 all-gather.34.cloned.1.call-done
  800.2 42.1 %all-gather.40.cloned.1.call-done = bf16[1280,1024]{1,0:T(8,128)(2,1)} async-done(((bf16[320,1024]{1,0:T(8,128)(2,1)}), bf16[1280,1024]{1,0:T(8,128)(2,1)}) %all-gather.40.cloned.1.call-update) | async-done | bytes 2621456 | tf_op jit(solution)/shard_map/all_gather | solution.py:74
  857.3 40.2 %all-gather.28.cloned.1.call-done = bf16[1280,1024]{1,0:T(8,128)(2,1)} async-done(((bf16[320,1024]{1,0:T(8,128)(2,1)}), bf16[1280,1024]{1,0:T(8,128)(2,1)}) %all-gather.28.cloned.1.call-update) | async-done | bytes 2621456 | tf_op jit(solution)/shard_map/all_gather | solution.py:50
  910.0 42.4 %all-gather.36.cloned.1.call-done = bf16[1280,1024]{1,0:T(8,128)(2,1)} async-done(((bf16[320,1024]{1,0:T(8,128)(2,1)}), bf16[1280,1024]{1,0:T(8,128)(2,1)}) %all-gather.36.cloned.1.call-update) | async-done | bytes 2621456 | tf_op jit(solution)/shard_map/all_gather | solution.py:74
  967.3 38.3 %reduce-scatter.24.cloned.1.call-done = bf16[320,1024]{1,0:T(8,128)(2,1)} async-done(((bf16[1280,1024]{1,0:T(8,128)(2,1)}), bf16[320,1024]{1,0:T(8,128)(2,1)}) %reduce-scatter.24.cloned.1.call-update) | async-done | bytes 655376 | tf_op jit(solution)/shard_map/reduce_scatter | solution.py:54
  1005.6 54.0 %reduce-scatter.32.cloned.1.call-done = bf16[320,1024]{1,0:T(8,128)(2,1)} async-done(((bf16[1280,1024]{1,0:T(8,128)(2,1)}), bf16[320,1024]{1,0:T(8,128)(2,1)}) %reduce-scatter.32.cloned.1.call-update) | async-done | bytes 655376 | tf_op jit(solution)/shard_map/reduce_scatter | solution.py:80
  1059.6 54.0 %reduce-scatter.20.cloned.1.call-done = bf16[320,1024]{1,0:T(8,128)(2,1)} async-done(((bf16[1280,1024]{1,0:T(8,128)(2,1)}), bf16[320,1024]{1,0:T(8,128)(2,1)}) %reduce-scatter.20.cloned.1.call-update) | async-done | bytes 655376 | tf_op jit(solution)/shard_map/reduce_scatter | solution.py:54
  1113.6 54.0 %reduce-scatter.26.cloned.1.call-done = bf16[320,1024]{1,0:T(8,128)(2,1)} async-done(((bf16[1280,1024]{1,0:T(8,128)(2,1)}), bf16[320,1024]{1,0:T(8,128)(2,1)}) %reduce-scatter.26.cloned.1.call-update) | async-done | bytes 655376 | tf_op jit(solution)/shard_map/reduce_scatter | solution.py:80
  1181.4 52.8 %all-gather.38.cloned.1.call-done = bf16[1280,1024]{1,0:T(8,128)(2,1)} async-done(((bf16[320,1024]{1,0:T(8,128)(2,1)}), bf16[1280,1024]{1,0:T(8,128)(2,1)}) %all-gather.38.cloned.1.call-update) | async-done | bytes 2621456 | tf_op jit(solution)/shard_map/all_gather | solution.py:74
  1249.2 40.0 %all-gather.42.cloned.1.call-done = bf16[1280,1024]{1,0:T(8,128)(2,1)} async-done(((bf16[320,1024]{1,0:T(8,128)(2,1)}), bf16[1280,1024]{1,0:T(8,128)(2,1)}) %all-gather.42.cloned.1.call-update) | async-done | bytes 2621456 | tf_op jit(solution)/shard_map/all_gather | solution.py:74
  1304.1 38.4 %reduce-scatter.28.cloned.1.call-done = bf16[320,1024]{1,0:T(8,128)(2,1)} async-done(((bf16[1280,1024]{1,0:T(8,128)(2,1)}), bf16[320,1024]{1,0:T(8,128)(2,1)}) %reduce-scatter.28.cloned.1.call-update) | async-done | bytes 655376 | tf_op jit(solution)/shard_map/reduce_scatter | solution.py:80
  1344.0 52.6 %reduce-scatter.34.cloned.1.call-done = bf16[320,1024]{1,0:T(8,128)(2,1)} async-done(((bf16[1280,1024]{1,0:T(8,128)(2,1)}), bf16[320,1024]{1,0:T(8,128)(2,1)}) %reduce-scatter.34.cloned.1.call-update) | async-done | bytes 655376 | tf_op jit(solution)/shard_map/reduce_scatter | solution.py:80
  1476.2 13.1 multiply_reduce_fusion
  1489.3 12.0 multiply_convert_fusion
  1513.7 13.2 multiply_reduce_fusion.1
  1527.0 12.8 multiply_convert_fusion.1
  1587.2 74.2 %reduce-scatter.30.cloned.1.call-done = bf16[256,2048]{0,1:T(8,128)(2,1)} async-done(((bf16[1024,2048]{0,1:T(8,128)(2,1)}), bf16[256,2048]{0,1:T(8,128)(2,1)}) %reduce-scatter.30.cloned.1.call-update) | async-done | bytes 1048592 | tf_op jit(solution)/shard_map/reduce_scatter | solution.py:319
  1792.4 18.7 all-reduce
  1817.1 130.7 %reduce-scatter.40.cloned.1.call-done = f32[32,1024]{1,0:T(8,128)} async-done(((f32[1024,1024]{1,0:T(8,128)}), f32[32,1024]{1,0:T(8,128)}) %reduce-scatter.40.cloned.1.call-update) | async-done | bytes 131088 | tf_op jit(solution)/shard_map/reduce_scatter | solution.py:343
  1947.8 157.2 %reduce-scatter.38.cloned.1.call-done = f32[32,3072]{1,0:T(8,128)} async-done(((f32[1024,3072]{1,0:T(8,128)}), f32[32,3072]{1,0:T(8,128)}) %reduce-scatter.38.cloned.1.call-update) | async-done | bytes 393232 | tf_op jit(solution)/shard_map/reduce_scatter | solution.py:342
  2105.1 184.7 %reduce-scatter.42.cloned.1.call-done = f32[32,4096]{1,0:T(8,128)} async-done(((f32[1024,4096]{1,0:T(8,128)}), f32[32,4096]{1,0:T(8,128)}) %reduce-scatter.42.cloned.1.call-update) | async-done | bytes 524304 | tf_op jit(solution)/shard_map/reduce_scatter | solution.py:344
  2289.7 187.5 %reduce-scatter.44.cloned.1.call-done = f32[128,1024]{1,0:T(8,128)} async-done(((f32[4096,1024]{1,0:T(8,128)}), f32[128,1024]{1,0:T(8,128)}) %reduce-scatter.44.cloned.1.call-update) | async-done | bytes 524304 | tf_op jit(solution)/shard_map/reduce_scatter | solution.py:345
  (614 shorter events, 608.8 us)
Async XLA Ops:
  7.2 75.6 %all-gather.16.cloned.1.call-start = ((), (), s32[]{:S(2)}) async-start(), calls=%async_computation.23 | async-start | bytes 6488064 | tf_op jit(solution)/shard_map/all_gather | solution.py:124
  7.9 160.0 %all-gather.18.cloned.1.call-start = ((), (), s32[]{:S(2)}) async-start(), calls=%async_computation.24 | async-start | bytes 5242880 | tf_op jit(solution)/shard_map/all_gather | solution.py:144
  88.5 160.8 %all-gather.30.cloned.1.call-start = ((), (), s32[]{:S(2)}) async-start(), calls=%async_computation.32 | async-start | bytes 5242880 | tf_op jit(solution)/shard_map/all_gather | solution.py:144
  95.4 211.3 %all-gather.20.cloned.1.call-start = ((), (), s32[]{:S(2)}) async-start(), calls=%async_computation.25 | async-start | bytes 2162688 | tf_op jit(solution)/shard_map/all_gather | solution.py:125
  96.0 289.4 %all-gather.22.cloned.1.call-start = ((), (), s32[]{:S(2)}) async-start(), calls=%async_computation.26 | async-start | bytes 8650752 | tf_op jit(solution)/shard_map/all_gather | solution.py:126
  96.6 367.2 %all-gather.24.cloned.1.call-start = ((), (), s32[]{:S(2)}) async-start(), calls=%async_computation.27 | async-start | bytes 8650752 | tf_op jit(solution)/shard_map/all_gather | solution.py:127
  473.1 21.6 all-to-all-start
  498.9 66.0 %all-gather.32.cloned.1.call-start = ((), (), s32[]{:S(2)}) async-start(), calls=%async_computation.33 | async-start | bytes 3276800 | tf_op jit(solution)/shard_map/all_gather | solution.py:50
  512.3 107.7 %all-gather.26.cloned.1.call-start = ((), (), s32[]{:S(2)}) async-start(), calls=%async_computation.28 | async-start | bytes 3276800 | tf_op jit(solution)/shard_map/all_gather | solution.py:50
  513.0 160.3 %reduce-scatter.22.cloned.1.call-start = ((), (), s32[]{:S(2)}) async-start(), calls=%async_computation.34 | async-start | bytes 3276800 | tf_op jit(solution)/shard_map/reduce_scatter | solution.py:54
  577.2 150.1 %reduce-scatter.18.cloned.1.call-start = ((), (), s32[]{:S(2)}) async-start(), calls=%async_computation.29 | async-start | bytes 3276800 | tf_op jit(solution)/shard_map/reduce_scatter | solution.py:54
  632.3 155.0 %all-gather.34.cloned.1.call-start = ((), (), s32[]{:S(2)}) async-start(), calls=%async_computation.35 | async-start | bytes 3276800 | tf_op jit(solution)/shard_map/all_gather | solution.py:50
  739.0 103.4 %all-gather.40.cloned.1.call-start = ((), (), s32[]{:S(2)}) async-start(), calls=%async_computation.42 | async-start | bytes 3276800 | tf_op jit(solution)/shard_map/all_gather | solution.py:74
  751.2 146.3 %all-gather.28.cloned.1.call-start = ((), (), s32[]{:S(2)}) async-start(), calls=%async_computation.30 | async-start | bytes 3276800 | tf_op jit(solution)/shard_map/all_gather | solution.py:50
  757.9 194.5 %all-gather.36.cloned.1.call-start = ((), (), s32[]{:S(2)}) async-start(), calls=%async_computation.37 | async-start | bytes 3276800 | tf_op jit(solution)/shard_map/all_gather | solution.py:74
  770.1 235.6 %reduce-scatter.24.cloned.1.call-start = ((), (), s32[]{:S(2)}) async-start(), calls=%async_computation.36 | async-start | bytes 3276800 | tf_op jit(solution)/shard_map/reduce_scatter | solution.py:54
  799.8 259.8 %reduce-scatter.32.cloned.1.call-start = ((), (), s32[]{:S(2)}) async-start(), calls=%async_computation.43 | async-start | bytes 3276800 | tf_op jit(solution)/shard_map/reduce_scatter | solution.py:80
  857.2 256.4 %reduce-scatter.20.cloned.1.call-start = ((), (), s32[]{:S(2)}) async-start(), calls=%async_computation.31 | async-start | bytes 3276800 | tf_op jit(solution)/shard_map/reduce_scatter | solution.py:54
  909.8 257.8 %reduce-scatter.26.cloned.1.call-start = ((), (), s32[]{:S(2)}) async-start(), calls=%async_computation.38 | async-start | bytes 3276800 | tf_op jit(solution)/shard_map/reduce_scatter | solution.py:80
  967.3 266.9 %all-gather.38.cloned.1.call-start = ((), (), s32[]{:S(2)}) async-start(), calls=%async_computation.39 | async-start | bytes 3276800 | tf_op jit(solution)/shard_map/all_gather | solution.py:74
  1179.7 109.4 %all-gather.42.cloned.1.call-start = ((), (), s32[]{:S(2)}) async-start(), calls=%async_computation.44 | async-start | bytes 3276800 | tf_op jit(solution)/shard_map/all_gather | solution.py:74
  1181.1 161.4 %reduce-scatter.28.cloned.1.call-start = ((), (), s32[]{:S(2)}) async-start(), calls=%async_computation.40 | async-start | bytes 3276800 | tf_op jit(solution)/shard_map/reduce_scatter | solution.py:80
  1249.1 147.5 %reduce-scatter.34.cloned.1.call-start = ((), (), s32[]{:S(2)}) async-start(), calls=%async_computation.45 | async-start | bytes 3276800 | tf_op jit(solution)/shard_map/reduce_scatter | solution.py:80
  1423.7 158.3 %reduce-scatter.36.cloned.1.call-start = ((), (), s32[]{:S(2)}) async-start(), calls=%async_computation.46 | async-start | bytes 5242880 | tf_op jit(solution)/shard_map/reduce_scatter | solution.py:319
  1507.3 154.1 %reduce-scatter.30.cloned.1.call-start = ((), (), s32[]{:S(2)}) async-start(), calls=%async_computation.41 | async-start | bytes 5242880 | tf_op jit(solution)/shard_map/reduce_scatter | solution.py:319
  1556.3 259.5 %reduce-scatter.46.cloned.1.call-start = ((), (), s32[]{:S(2)}) async-start(), calls=%async_computation.51 | async-start | bytes 540672
  1669.2 278.6 %reduce-scatter.40.cloned.1.call-start = ((), (), s32[]{:S(2)}) async-start(), calls=%async_computation.48 | async-start | bytes 4325376 | tf_op jit(solution)/shard_map/reduce_scatter | solution.py:343
  1674.1 431.0 %reduce-scatter.38.cloned.1.call-start = ((), (), s32[]{:S(2)}) async-start(), calls=%async_computation.47 | async-start | bytes 12976128 | tf_op jit(solution)/shard_map/reduce_scatter | solution.py:342
  1684.2 605.5 %reduce-scatter.42.cloned.1.call-start = ((), (), s32[]{:S(2)}) async-start(), calls=%async_computation.49 | async-start | bytes 17301504 | tf_op jit(solution)/shard_map/reduce_scatter | solution.py:344
  1695.9 781.4 %reduce-scatter.44.cloned.1.call-start = ((), (), s32[]{:S(2)}) async-start(), calls=%async_computation.50 | async-start | bytes 17301504 | tf_op jit(solution)/shard_map/reduce_scatter | solution.py:345
  1728.3 15.6 all-to-all-start.3
  1743.9 15.9 all-to-all-start.1
  (172 other events, 9634.4 us)
Sparse Core Ops, SparseCore 0:
  10.8 71.8 all-gather.15
  88.6 79.2 all-gather.17
  170.1 79.2 all-gather.29
  252.0 54.6 all-gather.19
  309.5 75.8 all-gather.21
  388.1 75.6 all-gather.23
  512.4 52.4 all-gather.31
  566.4 53.5 all-gather.25
  622.3 51.0 reduce-scatter.21
  675.5 51.7 reduce-scatter.17
  733.0 54.2 all-gather.33
  788.8 53.5 all-gather.39
  843.9 53.5 all-gather.27
  898.9 53.5 all-gather.35
  954.6 51.0 reduce-scatter.23
  1007.8 51.7 reduce-scatter.31
  1061.8 51.7 reduce-scatter.19
  1115.8 51.7 reduce-scatter.25
  1179.9 54.2 all-gather.37
  1235.6 53.5 all-gather.41
  1291.4 51.0 reduce-scatter.27
  1344.8 51.7 reduce-scatter.33
  1507.4 74.5 reduce-scatter.35
  1584.2 77.2 reduce-scatter.29
  1669.3 136.6 reduce-scatter.45
  1808.7 139.0 reduce-scatter.39
  1954.3 150.7 reduce-scatter.37
  2107.9 181.7 reduce-scatter.41
  2292.6 184.5 reduce-scatter.43
where the time goes:
time: 2490 us; the launch traced here: 2480 us
  waiting for transfers between devices  1830 us (73%)
  matrix products  362 us (15%)
  other arithmetic  110 us (4%)
  local copies, waits for them, and re-layouts  69.1 us (3%)
  blocking collectives  62.2 us (2%)
  starting transfers between devices  35.6 us (1%)
    reduce_scatter x4, waiting for transfers between devices, expert_backward(): lax.psum_scatter(normed_part.astype(jnp.bfloat16), 'dp', scatter_dimensio...  199 us
    reduce_scatter x1, waiting for transfers between devices, shards(): lax.psum_scatter(down_acc, ('dp', 'expert'), scatter_dimension=0, tiled=T...  188 us
    reduce_scatter x1, waiting for transfers between devices, shards(): lax.psum_scatter(up_acc, ('dp', 'expert'), scatter_dimension=0, tiled=True)  185 us
    reduce_scatter x4, waiting for transfers between devices, expert_forward(): lax.psum_scatter(partial_out.astype(jnp.bfloat16), 'dp', scatter_dimensio...  184 us
    all_gather x4, waiting for transfers between devices, expert_backward(): lax.all_gather(carried.astype(jnp.bfloat16), 'dp', axis=0, tiled=True)  177 us
    reduce_scatter x1, waiting for transfers between devices, shards(): lax.psum_scatter(qkv_acc, ('dp', 'expert'), scatter_dimension=0, tiled=True)  157 us
    all_gather x4, waiting for transfers between devices, expert_forward(): gathered = lax.all_gather(normed, 'dp', axis=0, tiled=True)  152 us
    all_gather x2, waiting for transfers between devices, shards(): key_value = lax.all_gather(qkv[:, width:], 'dp', axis=0, tiled=True)  138 us
  transfers between devices with their start and end apart: 37, of which 35 were waited for; matrix products, arithmetic and copies ran while one was open for 16% of the time, Pallas kernels for 0%

commit v1 on v0

--- a/solution.py
+++ b/solution.py
@@ -39,6 +39,57 @@
     return lax.dot_general(
         left, right, (((1,), (1,)), ((), ())), preferred_element_type=jnp.float32
     )
+
+
+def swap(values, bit):
+    count = lax.axis_size("expert")
+    return lax.ppermute(values, "expert", [(i, i ^ bit) for i in range(count)])
+
+
+def bit_orders():
+    count = lax.axis_size("expert")
+    bits = [1 << i for i in range(count.bit_length() - 1)]
+    upper = bits[1:]
+    half = len(upper) // 2
+    return upper[half:] + upper[:half] + bits[:1], upper[:half] + upper[half:] + bits[:1]
+
+
+def gather_rows(shard, order):
+    count = lax.axis_size("expert")
+    own = lax.axis_index("expert")
+    pieces = [(0, lax.all_gather(shard, "dp", axis=0))]
+    for bit in order:
+        pieces = pieces + [(mask ^ bit, swap(piece, bit)) for mask, piece in pieces]
+    dp_count, rows, cols = pieces[0][1].shape
+    full = jnp.zeros((dp_count, count, rows, cols), shard.dtype)
+    for mask, piece in pieces:
+        full = lax.dynamic_update_slice_in_dim(full, piece[:, None], own ^ mask, 1)
+    return full.reshape(dp_count * count * rows, cols)
+
+
+def scatter_rows(total, order):
+    count = lax.axis_size("expert")
+    dp_count = lax.axis_size("dp")
+    own = lax.axis_index("expert")
+    rows = total.shape[0] // (count * dp_count)
+    bits = sorted(order)
+    current = total.reshape((dp_count,) + (2,) * len(bits) + (rows, total.shape[1]))
+    left = sorted(bits, reverse=True)
+    for bit in order:
+        axis = 1 + left.index(bit)
+        mine = (own // bit) % 2
+        send = lax.dynamic_index_in_dim(current, 1 - mine, axis, keepdims=False)
+        keep = lax.dynamic_index_in_dim(current, mine, axis, keepdims=False)
+        received = swap(send, bit)
+        current = (keep.astype(jnp.float32) + received.astype(jnp.float32)).astype(jnp.bfloat16)
+        left.remove(bit)
+    return lax.psum_scatter(
+        current.reshape(dp_count * rows, -1), "dp", scatter_dimension=0, tiled=True
+    ).astype(jnp.float32)
+
+
+def spread_heads(blocks):
+    return lax.all_to_all(blocks, "dp", split_axis=0, concat_axis=0, tiled=True)
 
 
 def expert_forward(rows, gain, w_first, w_second, centroid):
@@ -116,17 +167,20 @@
     length = rows_dev * dp_count
     heads = width // HEAD_DIM
     scale = HEAD_DIM ** (-0.5)
-    query_pos = lax.axis_index("dp") * rows_dev + jnp.arange(rows_dev, dtype=jnp.int32)
     key_pos = jnp.arange(length, dtype=jnp.int32)
     slot_ids = jnp.arange(experts * capacity, dtype=jnp.int32)
     expert_ids = jnp.arange(experts, dtype=jnp.int32)
-    full_qkv, full_mix, full_up, full_down, full_gain = (
-        lax.all_gather(qkv_weight, ("dp", "expert"), axis=0, tiled=True),
-        lax.all_gather(mix_weight, ("dp", "expert"), axis=0, tiled=True),
-        lax.all_gather(up_weight, ("dp", "expert"), axis=0, tiled=True),
-        lax.all_gather(down_weight, ("dp", "expert"), axis=0, tiled=True),
-        lax.all_gather(dense_gain, ("dp", "expert"), axis=1, tiled=True),
-    )
+    order_a, order_b = bit_orders()
+    gain_cols = jnp.pad(dense_gain.T, ((0, 0), (0, 126)))
+    half = qkv_weight.shape[1] // 2
+    first_qkv = gather_rows(jnp.concatenate([qkv_weight[:, :half], gain_cols], 1), order_a)
+    full_qkv = jnp.concatenate(
+        [first_qkv[:, :half], gather_rows(qkv_weight[:, half:], order_b)], 1
+    )
+    full_gain = first_qkv[:, half : half + 2].T
+    full_mix = gather_rows(mix_weight, order_a)
+    full_up = gather_rows(up_weight, order_a)
+    full_down = gather_rows(down_weight, order_b)
     gains = full_gain.astype(jnp.float32)
 
     def scores_of(query, keys, allowed):
@@ -140,17 +194,20 @@
         inputs = tokens[micro, 0].astype(jnp.float32)
         normed = layer_norm(inputs, gains[0]).astype(jnp.bfloat16)
         qkv = jnp.dot(normed, full_qkv, preferred_element_type=jnp.float32).astype(jnp.bfloat16)
-        query = qkv[:, :width].reshape(rows_dev, heads, HEAD_DIM)
-        key_value = lax.all_gather(qkv[:, width:], "dp", axis=0, tiled=True)
-        keys = key_value[:, :width].reshape(length, heads, HEAD_DIM)
-        values = key_value[:, width:].reshape(length, heads, HEAD_DIM)
-        allowed = (key_pos[None, :] <= query_pos[:, None]) | (key_pos[None, :] < prefix[micro, 0])
+        mine = width // dp_count
+        blocks = qkv.reshape(rows_dev, 3, dp_count, mine).transpose(2, 0, 1, 3)
+        whole = spread_heads(blocks.reshape(dp_count, rows_dev, 3 * mine)).reshape(
+            length, 3, heads // dp_count, HEAD_DIM
+        )
+        query, keys, values = (whole[:, 0], whole[:, 1], whole[:, 2])
+        allowed = (key_pos[None, :] <= key_pos[:, None]) | (key_pos[None, :] < prefix[micro, 0])
         scores = scores_of(query, keys, allowed)
         row_max = jnp.max(scores, -1, keepdims=True)
         log_total = jnp.log(jnp.sum(jnp.exp(scores - row_max), -1, keepdims=True)) + row_max
         probs_low = jnp.exp(scores - log_total).astype(jnp.bfloat16)
         mixed = jnp.einsum("htl,lhd->thd", probs_low, values, preferred_element_type=jnp.float32)
-        mixed = mixed.reshape(rows_dev, width).astype(jnp.bfloat16)
+        mixed = mixed.astype(jnp.bfloat16).reshape(dp_count, rows_dev, mine)
+        mixed = spread_heads(mixed).transpose(1, 0, 2).reshape(rows_dev, width)
         attn = jnp.dot(mixed, full_mix, preferred_element_type=jnp.float32)
         resid = inputs + attn
         normed2 = layer_norm(resid, gains[1]).astype(jnp.bfloat16)
@@ -215,14 +272,13 @@
                 saved,
             )
         )
-    back_qkv, back_mix, back_up, back_down, back_gain = (
-        lax.all_gather(qkv_weight, ("dp", "expert"), axis=0, tiled=True),
-        lax.all_gather(mix_weight, ("dp", "expert"), axis=0, tiled=True),
-        lax.all_gather(up_weight, ("dp", "expert"), axis=0, tiled=True),
-        lax.all_gather(down_weight, ("dp", "expert"), axis=0, tiled=True),
-        lax.all_gather(dense_gain, ("dp", "expert"), axis=1, tiled=True),
-    )
-    back_gains = back_gain.astype(jnp.float32)
+    back_qkv, back_mix, back_up, back_down, back_gains = (
+        full_qkv,
+        full_mix,
+        full_up,
+        full_down,
+        gains,
+    )
     ex_up_acc = jnp.zeros(expert_up.shape[1:], jnp.float32)
     ex_down_acc = jnp.zeros(expert_down.shape[1:], jnp.float32)
     ex_gain_acc = jnp.zeros((2, width), jnp.float32)
@@ -291,11 +347,9 @@
         resid_part, gain2_grad = norm_back(resid, back_gains[1], normed2_grad)
         resid_grad = after_grad + resid_part
         attn_low = resid_grad.astype(jnp.bfloat16)
-        mixed_grad = (
-            contract_cols(attn_low, back_mix)
-            .astype(jnp.bfloat16)
-            .reshape(rows_dev, heads, HEAD_DIM)
-        )
+        mixed_grad = contract_cols(attn_low, back_mix).astype(jnp.bfloat16)
+        mixed_grad = mixed_grad.reshape(rows_dev, dp_count, mine).transpose(1, 0, 2)
+        mixed_grad = spread_heads(mixed_grad).reshape(length, heads // dp_count, HEAD_DIM)
         probs = jnp.exp(scores_of(query, keys, allowed) - log_total)
         probs_back = probs.astype(jnp.bfloat16)
         prob_grad = jnp.einsum(
@@ -313,15 +367,10 @@
         value_grad = jnp.einsum(
             "htl,thd->lhd", probs_back, mixed_grad, preferred_element_type=jnp.float32
         )
-        both_grads = jnp.concatenate(
-            [key_grad.reshape(length, width), value_grad.reshape(length, width)], 1
-        )
-        own_grads = lax.psum_scatter(
-            both_grads.astype(jnp.bfloat16), "dp", scatter_dimension=0, tiled=True
-        ).astype(jnp.float32)
-        qkv_grad = jnp.concatenate([query_grad.reshape(rows_dev, width), own_grads], 1).astype(
-            jnp.bfloat16
-        )
+        own_grads = jnp.stack([query_grad, key_grad, value_grad], 1).astype(jnp.bfloat16)
+        own_grads = spread_heads(own_grads.reshape(dp_count, rows_dev, 3 * mine))
+        qkv_grad = own_grads.reshape(dp_count, rows_dev, 3, mine).transpose(1, 2, 0, 3)
+        qkv_grad = qkv_grad.reshape(rows_dev, 3 * width)
         normed_grad = contract_cols(qkv_grad, back_qkv)
         input_part, gain1_grad = norm_back(inputs, back_gains[0], normed_grad)
         input_grads.append(resid_grad + input_part)
@@ -338,12 +387,18 @@
     mix_acc = contract_rows(jnp.concatenate(mixed_rows, 0), jnp.concatenate(attn_rows, 0))
     up_acc = contract_rows(jnp.concatenate(normed2_rows, 0), jnp.concatenate(pre_grad_rows, 0))
     down_acc = contract_rows(jnp.concatenate(hidden_rows, 0), jnp.concatenate(ffn_rows, 0))
-    qkv_out, mix_out, up_out, down_out, gain_out = (
-        lax.psum_scatter(qkv_acc, ("dp", "expert"), scatter_dimension=0, tiled=True),
-        lax.psum_scatter(mix_acc, ("dp", "expert"), scatter_dimension=0, tiled=True),
-        lax.psum_scatter(up_acc, ("dp", "expert"), scatter_dimension=0, tiled=True),
-        lax.psum_scatter(down_acc, ("dp", "expert"), scatter_dimension=0, tiled=True),
-        lax.psum_scatter(gain_acc, ("dp", "expert"), scatter_dimension=1, tiled=True),
+    low = jnp.bfloat16
+    order_c, order_d = (order_a[::-1], order_b[::-1])
+    half = 3 * width // 2
+    down_out = scatter_rows(down_acc.astype(low), order_c)
+    up_out = scatter_rows(up_acc.astype(low), order_d)
+    mix_out = scatter_rows(mix_acc.astype(low), order_d)
+    qkv_low = qkv_acc.astype(low)
+    qkv_out = jnp.concatenate(
+        [scatter_rows(qkv_low[:, :half], order_c), scatter_rows(qkv_low[:, half:], order_d)], 1
+    )
+    gain_out = lax.psum_scatter(
+        gain_acc, ("dp", "expert"), scatter_dimension=1, tiled=True
     )
     stat_sums, ex_gain_sum, cent_sum = lax.psum(
         (jnp.stack(stat_list, 1), ex_gain_acc, cent_acc), "dp"

time: 2490 us -> 1840 us (0.74)
  waiting for transfers between devices: 1830 us -> 942 us
  local copies, waits for them, and re-layouts: 69.1 us -> 174 us
  starting transfers between devices: 35.6 us -> 117 us
  other arithmetic: 110 us -> 152 us
    reduce_scatter x6 -> x5, waiting for transfers between devices: 745 us -> 28.3 us  [scatter_rows(): lax.psum_scatter(current.reshape(dp_count * rows, -1), 'dp', scatter_dime...]
    all_gather x6 -> x2, waiting for transfers between devices: 310 us -> 0.02 us  [gather_rows(): pieces = [(0, lax.all_gather(shard, 'dp', axis=0))]]
    ppermute x0 -> x50, waiting for transfers between devices: none -> 179 us  [swap(): return lax.ppermute(values, 'expert', [(i, i ^ bit) for i in range(count)])]
    reduce_scatter x4, waiting for transfers between devices: 199 us -> 139 us  [expert_backward(): lax.psum_scatter(normed_part.astype(jnp.bfloat16), 'dp', scatter_dimensio...]
    dynamic_update_slice x0 -> x40, local copies, waits for them, and re-layouts: none -> 51.1 us  [gather_rows(): full = lax.dynamic_update_slice_in_dim(full, piece[:, None], own ^ mask, 1)]
    all_to_all x0 -> x8, starting transfers between devices: none -> 47 us  [spread_heads(): return lax.all_to_all(blocks, 'dp', split_axis=0, concat_axis=0, tiled=True)]
    all_to_all x0 -> x8, waiting for transfers between devices: none -> 40.9 us  [spread_heads(): return lax.all_to_all(blocks, 'dp', split_axis=0, concat_axis=0, tiled=True)]
    ppermute x0 -> x50, starting transfers between devices: none -> 35.8 us  [swap(): return lax.ppermute(values, 'expert', [(i, i ^ bit) for i in range(count)])]
  transfers between devices with their start and end apart: 37 -> 90, of which waited for: 35 -> 46; matrix products, arithmetic and copies ran while one was open for 16% -> 31% of each run, Pallas kernels for 0% -> 0%
where the time goes in v1:
time: 1840 us; the launch traced here: 1830 us
  waiting for transfers between devices  942 us (51%)
  matrix products  351 us (19%)
  local copies, waits for them, and re-layouts  174 us (9%)
  other arithmetic  152 us (8%)
  starting transfers between devices  117 us (6%)
  blocking collectives  72.9 us (4%)
    reduce_scatter x4, waiting for transfers between devices, expert_forward(): lax.psum_scatter(partial_out.astype(jnp.bfloat16), 'dp', scatter_dimensio...  185 us
    ppermute x50, waiting for transfers between devices, swap(): return lax.ppermute(values, 'expert', [(i, i ^ bit) for i in range(count)])  179 us
    all_gather x4, waiting for transfers between devices, expert_backward(): lax.all_gather(carried.astype(jnp.bfloat16), 'dp', axis=0, tiled=True)  177 us
    all_gather x4, waiting for transfers between devices, expert_forward(): gathered = lax.all_gather(normed, 'dp', axis=0, tiled=True)  151 us
    reduce_scatter x4, waiting for transfers between devices, expert_backward(): lax.psum_scatter(normed_part.astype(jnp.bfloat16), 'dp', scatter_dimensio...  139 us
    dot_general x16, matrix products, contract_cols(): lax.dot_general(left, right, (((1,), (1,)), ((), ())), preferred_element_...  94.8 us
    dot_general x16, matrix products, contract_rows(): lax.dot_general(left, right, (((0,), (0,)), ((), ())), preferred_element_...  92.1 us
    all_gather x3, blocking collectives, gather_rows(): pieces = [(0, lax.all_gather(shard, 'dp', axis=0))]  55.2 us
  transfers between devices with their start and end apart: 90, of which 46 were waited for; matrix products, arithmetic and copies ran while one was open for 31% of the time, Pallas kernels for 0%

profile of v1, /device:TPU:0, one launch (start us, length us, event | category | flops | bytes accessed | tf_op | source)
XLA Modules:
  0.0 1826.4 jit_solution(7272937837150078258)
XLA Ops:
  8.0 16.7 all-gather.2
  28.6 19.6 %all-gather.1 = bf16[128,1536]{1,0:T(8,128)(2,1)S(1)} all-gather(bf16[32,1536]{1,0:T(8,128)(2,1)S(1)} %get-tuple-element.122), channel_id=3, replica_groups=mesh['dp'=4,'expert'=8] {'dp'}, dimensions={0}, use_global_device_ids=true | all-gather | bytes 491520 | tf_op jit(solution)/shard_map/all_gather | solution.py:60
  60.5 19.0 %all-gather = bf16[128,1664]{1,0:T(8,128)(2,1)S(1)} all-gather(bf16[32,1664]{1,0:T(8,128)(2,1)S(1)} %fusion.234), channel_id=2, replica_groups=mesh['dp'=4,'expert'=8] {'dp'}, dimensions={0}, use_global_device_ids=true | all-gather | bytes 532480 | tf_op jit(solution)/shard_map/all_gather | solution.py:60
  162.6 15.4 all-to-all-start
  244.3 12.5 all-to-all-done.4
  318.1 18.4 %collective-permute-done.30 = bf16[4,128,1024]{2,1,0:T(8,128)(2,1)} collective-permute-done((bf16[4,128,1024]{2,1,0:T(8,128)(2,1)}, bf16[4,128,1024]{2,1,0:T(8,128)(2,1)}, u32[]{:S(2)}, u32[]{:S(2)}) %collective-permute-start.30) | collective-permute-done | bytes 1048608 | tf_op jit(solution)/shard_map/ppermute | solution.py:46
  427.5 51.5 %all-gather.20.cloned.1.call-done = bf16[1280,1024]{1,0:T(8,128)(2,1)} async-done(((bf16[320,1024]{1,0:T(8,128)(2,1)}), bf16[1280,1024]{1,0:T(8,128)(2,1)}) %all-gather.20.cloned.1.call-update) | async-done | bytes 2621456 | tf_op jit(solution)/shard_map/all_gather | solution.py:101
  491.7 42.3 %all-gather.16.cloned.1.call-done = bf16[1280,1024]{1,0:T(8,128)(2,1)} async-done(((bf16[320,1024]{1,0:T(8,128)(2,1)}), bf16[1280,1024]{1,0:T(8,128)(2,1)}) %all-gather.16.cloned.1.call-update) | async-done | bytes 2621456 | tf_op jit(solution)/shard_map/all_gather | solution.py:101
  546.4 40.8 %reduce-scatter.21.cloned.1.call-done = bf16[320,1024]{1,0:T(8,128)(2,1)} async-done(((bf16[1280,1024]{1,0:T(8,128)(2,1)}), bf16[320,1024]{1,0:T(8,128)(2,1)}) %reduce-scatter.21.cloned.1.call-update) | async-done | bytes 655376 | tf_op jit(solution)/shard_map/reduce_scatter | solution.py:105
  590.1 51.1 %reduce-scatter.17.cloned.1.call-done = bf16[320,1024]{1,0:T(8,128)(2,1)} async-done(((bf16[1280,1024]{1,0:T(8,128)(2,1)}), bf16[320,1024]{1,0:T(8,128)(2,1)}) %reduce-scatter.17.cloned.1.call-update) | async-done | bytes 655376 | tf_op jit(solution)/shard_map/reduce_scatter | solution.py:105
  684.0 17.2 all-gather.22.cloned.1.call-done
  714.0 42.2 %all-gather.28.cloned.1.call-done = bf16[1280,1024]{1,0:T(8,128)(2,1)} async-done(((bf16[320,1024]{1,0:T(8,128)(2,1)}), bf16[1280,1024]{1,0:T(8,128)(2,1)}) %all-gather.28.cloned.1.call-update) | async-done | bytes 2621456 | tf_op jit(solution)/shard_map/all_gather | solution.py:125
  771.1 40.2 %all-gather.18.cloned.1.call-done = bf16[1280,1024]{1,0:T(8,128)(2,1)} async-done(((bf16[320,1024]{1,0:T(8,128)(2,1)}), bf16[1280,1024]{1,0:T(8,128)(2,1)}) %all-gather.18.cloned.1.call-update) | async-done | bytes 2621456 | tf_op jit(solution)/shard_map/all_gather | solution.py:101
  823.9 42.4 %all-gather.24.cloned.1.call-done = bf16[1280,1024]{1,0:T(8,128)(2,1)} async-done(((bf16[320,1024]{1,0:T(8,128)(2,1)}), bf16[1280,1024]{1,0:T(8,128)(2,1)}) %all-gather.24.cloned.1.call-update) | async-done | bytes 2621456 | tf_op jit(solution)/shard_map/all_gather | solution.py:125
  881.2 38.5 %reduce-scatter.23.cloned.1.call-done = bf16[320,1024]{1,0:T(8,128)(2,1)} async-done(((bf16[1280,1024]{1,0:T(8,128)(2,1)}), bf16[320,1024]{1,0:T(8,128)(2,1)}) %reduce-scatter.23.cloned.1.call-update) | async-done | bytes 655376 | tf_op jit(solution)/shard_map/reduce_scatter | solution.py:105
  919.7 54.0 %reduce-scatter.29.cloned.1.call-done = bf16[320,1024]{1,0:T(8,128)(2,1)} async-done(((bf16[1280,1024]{1,0:T(8,128)(2,1)}), bf16[320,1024]{1,0:T(8,128)(2,1)}) %reduce-scatter.29.cloned.1.call-update) | async-done | bytes 655376 | tf_op jit(solution)/shard_map/reduce_scatter | solution.py:131
  973.7 54.1 %reduce-scatter.19.cloned.1.call-done = bf16[320,1024]{1,0:T(8,128)(2,1)} async-done(((bf16[1280,1024]{1,0:T(8,128)(2,1)}), bf16[320,1024]{1,0:T(8,128)(2,1)}) %reduce-scatter.19.cloned.1.call-update) | async-done | bytes 655376 | tf_op jit(solution)/shard_map/reduce_scatter | solution.py:105
  1027.8 54.0 %reduce-scatter.25.cloned.1.call-done = bf16[320,1024]{1,0:T(8,128)(2,1)} async-done(((bf16[1280,1024]{1,0:T(8,128)(2,1)}), bf16[320,1024]{1,0:T(8,128)(2,1)}) %reduce-scatter.25.cloned.1.call-update) | async-done | bytes 655376 | tf_op jit(solution)/shard_map/reduce_scatter | solution.py:131
  1095.4 53.0 %all-gather.26.cloned.1.call-done = bf16[1280,1024]{1,0:T(8,128)(2,1)} async-done(((bf16[320,1024]{1,0:T(8,128)(2,1)}), bf16[1280,1024]{1,0:T(8,128)(2,1)}) %all-gather.26.cloned.1.call-update) | async-done | bytes 2621456 | tf_op jit(solution)/shard_map/all_gather | solution.py:125
  1163.9 39.4 %all-gather.30.cloned.1.call-done = bf16[1280,1024]{1,0:T(8,128)(2,1)} async-done(((bf16[320,1024]{1,0:T(8,128)(2,1)}), bf16[1280,1024]{1,0:T(8,128)(2,1)}) %all-gather.30.cloned.1.call-update) | async-done | bytes 2621456 | tf_op jit(solution)/shard_map/all_gather | solution.py:125
  1279.2 31.4 %reduce-scatter.31.cloned.1.call-done = bf16[320,1024]{1,0:T(8,128)(2,1)} async-done(((bf16[1280,1024]{1,0:T(8,128)(2,1)}), bf16[320,1024]{1,0:T(8,128)(2,1)}) %reduce-scatter.31.cloned.1.call-update) | async-done | bytes 655376 | tf_op jit(solution)/shard_map/reduce_scatter | solution.py:131
  1423.1 12.1 multiply_reduce_fusion
  1435.2 12.1 multiply_convert_fusion
  1465.7 12.0 multiply_reduce_fusion.1
  1477.7 12.1 multiply_convert_fusion.1
  1583.0 12.8 collective-permute-done.36
  1596.8 41.5 %collective-permute-done.39 = bf16[4,2,32,1536]{3,2,1,0:T(8,128)(2,1)} collective-permute-done((bf16[4,2,32,1536]{3,2,1,0:T(8,128)(2,1)}, bf16[4,2,32,1536]{3,2,1,0:T(8,128)(2,1)}, u32[]{:S(2)}, u32[]{:S(2)}) %collective-permute-start.39) | collective-permute-done | bytes 786464 | tf_op jit(solution)/shard_map/ppermute | solution.py:46
  1663.2 15.3 collective-permute-done.46
  1688.7 34.4 %collective-permute-done.48 = bf16[4,2,128,1024]{3,2,1,0:T(8,128)(2,1)} collective-permute-done((bf16[4,2,128,1024]{3,2,1,0:T(8,128)(2,1)}, bf16[4,2,128,1024]{3,2,1,0:T(8,128)(2,1)}, u32[]{:S(2)}, u32[]{:S(2)}) %collective-permute-start.48) | collective-permute-done | bytes 2097184 | tf_op jit(solution)/shard_map/ppermute | solution.py:46
  1737.7 11.5 collective-permute-done.49
  1760.4 17.7 all-reduce.1
  1791.4 26.2 %reduce-scatter.41.cloned.1.call-done = bf16[128,1024]{1,0:T(8,128)(2,1)} async-done(((bf16[512,1024]{1,0:T(8,128)(2,1)}), bf16[128,1024]{1,0:T(8,128)(2,1)}) %reduce-scatter.41.cloned.1.call-update) | async-done | bytes 262160 | tf_op jit(solution)/shard_map/reduce_scatter | solution.py:86
  (803 shorter events, 847.5 us)
Async XLA Ops:
  7.2 176.3 %all-gather.34.cloned.1.call-start = ((), (), s32[]{:S(2)}) async-start(), calls=%async_computation.52 | async-start | bytes 1310720 | tf_op jit(solution)/shard_map/all_gather | solution.py:60
  7.9 191.6 %all-gather.32.cloned.1.call-start = ((), (), s32[]{:S(2)}) async-start(), calls=%async_computation.51 | async-start | bytes 1310720 | tf_op jit(solution)/shard_map/all_gather | solution.py:60
  24.6 98.4 %collective-permute-start.15 = (bf16[4,32,1024]{2,1,0:T(8,128)(2,1)S(1)}, bf16[4,32,1024]{2,1,0:T(8,128)(2,1)}, u32[]{:S(2)}, u32[]{:S(2)}) collective-permute-start(bf16[4,32,1024]{2,1,0:T(8,128)(2,1)S(1)} %bitcast.729), channel_id=1, source_target_pairs={{0,2},{1,3},{2,0},{3,1},{4,6},{5,7},{6,4},{7,5},{8,10},{9,11},{10,... | collective-permute-start | bytes 786440 | tf_op jit(solution)/shard_map/ppermute | solution.py:46
  27.6 152.8 %collective-permute-start.17 = (bf16[4,32,1024]{2,1,0:T(8,128)(2,1)S(1)}, bf16[4,32,1024]{2,1,0:T(8,128)(2,1)}, u32[]{:S(2)}, u32[]{:S(2)}) collective-permute-start(bf16[4,32,1024]{2,1,0:T(8,128)(2,1)S(1)} %bitcast.731), channel_id=1, source_target_pairs={{0,1},{1,0},{2,3},{3,2},{4,5},{5,4},{6,7},{7,6},{8,9},{9,8},{10,11... | collective-permute-start | bytes 786440 | tf_op jit(solution)/shard_map/ppermute | solution.py:46
  199.5 140.8 %collective-permute-start.31 = (bf16[4,128,1024]{2,1,0:T(8,128)(2,1)}, bf16[4,128,1024]{2,1,0:T(8,128)(2,1)}, u32[]{:S(2)}, u32[]{:S(2)}) collective-permute-start(bf16[4,128,1024]{2,1,0:T(8,128)(2,1)} %bitcast.723), channel_id=1, source_target_pairs={{0,1},{1,0},{2,3},{3,2},{4,5},{5,4},{6,7},{7,6},{8,9},{9,8},{10,11... | collective-permute-start | bytes 3145736 | tf_op jit(solution)/shard_map/ppermute | solution.py:46
  219.9 95.9 %collective-permute-start.24 = (bf16[4,32,4096]{2,1,0:T(8,128)(2,1)}, bf16[4,32,4096]{2,1,0:T(8,128)(2,1)}, u32[]{:S(2)}, u32[]{:S(2)}) collective-permute-start(bf16[4,32,4096]{2,1,0:T(8,128)(2,1)} %bitcast.727), channel_id=1, source_target_pairs={{0,1},{1,0},{2,3},{3,2},{4,5},{5,4},{6,7},{7,6},{8,9},{9,8},{10,11... | collective-permute-start | bytes 3145736 | tf_op jit(solution)/shard_map/ppermute | solution.py:46
  220.0 131.1 %collective-permute-start.33 = (bf16[4,128,1024]{2,1,0:T(8,128)(2,1)}, bf16[4,128,1024]{2,1,0:T(8,128)(2,1)}, u32[]{:S(2)}, u32[]{:S(2)}) collective-permute-start(bf16[4,128,1024]{2,1,0:T(8,128)(2,1)} %collective-permute-done.29), channel_id=1, source_target_pairs={{0,1},{1,0},{2,3},{3,2},{4,5},{5,4},{6,7},{7,6},{8,9},{9,8},{10,11... | collective-permute-start | bytes 3145736 | tf_op jit(solution)/shard_map/ppermute | solution.py:46
  231.5 117.3 %collective-permute-start.32 = (bf16[4,128,1024]{2,1,0:T(8,128)(2,1)}, bf16[4,128,1024]{2,1,0:T(8,128)(2,1)}, u32[]{:S(2)}, u32[]{:S(2)}) collective-permute-start(bf16[4,128,1024]{2,1,0:T(8,128)(2,1)} %collective-permute-done.28), channel_id=1, source_target_pairs={{0,1},{1,0},{2,3},{3,2},{4,5},{5,4},{6,7},{7,6},{8,9},{9,8},{10,11... | collective-permute-start | bytes 3145736 | tf_op jit(solution)/shard_map/ppermute | solution.py:46
  233.8 78.2 %collective-permute-start.23 = (bf16[4,32,4096]{2,1,0:T(8,128)(2,1)}, bf16[4,32,4096]{2,1,0:T(8,128)(2,1)}, u32[]{:S(2)}, u32[]{:S(2)}) collective-permute-start(bf16[4,32,4096]{2,1,0:T(8,128)(2,1)} %collective-permute-done.21), channel_id=1, source_target_pairs={{0,2},{1,3},{2,0},{3,1},{4,6},{5,7},{6,4},{7,5},{8,10},{9,11},{10,... | collective-permute-start | bytes 3145736 | tf_op jit(solution)/shard_map/ppermute | solution.py:46
  426.9 107.1 %all-gather.16.cloned.1.call-start = ((), (), s32[]{:S(2)}) async-start(), calls=%async_computation.30 | async-start | bytes 3276800 | tf_op jit(solution)/shard_map/all_gather | solution.py:101
  427.5 159.7 %reduce-scatter.21.cloned.1.call-start = ((), (), s32[]{:S(2)}) async-start(), calls=%async_computation.35 | async-start | bytes 3276800 | tf_op jit(solution)/shard_map/reduce_scatter | solution.py:105
  491.4 149.8 %reduce-scatter.17.cloned.1.call-start = ((), (), s32[]{:S(2)}) async-start(), calls=%async_computation.31 | async-start | bytes 3276800 | tf_op jit(solution)/shard_map/reduce_scatter | solution.py:105
  546.3 154.9 %all-gather.22.cloned.1.call-start = ((), (), s32[]{:S(2)}) async-start(), calls=%async_computation.36 | async-start | bytes 3276800 | tf_op jit(solution)/shard_map/all_gather | solution.py:101
  652.9 103.4 %all-gather.28.cloned.1.call-start = ((), (), s32[]{:S(2)}) async-start(), calls=%async_computation.42 | async-start | bytes 3276800 | tf_op jit(solution)/shard_map/all_gather | solution.py:125
  665.0 146.3 %all-gather.18.cloned.1.call-start = ((), (), s32[]{:S(2)}) async-start(), calls=%async_computation.32 | async-start | bytes 3276800 | tf_op jit(solution)/shard_map/all_gather | solution.py:101
  671.7 194.6 %all-gather.24.cloned.1.call-start = ((), (), s32[]{:S(2)}) async-start(), calls=%async_computation.38 | async-start | bytes 3276800 | tf_op jit(solution)/shard_map/all_gather | solution.py:125
  684.0 235.7 %reduce-scatter.23.cloned.1.call-start = ((), (), s32[]{:S(2)}) async-start(), calls=%async_computation.37 | async-start | bytes 3276800 | tf_op jit(solution)/shard_map/reduce_scatter | solution.py:105
  713.6 260.1 %reduce-scatter.29.cloned.1.call-start = ((), (), s32[]{:S(2)}) async-start(), calls=%async_computation.43 | async-start | bytes 3276800 | tf_op jit(solution)/shard_map/reduce_scatter | solution.py:131
  771.0 256.7 %reduce-scatter.19.cloned.1.call-start = ((), (), s32[]{:S(2)}) async-start(), calls=%async_computation.33 | async-start | bytes 3276800 | tf_op jit(solution)/shard_map/reduce_scatter | solution.py:105
  823.6 258.1 %reduce-scatter.25.cloned.1.call-start = ((), (), s32[]{:S(2)}) async-start(), calls=%async_computation.39 | async-start | bytes 3276800 | tf_op jit(solution)/shard_map/reduce_scatter | solution.py:131
  881.1 267.3 %all-gather.26.cloned.1.call-start = ((), (), s32[]{:S(2)}) async-start(), calls=%async_computation.40 | async-start | bytes 3276800 | tf_op jit(solution)/shard_map/all_gather | solution.py:125
  1094.0 109.4 %all-gather.30.cloned.1.call-start = ((), (), s32[]{:S(2)}) async-start(), calls=%async_computation.44 | async-start | bytes 3276800 | tf_op jit(solution)/shard_map/all_gather | solution.py:125
  1095.3 182.3 %reduce-scatter.27.cloned.1.call-start = ((), (), s32[]{:S(2)}) async-start(), calls=%async_computation.41 | async-start | bytes 3276800 | tf_op jit(solution)/shard_map/reduce_scatter | solution.py:131
  1163.3 147.3 %reduce-scatter.31.cloned.1.call-start = ((), (), s32[]{:S(2)}) async-start(), calls=%async_computation.45 | async-start | bytes 3276800 | tf_op jit(solution)/shard_map/reduce_scatter | solution.py:131
  1395.4 114.7 %collective-permute-start.41 = (bf16[4,2,2,32,1024]{4,3,2,1,0:T(8,128)(2,1)}, bf16[4,2,2,32,1024]{4,3,2,1,0:T(8,128)(2,1)}, u32[]{:S(2)}, u32[]{:S(2)}) collective-permute-start(bf16[4,2,2,32,1024]{4,3,2,1,0:T(8,128)(2,1)} %dynamic-slice_bitcast_fusion.8), channel_id=1, source_target_pairs={{0,1},{1,0},{2,3},{3,2},{4,5},{5,4},{6,7},{7,6},{8,9},{9,8},{10,11... | collective-permute-start | bytes 3145736 | tf_op jit(solution)/shard_map/ppermute | solution.py:46
  1510.1 268.6 %reduce-scatter.37.cloned.1.call-start = ((), (), s32[]{:S(2)}) async-start(), calls=%async_computation.48 | async-start | bytes 327680 | tf_op jit(solution)/shard_map/reduce_scatter | solution.py:86
  1533.2 119.4 %collective-permute-start.47 = (bf16[4,2,2,128,1024]{4,3,2,1,0:T(8,128)(2,1)}, bf16[4,2,2,128,1024]{4,3,2,1,0:T(8,128)(2,1)}, u32[]{:S(2)}, u32[]{:S(2)}) collective-permute-start(bf16[4,2,2,128,1024]{4,3,2,1,0:T(8,128)(2,1)} %dynamic-slice_bitcast_fusion), channel_id=1, source_target_pairs={{0,1},{1,0},{2,3},{3,2},{4,5},{5,4},{6,7},{7,6},{8,9},{9,8},{10,11... | collective-permute-start | bytes 12582920 | tf_op jit(solution)/shard_map/ppermute | solution.py:46
  1534.5 250.0 %reduce-scatter.43.cloned.1.call-start = ((), (), s32[]{:S(2)}) async-start(), calls=%async_computation.53 | async-start | bytes 540672
  1582.9 202.9 %reduce-scatter.33.cloned.1.call-start = ((), (), s32[]{:S(2)}) async-start(), calls=%async_computation.46 | async-start | bytes 491520 | tf_op jit(solution)/shard_map/reduce_scatter | solution.py:86
  1646.7 139.1 %reduce-scatter.35.cloned.1.call-start = ((), (), s32[]{:S(2)}) async-start(), calls=%async_computation.47 | async-start | bytes 491520 | tf_op jit(solution)/shard_map/reduce_scatter | solution.py:86
  1663.1 126.5 %reduce-scatter.39.cloned.1.call-start = ((), (), s32[]{:S(2)}) async-start(), calls=%async_computation.49 | async-start | bytes 1310720 | tf_op jit(solution)/shard_map/reduce_scatter | solution.py:86
  1680.9 136.6 %reduce-scatter.41.cloned.1.call-start = ((), (), s32[]{:S(2)}) async-start(), calls=%async_computation.50 | async-start | bytes 1310720 | tf_op jit(solution)/shard_map/reduce_scatter | solution.py:86
  (221 other events, 5117.9 us)
Sparse Core Ops, SparseCore 0:
  9.6 36.4 all-gather.33
  50.3 34.1 all-gather.31
  427.0 51.9 all-gather.19
  480.4 53.5 all-gather.15
  536.1 51.0 reduce-scatter.20
  589.3 51.7 reduce-scatter.16
  646.9 54.2 all-gather.21
  702.8 53.3 all-gather.27
  757.8 53.5 all-gather.17
  812.7 53.5 all-gather.23
  868.6 51.0 reduce-scatter.22
  921.8 51.7 reduce-scatter.28
  976.0 51.7 reduce-scatter.18
  1029.9 51.7 reduce-scatter.24
  1094.1 54.2 all-gather.25
  1149.8 53.5 all-gather.29
  1205.5 51.0 reduce-scatter.26
  1258.7 51.7 reduce-scatter.30
  1534.6 20.3 reduce-scatter.36
  1583.0 137.0 reduce-scatter.42
  1723.0 16.6 reduce-scatter.32
  1742.5 19.0 reduce-scatter.34
  1763.9 25.6 reduce-scatter.38
  1791.7 25.7 reduce-scatter.40

commit v2 on v1

v2 whole, which is shorter than its diff:
```python
import functools

import jax
import jax.numpy as jnp
from jax import lax
from jax.experimental import pallas as pl
from jax.experimental.pallas import tpu as pltpu
from jax.sharding import PartitionSpec as P

HEAD_DIM = 64


eps = 1e-05


def layer_norm(values, gain):
    centred = values - jnp.mean(values, -1, keepdims=True)
    spread = jnp.mean(centred * centred, -1, keepdims=True)
    return centred * lax.rsqrt(spread + eps) * gain


def norm_back(values, gain, grads):
    _, pullback = jax.vjp(layer_norm, values, gain)
    return pullback(grads)


def gelu(values):
    return jax.nn.gelu(values, approximate=True)


def gelu_back(values, grads):
    _, pullback = jax.vjp(gelu, values)
    return pullback(grads)[0]


def contract_rows(left, right):
    return lax.dot_general(
        left, right, (((0,), (0,)), ((), ())), preferred_element_type=jnp.float32
    )


def contract_cols(left, right):
    return lax.dot_general(
        left, right, (((1,), (1,)), ((), ())), preferred_element_type=jnp.float32
    )


def swap(values, bit):
    count = lax.axis_size("expert")
    return lax.ppermute(values, "expert", [(i, i ^ bit) for i in range(count)])


def turn(values, shift):
    count = lax.axis_size("dp")
    return lax.ppermute(values, "dp", [(i, (i + shift) % count) for i in range(count)])


def sum_small(values):
    total = values
    for shift in range(1, lax.axis_size("dp")):
        total = total + turn(values, shift)
    return total


def bit_orders():
    count = lax.axis_size("expert")
    bits = [1 << i for i in range(count.bit_length() - 1)]
    upper = bits[1:]
    half = len(upper) // 2
    return upper[half:] + upper[:half] + bits[:1], upper[:half] + upper[half:] + bits[:1]


def assemble_kernel(masks, *refs):
    pieces, full, sems = refs[: len(masks)], refs[-2], refs[-1]
    own = lax.axis_index("expert")
    copies = []
    for i, mask in enumerate(masks):
        copies.append(
            pltpu.make_async_copy(pieces[i], full.at[:, jnp.bitwise_xor(own, mask)], sems.at[i])
        )
    for copy in copies:
        copy.start()
    for copy in copies:
        copy.wait()


def assemble(pieces):
    masks = [mask for mask, _ in pieces]
    arrays = [piece for _, piece in pieces]
    dp_count, rows, cols = arrays[0].shape
    full = pl.pallas_call(
        functools.partial(assemble_kernel, masks),
        out_shape=jax.ShapeDtypeStruct((dp_count, len(masks), rows, cols), arrays[0].dtype),
        in_specs=[pl.BlockSpec(memory_space=pl.ANY)] * len(masks),
        out_specs=pl.BlockSpec(memory_space=pl.ANY),
        scratch_shapes=[pltpu.SemaphoreType.DMA((len(masks),))],
        name="assemble",
    )(*arrays)
    return full.reshape(dp_count * len(masks) * rows, cols)


def spread(piece, order):
    pieces = [(0, piece)]
    for bit in order:
        pieces = pieces + [(mask ^ bit, swap(part, bit)) for mask, part in pieces]
    return pieces


def gather_dp(shard):
    return lax.all_gather(shard, "dp", axis=0)


def turn_gather(shard):
    count = lax.axis_size("dp")
    own = lax.axis_index("dp")
    full = jnp.zeros((count,) + shard.shape, shard.dtype)
    for shift in range(count):
        part = shard if shift == 0 else turn(shard, shift)
        full = lax.dynamic_update_slice_in_dim(full, part[None], (own - shift) % count, 0)
    return full


def scatter_rows(total, order):
    count = lax.axis_size("expert")
    dp_count = lax.axis_size("dp")
    own = lax.axis_index("expert")
    rows = total.shape[0] // (count * dp_count)
    bits = sorted(order)
    current = total.reshape((dp_count,) + (2,) * len(bits) + (rows, total.shape[1]))
    left = sorted(bits, reverse=True)
    for bit in order:
        axis = 1 + left.index(bit)
        mine = (own // bit) % 2
        send = lax.dynamic_index_in_dim(current, 1 - mine, axis, keepdims=False)
        keep = lax.dynamic_index_in_dim(current, mine, axis, keepdims=False)
        received = swap(send, bit)
        current = (keep.astype(jnp.float32) + received.astype(jnp.float32)).astype(jnp.bfloat16)
        left.remove(bit)
    return lax.psum_scatter(
        current.reshape(dp_count * rows, -1), "dp", scatter_dimension=0, tiled=True
    ).astype(jnp.float32)


def swap_heads(blocks):
    return lax.all_to_all(blocks, "dp", split_axis=0, concat_axis=0, tiled=True)


def swap_experts(slots):
    count = lax.axis_size("expert")
    blocks = slots.reshape(count, -1, slots.shape[1])
    return lax.all_to_all(blocks, "expert", split_axis=0, concat_axis=0, tiled=True).reshape(
        slots.shape
    )


def head_probs(x_ref, query, allowed, width, h):
    keys = x_ref[:, width + h * HEAD_DIM : width + (h + 1) * HEAD_DIM]
    values = x_ref[:, 2 * width + h * HEAD_DIM : 2 * width + (h + 1) * HEAD_DIM]
    scores = jnp.where(allowed, contract_cols(keys, query), -1e30)
    top = jnp.max(scores, 0, keepdims=True)
    weights = jnp.exp(scores - top)
    return keys, values, weights, jnp.sum(weights, 0, keepdims=True)


def allowed_pairs(length, block, start, prefix):
    key_pos = lax.broadcasted_iota(jnp.int32, (length, block), 0)
    query_pos = start + lax.broadcasted_iota(jnp.int32, (length, block), 1)
    return (key_pos <= query_pos) | (key_pos < prefix)


def attend_kernel(prefix_ref, x_ref, out_ref):
    block, width = out_ref.shape
    length = x_ref.shape[0]
    start = pl.multiple_of(pl.program_id(0) * block, block)
    allowed = allowed_pairs(length, block, start, prefix_ref[0])
    query = x_ref[pl.ds(start, block), :width]
    parts = []
    for h in range(width // HEAD_DIM):
        own = query[:, h * HEAD_DIM : (h + 1) * HEAD_DIM] * HEAD_DIM ** (-0.5)
        _, values, weights, total = head_probs(x_ref, own, allowed, width, h)
        parts.append(contract_rows(values, weights.astype(jnp.bfloat16)) * (1.0 / total))
    out_ref[...] = jnp.concatenate(parts, 0).T.astype(out_ref.dtype)


def attend(whole, prefix, block):
    length, cols = whole.shape
    width = cols // 3
    return pl.pallas_call(
        attend_kernel,
        out_shape=jax.ShapeDtypeStruct((length, width), whole.dtype),
        grid=(length // block,),
        in_specs=[
            pl.BlockSpec(memory_space=pltpu.SMEM),
            pl.BlockSpec((length, cols), lambda i: (0, 0)),
        ],
        out_specs=pl.BlockSpec((block, width), lambda i: (i, 0)),
        name="attend",
    )(prefix, whole)


def attend_back_kernel(prefix_ref, x_ref, grad_ref, out_ref, key_acc, value_acc):
    block, width = grad_ref.shape
    length = x_ref.shape[0]
    step = pl.program_id(0)
    start = pl.multiple_of(step * block, block)
    allowed = allowed_pairs(length, block, start, prefix_ref[0])
    query = x_ref[pl.ds(start, block), :width]
    heads = width // HEAD_DIM

    @pl.when(step == 0)
    def _():
        key_acc[...] = jnp.zeros_like(key_acc)
        value_acc[...] = jnp.zeros_like(value_acc)

    parts = []
    for h in range(heads):
        own = query[:, h * HEAD_DIM : (h + 1) * HEAD_DIM] * HEAD_DIM ** (-0.5)
        grad = grad_ref[:, h * HEAD_DIM : (h + 1) * HEAD_DIM]
        keys, values, weights, total = head_probs(x_ref, own, allowed, width, h)
        probs = weights * (1.0 / total)
        prob_grad = contract_cols(values, grad)
        inner = jnp.sum(probs * prob_grad, 0, keepdims=True)
        score_grad = (probs * (prob_grad - inner)).astype(jnp.bfloat16)
        value_acc[h] += jnp.dot(
            probs.astype(jnp.bfloat16), grad, preferred_element_type=jnp.float32
        )
        key_acc[h] += jnp.dot(score_grad, own, preferred_element_type=jnp.float32)
        parts.append(contract_rows(keys, score_grad) * HEAD_DIM ** (-0.5))
    out_ref[pl.ds(start, block), :width] = jnp.concatenate(parts, 0).T.astype(out_ref.dtype)

    @pl.when(step == pl.num_programs(0) - 1)
    def _():
        out_ref[:, width : 2 * width] = jnp.concatenate(
            [key_acc[h] for h in range(heads)], 1
        ).astype(out_ref.dtype)
        out_ref[:, 2 * width :] = jnp.concatenate(
            [value_acc[h] for h in range(heads)], 1
        ).astype(out_ref.dtype)


def attend_back(whole, grads, prefix, block):
    length, cols = whole.shape
    width = cols // 3
    heads = width // HEAD_DIM
    return pl.pallas_call(
        attend_back_kernel,
        out_shape=jax.ShapeDtypeStruct((length, cols), whole.dtype),
        grid=(length // block,),
        in_specs=[
            pl.BlockSpec(memory_space=pltpu.SMEM),
            pl.BlockSpec((length, cols), lambda i: (0, 0)),
            pl.BlockSpec((block, width), lambda i: (i, 0)),
        ],
        out_specs=pl.BlockSpec((length, cols), lambda i: (0, 0)),
        scratch_shapes=[
            pltpu.VMEM((heads, length, HEAD_DIM), jnp.float32),
            pltpu.VMEM((heads, length, HEAD_DIM), jnp.float32),
        ],
        name="attend_back",
    )(prefix, whole, grads)


def gather_slots(rows):
    return lax.all_gather(rows, "dp", axis=0, tiled=True)


def scatter_slots(partial_sums):
    return lax.psum_scatter(partial_sums, "dp", scatter_dimension=0, tiled=True)


def sum_slots(partial_sums):
    return gather_slots(scatter_slots(partial_sums))


def own_slots(values):
    count = lax.axis_size("dp")
    size = values.shape[0] // count
    return lax.dynamic_slice_in_dim(values, lax.axis_index("dp") * size, size, 0)


def shards(
    tokens,
    cotangent,
    routes,
    prefix,
    qkv_weight,
    mix_weight,
    up_weight,
    down_weight,
    dense_gain,
    expert_up,
    expert_down,
    expert_gain,
    centroids,
):
    f32, low = jnp.float32, jnp.bfloat16
    micro_count, _, rows_dev, width = tokens.shape
    dp_count = lax.axis_size("dp")
    experts = lax.axis_size("expert")
    capacity = max(2, 5 * rows_dev // (4 * experts))
    length = rows_dev * dp_count
    mine = width // dp_count
    block = min(256, length)
    micros = range(micro_count)
    slot_ids = jnp.arange(experts * capacity, dtype=jnp.int32)
    expert_ids = jnp.arange(experts, dtype=jnp.int32)
    up_ex, down_ex, centroid = (expert_up[0], expert_down[0], centroids[0])
    gain_ex = expert_gain[0].astype(f32)

    places, grad_slots, grad_rows = ([], [], [])
    for micro in micros:
        route = routes[micro, 0, :, 0]
        onehot = (route[:, None] == expert_ids[None, :]).astype(jnp.int32)
        rank = jnp.sum((jnp.cumsum(onehot, 0) - 1) * onehot, 1)
        slot = route * capacity + rank
        place = (slot[None, :] == slot_ids[:, None]).astype(low)
        places.append(place)
        grad_sent = jnp.dot(
            place, cotangent[micro, 0].astype(low), preferred_element_type=f32
        ).astype(low)
        grad_slots.append(swap_experts(grad_sent))

    order_a, order_b = bit_orders()
    rows_qkv = qkv_weight.shape[0]
    by_dest = (
        qkv_weight.reshape(rows_qkv, 3, dp_count, mine)
        .transpose(0, 2, 1, 3)
        .reshape(rows_qkv, 3 * width)
    )
    half = 3 * width // 2
    gain_cols = jnp.pad(dense_gain.T, ((0, 0), (0, 126)))
    first = turn_gather(jnp.concatenate([by_dest, gain_cols], 1))
    part_a = spread(first[:, :, :half], order_a)
    part_b = spread(first[:, :, half:], order_b)
    qkv_pieces = dict(part_b)
    full_qkv = assemble(
        [(mask, jnp.concatenate([piece, qkv_pieces[mask][:, :, :half]], 2)) for mask, piece in part_a]
    )
    full_gain = assemble([(mask, piece[:, :, half:]) for mask, piece in part_b])
    gains = full_gain[:, :2].T.astype(f32)
    tie, by_dp_mix, by_dp_up, by_dp_down = (
        None,
        gather_dp(mix_weight),
        gather_dp(up_weight),
        gather_dp(down_weight),
    )
    full_mix = assemble(spread(by_dp_mix, order_a))
    full_up = assemble(spread(by_dp_up, order_a))
    full_down = assemble(spread(by_dp_down, order_b))
    for micro in micros:
        grad_rows.append(gather_slots(grad_slots[micro]))

    dense = []
    slots_in = []
    for micro in micros:
        source = tokens[micro, 0]
        if micro > 0:
            source, _ = lax.optimization_barrier((source, dense[micro - 1][6]))
        inputs = source.astype(f32)
        normed = layer_norm(inputs, gains[0]).astype(low)
        qkv = jnp.dot(normed, full_qkv, preferred_element_type=f32).astype(low)
        blocks = qkv.reshape(rows_dev, dp_count, 3 * mine).transpose(1, 0, 2)
        whole = swap_heads(blocks).reshape(length, 3 * mine)
        mixed = attend(whole, prefix[micro], block).reshape(dp_count, rows_dev, mine)
        mixed = swap_heads(mixed).transpose(1, 0, 2).reshape(rows_dev, width)
        attn = jnp.dot(mixed, full_mix, preferred_element_type=f32)
        resid = inputs + attn
        normed2 = layer_norm(resid, gains[1]).astype(low)
        pre = jnp.dot(normed2, full_up, preferred_element_type=f32)
        hidden = gelu(pre).astype(low)
        ffn = jnp.dot(hidden, full_down, preferred_element_type=f32)
        after = resid + ffn
        sent = jnp.dot(places[micro], after.astype(low), preferred_element_type=f32).astype(low)
        dense.append((inputs, normed, whole, mixed, attn, resid, ffn, normed2, pre, hidden, after))
        slots_in.append(swap_experts(sent))

    own_in, *grad_rows = lax.optimization_barrier((slots_in[0], *grad_rows))
    slots_in[0] = own_in
    up_sum = [None, None]
    down_sum = [None, None]
    gain_one = jnp.zeros((width,), f32)
    state = []
    for micro in micros:
        rows = gather_slots(slots_in[micro])
        sig = jax.nn.sigmoid(jnp.dot(rows, centroid, preferred_element_type=f32))[:, None]
        state0 = rows.astype(f32)
        z0 = layer_norm(state0, gain_ex[0]).astype(low)
        pre0 = jnp.dot(z0, up_ex[0], preferred_element_type=f32)
        h0 = gelu(pre0).astype(low)
        out0 = jnp.dot(h0, down_ex[0], preferred_element_type=f32).astype(low)
        state1 = state0 + sum_slots(out0).astype(f32)
        z1 = layer_norm(state1, gain_ex[1]).astype(low)
        pre1 = jnp.dot(z1, up_ex[1], preferred_element_type=f32)
        h1 = gelu(pre1).astype(low)
        out1 = jnp.dot(h1, down_ex[1], preferred_element_type=f32).astype(low)
        state.append((rows, sig, z0, pre0, h0, state1, z1, pre1, h1, out1))

    own_grads = []
    for micro in micros:
        rows, sig, z0, pre0, h0, state1, z1, pre1, h1, out1 = state[micro]
        incoming = grad_rows[micro].astype(f32)
        score_part = jnp.sum(incoming * out1.astype(f32), 1)
        grad2 = incoming * sig
        grad_y = grad2.astype(low)
        pre_grad = gelu_back(pre1, contract_cols(grad_y, down_ex[1])).astype(low)
        normed_grad = sum_slots(contract_cols(pre_grad, up_ex[1]).astype(low)).astype(f32)
        down_part, up_part = (contract_rows(h1, grad_y), contract_rows(z1, pre_grad))
        down_sum[1] = down_part if micro == 0 else down_sum[1] + down_part
        up_sum[1] = up_part if micro == 0 else up_sum[1] + up_part
        state_grad, gain_grad = norm_back(state1, gain_ex[1], normed_grad)
        gain_one = gain_one + gain_grad
        grad1 = grad2 + state_grad
        grad_y = grad1.astype(low)
        pre_grad = gelu_back(pre0, contract_cols(grad_y, down_ex[0])).astype(low)
        normed_grad = scatter_slots(contract_cols(pre_grad, up_ex[0]).astype(low)).astype(f32)
        down_part, up_part = (contract_rows(h0, grad_y), contract_rows(z0, pre_grad))
        down_sum[0] = down_part if micro == 0 else down_sum[0] + down_part
        up_sum[0] = up_part if micro == 0 else up_sum[0] + up_part
        own_rows = own_slots(rows).astype(f32)
        state_grad, gain_grad = norm_back(own_rows, gain_ex[0], normed_grad)
        own_sig = own_slots(sig)[:, 0]
        score_grad = own_slots(sum_small(score_part)) + jnp.sum(
            own_slots(incoming) * own_slots(state1), 1
        )
        score_grad = score_grad * own_sig * (1.0 - own_sig)
        row_grad = own_slots(grad1) + state_grad + score_grad[:, None] * centroid.astype(f32)
        cent_grad = jnp.sum(score_grad[:, None] * own_rows, 0)
        own_grads.append((row_grad.astype(low), gain_grad, cent_grad, normed_grad))

    gain_acc = jnp.zeros((2, width), f32)
    input_grads = []
    kept = []
    for micro in micros:
        inputs, normed, whole, mixed, attn, resid, ffn, normed2, pre, hidden, after = dense[micro]
        grad_back = swap_experts(own_grads[micro][0])
        after_grad = cotangent[micro, 0] + contract_rows(places[micro], grad_back)
        ffn_low = after_grad.astype(low)
        hidden_grad = contract_cols(ffn_low, full_down)
        pre_grad = gelu_back(pre, hidden_grad).astype(low)
        normed2_grad = contract_cols(pre_grad, full_up)
        resid_part, gain2_grad = norm_back(resid, gains[1], normed2_grad)
        resid_grad = after_grad + resid_part
        attn_low = resid_grad.astype(low)
        mixed_grad = contract_cols(attn_low, full_mix).astype(low)
        mixed_grad = mixed_grad.reshape(rows_dev, dp_count, mine).transpose(1, 0, 2)
        mixed_grad = swap_heads(mixed_grad).reshape(length, mine)
        whole_grad = attend_back(whole, mixed_grad, prefix[micro], block)
        qkv_grad = swap_heads(whole_grad.reshape(dp_count, rows_dev, 3 * mine))
        qkv_grad = qkv_grad.transpose(1, 0, 2).reshape(rows_dev, 3 * width)
        normed_grad = contract_cols(qkv_grad, full_qkv)
        input_part, gain1_grad = norm_back(inputs, gains[0], normed_grad)
        input_grads.append(resid_grad + input_part)
        gain_acc = gain_acc + jnp.stack([gain1_grad, gain2_grad])
        kept.append((normed, qkv_grad, mixed, attn_low, normed2, pre_grad, hidden, ffn_low))
    joined = [jnp.concatenate(parts, 0) for parts in zip(*kept)]
    order_c, order_d = (order_a[::-1], order_b[::-1])
    down_out = scatter_rows(contract_rows(joined[6], joined[7]).astype(low), order_c)
    up_out = scatter_rows(contract_rows(joined[4], joined[5]).astype(low), order_d)
    mix_out = scatter_rows(contract_rows(joined[2], joined[3]).astype(low), order_d)
    qkv_low = contract_rows(joined[0], joined[1]).astype(low)
    qkv_out = jnp.concatenate(
        [scatter_rows(qkv_low[:, :half], order_c), scatter_rows(qkv_low[:, half:], order_d)], 1
    )
    qkv_out = (
        qkv_out.reshape(rows_qkv, dp_count, 3, mine)
        .transpose(0, 2, 1, 3)
        .reshape(rows_qkv, 3 * width)
    )

    output_list = []
    stat_list = []
    for micro in micros:
        rows, sig, state1, out1 = (state[micro][i] for i in (0, 1, 5, 9))
        attn, ffn, after = (dense[micro][i] for i in (4, 6, 10))
        late, _ = lax.optimization_barrier((out1, own_grads[-1][3]))
        state2 = own_slots(state1) + scatter_slots(late).astype(f32)
        returned = swap_experts((own_slots(sig) * state2).astype(low))
        branch = contract_rows(places[micro], returned)
        final = after + branch
        output_list.append(final.astype(low))
        stat_list.append(jnp.stack([jnp.sum(v * v) for v in (final, attn, ffn, branch)]))

    small = jnp.concatenate(
        [
            jnp.stack(stat_list, 1).reshape(-1),
            sum(part[1] for part in own_grads),
            sum(part[2] for part in own_grads),
        ]
    )
    small = sum_small(small)
    stats = 4 * micro_count
    branch_rms = jnp.sqrt(small[:stats] / (length * width)).reshape(4, micro_count, 1)
    ex_gain = jnp.stack([small[stats : stats + width], gain_one])
    gain_sum = sum_small(gain_acc)
    for bit in order_a:
        gain_sum = gain_sum + swap(gain_sum, bit)
    device = lax.axis_index("dp") * experts + lax.axis_index("expert")
    gain_out = lax.dynamic_index_in_dim(
        gain_sum.reshape(2, dp_count * experts, -1), device, 1, keepdims=False
    )
    return (
        jnp.stack(output_list)[:, None],
        jnp.stack(input_grads)[:, None],
        qkv_out,
        mix_out,
        up_out,
        down_out,
        gain_out,
        jnp.stack(up_sum)[None],
        jnp.stack(down_sum)[None],
        ex_gain[None],
        small[None, stats + width :],
        branch_rms,
    )


def solution(mesh):
    return jax.shard_map(
        shards,
        mesh=mesh,
        in_specs=(
            P(None, "expert", "dp", None),
            P(None, "expert", "dp", None),
            P(None, "expert", "dp", None),
            P(None, "expert"),
            P(("dp", "expert"), None),
            P(("dp", "expert"), None),
            P(("dp", "expert"), None),
            P(("dp", "expert"), None),
            P(None, ("dp", "expert")),
            P("expert", None, None, "dp"),
            P("expert", None, "dp", None),
            P("expert", None, None),
            P("expert", None),
        ),
        out_specs=(
            P(None, "expert", "dp", None),
            P(None, "expert", "dp", None),
            P(("dp", "expert"), None),
            P(("dp", "expert"), None),
            P(("dp", "expert"), None),
            P(("dp", "expert"), None),
            P(None, ("dp", "expert")),
            P("expert", None, None, "dp"),
            P("expert", None, "dp", None),
            P("expert", None, None),
            P("expert", None),
            P(None, None, "expert"),
        ),
        check_vma=False,
    )
```

time: 1840 us -> 2400 us (1.30)
  Pallas kernels: 0 us -> 855 us
  waiting for transfers between devices: 942 us -> 818 us
  local copies, waits for them, and re-layouts: 174 us -> 81.3 us
  matrix products: 351 us -> 284 us
    pallas_call x0 -> x9, Pallas kernels: none -> 855 us  [the longest x5 776 us: assemble(): pl.pallas_call(functools.partial(assemble_kernel, masks), out_shape=jax.S...]
    all_gather x10, waiting for transfers between devices: 328 us -> 246 us  [the longest x8 246 us: gather_slots(): return lax.all_gather(rows, 'dp', axis=0, tiled=True)]
    dot_general x34 -> x22, matrix products: 164 us -> 105 us  [the longest x2 25.3 us: shards(): out1 = jnp.dot(h1, down_ex[1], preferred_element_type=f32).astype(low)]
    dynamic_update_slice x40 -> x3, local copies, waits for them, and re-layouts: 51.1 us -> 1.01 us  [turn_gather(): lax.dynamic_update_slice_in_dim(full, part[None], (own - shift) % count, 0)]
    ppermute x50 -> x53, waiting for transfers between devices: 179 us -> 139 us  [swap(): return lax.ppermute(values, 'expert', [(i, i ^ bit) for i in range(count)])]
    convert_element_type x15 -> x9, other arithmetic: 40.3 us -> 15.5 us  [the longest x2 8.21 us: shards(): incoming = grad_rows[micro].astype(f32)]
    all_gather x3 -> x1, blocking collectives: 55.2 us -> 44.1 us  [gather_dp(): return lax.all_gather(shard, 'dp', axis=0)]
    all_to_all x16 -> x15, starting transfers between devices: 78.9 us -> 70.3 us  [the longest x8 44.4 us: swap_heads(): return lax.all_to_all(blocks, 'dp', split_axis=0, concat_axis=0, tiled=True)]
  transfers between devices with their start and end apart: 90 -> 106, of which waited for: 46 -> 37; matrix products, arithmetic and copies ran while one was open for 31% -> 18% of each run, Pallas kernels for 0% -> 36%
where the time goes in v2:
time: 2400 us; the launch traced here: 2390 us
  Pallas kernels  855 us (36%)
  waiting for transfers between devices  818 us (34%)
  matrix products  284 us (12%)
  other arithmetic  138 us (6%)
  starting transfers between devices  133 us (6%)
  local copies, waits for them, and re-layouts  81.3 us (3%)
  blocking collectives  59 us (2%)
    pallas_call x5, Pallas kernels, assemble(): pl.pallas_call(functools.partial(assemble_kernel, masks), out_shape=jax.S...  776 us
    reduce_scatter x8, waiting for transfers between devices, scatter_slots(): return lax.psum_scatter(partial_sums, 'dp', scatter_dimension=0, tiled=True)  320 us
    all_gather x8, waiting for transfers between devices, gather_slots(): return lax.all_gather(rows, 'dp', axis=0, tiled=True)  246 us
    ppermute x53, waiting for transfers between devices, swap(): return lax.ppermute(values, 'expert', [(i, i ^ bit) for i in range(count)])  139 us
    dot_general x16, matrix products, contract_cols(): lax.dot_general(left, right, (((1,), (1,)), ((), ())), preferred_element_...  91.4 us
    dot_general x16, matrix products, contract_rows(): lax.dot_general(left, right, (((0,), (0,)), ((), ())), preferred_element_...  87 us
    all_to_all x8, waiting for transfers between devices, swap_heads(): return lax.all_to_all(blocks, 'dp', split_axis=0, concat_axis=0, tiled=True)  79.8 us
    pallas_call x2, Pallas kernels, attend_back(): pl.pallas_call(attend_back_kernel, out_shape=jax.ShapeDtypeStruct((length...  49.3 us
  transfers between devices with their start and end apart: 106, of which 37 were waited for; matrix products, arithmetic and copies ran while one was open for 18% of the time, Pallas kernels for 36%

profile of v2, /device:TPU:0, one launch (start us, length us, event | category | flops | bytes accessed | tf_op | source)
XLA Modules:
  0.0 2386.4 jit_solution(3242598839171316485)
XLA Ops:
  93.9 191.8 %assemble.6 = bf16[4,8,32,3072]{3,2,1,0:T(8,128)(2,1)} custom-call(bf16[4,32,3072]{2,1,0:T(8,128)(2,1)} %concatenate.77.refs_0_, bf16[4,32,3072]{2,1,0:T(8,128)(2,1)} %pad_maximum_fusion.refs_1_, bf16[4,32,3072]{2,1,0:T(8,128)(2,1)} %pad_maximum_fusion.1.refs_2_, bf16[4,32,3072]{2,1,0:T(8,128)(2,1)} %pad_maximum_fusion.2.refs_3_, ...), custom_call_target="tpu_custom_call" | custom-call | tf_op jit(solution)/shard_map/assemble/pallas_call | solution.py:91
  291.6 13.5 all-to-all-start
  306.6 44.1 %all-gather = bf16[128,1024]{1,0:T(8,128)(2,1)S(1)} all-gather(bf16[32,1024]{1,0:T(8,128)(2,1)S(1)} %copy-done.81), channel_id=2, replica_groups=mesh['dp'=4,'expert'=8] {'dp'}, dimensions={0}, use_global_device_ids=true | all-gather | bytes 327680 | tf_op jit(solution)/shard_map/all_gather | solution.py:110
  376.6 14.9 attend.2
  402.8 17.4 collective-permute-done.31.refs_1_
  422.9 64.7 %assemble.7 = bf16[4,8,32,1024]{3,2,1,0:T(8,128)(2,1)} custom-call(bf16[4,32,1024]{2,1,0:T(8,128)(2,1)} %bitcast.455, bf16[4,32,1024]{2,1,0:T(8,128)(2,1)} %copy-done.71, bf16[4,32,1024]{2,1,0:T(8,128)(2,1)} %copy-done.72, bf16[4,32,1024]{2,1,0:T(8,128)(2,1)} %copy-done.74, bf16[4,32,1024]{2,1,0:T(8,128)(2,1)} %copy-done.73, ...), custom_call_target="tpu_custom_call" | custom-call | tf_op jit(solution)/shard_map/assemble/pallas_call | solution.py:91
  493.5 255.3 %assemble.8 = bf16[4,8,32,4096]{3,2,1,0:T(8,128)(2,1)} custom-call(bf16[4,32,4096]{2,1,0:T(8,128)(2,1)} %bitcast.451, bf16[4,32,4096]{2,1,0:T(8,128)(2,1)} %collective-permute-done.24.refs_1_, bf16[4,32,4096]{2,1,0:T(8,128)(2,1)} %collective-permute-done.25.refs_2_, bf16[4,32,4096]{2,1,0:T(8,128)(2,1)} %collective-permute-done.26.refs_3_, ...), custom_call_target="tpu_custom_call" | custom-call | tf_op jit(solution)/shard_map/assemble/pallas_call | solution.py:91
  759.0 255.3 %assemble.9 = bf16[4,8,128,1024]{3,2,1,0:T(8,128)(2,1)} custom-call(bf16[4,128,1024]{2,1,0:T(8,128)(2,1)} %bitcast.23.refs_0_, bf16[4,128,1024]{2,1,0:T(8,128)(2,1)} %collective-permute-done.31.refs_1_, bf16[4,128,1024]{2,1,0:T(8,128)(2,1)} %collective-permute-done.32.refs_2_, bf16[4,128,1024]{2,1,0:T(8,128)(2,1)} %collective-permute-done.33.refs_3_, ...), custom_call_target="tpu_custom_call" | custom-call | tf_op jit(solution)/shard_map/assemble/pallas_call | solution.py:91
  1036.3 35.3 %all-to-all-done.5 = bf16[4,256,768]{2,1,0:T(8,128)(2,1)} async-done(((bf16[4,256,768]{2,1,0:T(8,128)(2,1)}), bf16[4,256,768]{2,1,0:T(8,128)(2,1)}, u32[]{:S(2)}, u32[]{:S(2)}) %all-to-all-start.5) | async-done | bytes 1572896 | tf_op jit(solution)/shard_map/all_to_all | solution.py:145
  1075.4 14.9 attend.3
  1097.2 14.9 all-to-all-done.6
  1129.1 14.9 all_to_all.80
  1170.4 39.9 %all-gather.22.cloned.1.call-done = bf16[1280,1024]{1,0:T(8,128)(2,1)} async-done(((bf16[320,1024]{1,0:T(8,128)(2,1)}), bf16[1280,1024]{1,0:T(8,128)(2,1)}) %all-gather.22.cloned.1.call-update) | async-done | bytes 2621456 | tf_op jit(solution)/shard_map/all_gather | solution.py:264
  1225.4 38.2 %reduce-scatter.14.cloned.1.call-done = bf16[320,1024]{1,0:T(8,128)(2,1)} async-done(((bf16[1280,1024]{1,0:T(8,128)(2,1)}), bf16[320,1024]{1,0:T(8,128)(2,1)}) %reduce-scatter.14.cloned.1.call-update) | async-done | bytes 655376 | tf_op jit(solution)/shard_map/reduce_scatter | solution.py:268
  1264.5 53.2 %reduce-scatter.16.cloned.1.call-done = bf16[320,1024]{1,0:T(8,128)(2,1)} async-done(((bf16[1280,1024]{1,0:T(8,128)(2,1)}), bf16[320,1024]{1,0:T(8,128)(2,1)}) %reduce-scatter.16.cloned.1.call-update) | async-done | bytes 655376 | tf_op jit(solution)/shard_map/reduce_scatter | solution.py:268
  1318.0 55.7 %all-gather.20.cloned.1.call-done = bf16[1280,1024]{1,0:T(8,128)(2,1)} async-done(((bf16[320,1024]{1,0:T(8,128)(2,1)}), bf16[1280,1024]{1,0:T(8,128)(2,1)}) %all-gather.20.cloned.1.call-update) | async-done | bytes 2621456 | tf_op jit(solution)/shard_map/all_gather | solution.py:264
  1395.5 33.2 %all-gather.24.cloned.1.call-done = bf16[1280,1024]{1,0:T(8,128)(2,1)} async-done(((bf16[320,1024]{1,0:T(8,128)(2,1)}), bf16[1280,1024]{1,0:T(8,128)(2,1)}) %all-gather.24.cloned.1.call-update) | async-done | bytes 2621456 | tf_op jit(solution)/shard_map/all_gather | solution.py:264
  1449.4 32.6 %reduce-scatter.26.cloned.1.call-done = bf16[320,1024]{1,0:T(8,128)(2,1)} async-done(((bf16[1280,1024]{1,0:T(8,128)(2,1)}), bf16[320,1024]{1,0:T(8,128)(2,1)}) %reduce-scatter.26.cloned.1.call-update) | async-done | bytes 655376 | tf_op jit(solution)/shard_map/reduce_scatter | solution.py:268
  1482.1 53.9 %reduce-scatter.18.cloned.1.call-done = bf16[320,1024]{1,0:T(8,128)(2,1)} async-done(((bf16[1280,1024]{1,0:T(8,128)(2,1)}), bf16[320,1024]{1,0:T(8,128)(2,1)}) %reduce-scatter.18.cloned.1.call-update) | async-done | bytes 655376 | tf_op jit(solution)/shard_map/reduce_scatter | solution.py:268
  1536.5 55.4 %all-gather.28.cloned.1.call-done = bf16[1280,1024]{1,0:T(8,128)(2,1)} async-done(((bf16[320,1024]{1,0:T(8,128)(2,1)}), bf16[1280,1024]{1,0:T(8,128)(2,1)}) %all-gather.28.cloned.1.call-update) | async-done | bytes 2621456 | tf_op jit(solution)/shard_map/all_gather | solution.py:264
  1596.0 50.9 %all-gather.26.cloned.1.call-done = bf16[1280,1024]{1,0:T(8,128)(2,1)} async-done(((bf16[320,1024]{1,0:T(8,128)(2,1)}), bf16[1280,1024]{1,0:T(8,128)(2,1)}) %all-gather.26.cloned.1.call-update) | async-done | bytes 2621456 | tf_op jit(solution)/shard_map/all_gather | solution.py:264
  1657.3 14.9 add_add_fusion.2
  1698.6 51.1 %reduce-scatter.20.cloned.1.call-done = bf16[320,1024]{1,0:T(8,128)(2,1)} async-done(((bf16[1280,1024]{1,0:T(8,128)(2,1)}), bf16[320,1024]{1,0:T(8,128)(2,1)}) %reduce-scatter.20.cloned.1.call-update) | async-done | bytes 655376 | tf_op jit(solution)/shard_map/reduce_scatter | solution.py:268
  1814.0 43.9 %reduce-scatter.22.cloned.1.call-done = bf16[320,1024]{1,0:T(8,128)(2,1)} async-done(((bf16[1280,1024]{1,0:T(8,128)(2,1)}), bf16[320,1024]{1,0:T(8,128)(2,1)}) %reduce-scatter.22.cloned.1.call-update) | async-done | bytes 655376 | tf_op jit(solution)/shard_map/reduce_scatter | solution.py:268
  1864.6 47.3 %reduce-scatter.28.cloned.1.call-done = bf16[320,1024]{1,0:T(8,128)(2,1)} async-done(((bf16[1280,1024]{1,0:T(8,128)(2,1)}), bf16[320,1024]{1,0:T(8,128)(2,1)}) %reduce-scatter.28.cloned.1.call-update) | async-done | bytes 655376 | tf_op jit(solution)/shard_map/reduce_scatter | solution.py:268
  2030.0 24.7 %attend_back.3 = bf16[1024,768]{1,0:T(8,128)(2,1)} custom-call(s32[1]{0:T(128)} %bitcast.48.prefix_ref, bf16[1024,768]{1,0:T(8,128)(2,1)} %bitcast.50.x_ref, bf16[1024,256]{1,0:T(8,128)(2,1)} %bitcast.75.grad_ref), custom_call_target="tpu_custom_call" | custom-call | tf_op jit(solution)/shard_map/attend_back/pallas_call | solution.py:245
  2089.4 24.6 %attend_back.2 = bf16[1024,768]{1,0:T(8,128)(2,1)} custom-call(s32[1]{0:T(128)} %bitcast.1.prefix_ref, bf16[1024,768]{1,0:T(8,128)(2,1)} %bitcast.392, bf16[1024,256]{1,0:T(8,128)(2,1)} %bitcast.67.grad_ref), custom_call_target="tpu_custom_call" | custom-call | tf_op jit(solution)/shard_map/attend_back/pallas_call | solution.py:245
  2142.7 20.1 all-to-all-done.12
  2210.0 48.4 %collective-permute-done.45 = bf16[4,2,32,1536]{3,2,1,0:T(8,128)(2,1)S(1)} collective-permute-done((bf16[4,2,32,1536]{3,2,1,0:T(8,128)(2,1)S(1)}, bf16[4,2,32,1536]{3,2,1,0:T(8,128)(2,1)S(1)}, u32[]{:S(2)}, u32[]{:S(2)}) %collective-permute-start.45) | collective-permute-done | bytes 786464 | tf_op jit(solution)/shard_map/ppermute | solution.py:50
  2262.8 16.3 collective-permute-done.46
  2293.9 16.4 collective-permute-done.58
  2364.3 13.6 reduce-scatter.36.cloned.1.call-done
  (815 shorter events, 697.7 us)
Async XLA Ops:
  7.2 297.9 %all-gather.30.cloned.1.call-start = ((), (), s32[]{:S(2)}) async-start(), calls=%async_computation.50 | async-start | bytes 1310720 | tf_op jit(solution)/shard_map/all_gather | solution.py:110
  26.1 335.0 %all-gather.32.cloned.1.call-start = ((), (), s32[]{:S(2)}) async-start(), calls=%async_computation.51 | async-start | bytes 1310720 | tf_op jit(solution)/shard_map/all_gather | solution.py:110
  26.8 1069.8 %all-gather.14.cloned.1.call-start = ((), (), s32[]{:S(2)}) async-start(), calls=%async_computation.29 | async-start | bytes 3276800 | tf_op jit(solution)/shard_map/all_gather | solution.py:264
  363.1 124.6 %collective-permute-start.26 = (bf16[4,32,4096]{2,1,0:T(8,128)(2,1)}, bf16[4,32,4096]{2,1,0:T(8,128)(2,1)}, u32[]{:S(2)}, u32[]{:S(2)}) collective-permute-start(bf16[4,32,4096]{2,1,0:T(8,128)(2,1)} %collective-permute-done.24.refs_1_), channel_id=1, source_target_pairs={{0,2},{1,3},{2,0},{3,1},{4,6},{5,7},{6,4},{7,5},{8,10},{9,11},{10,... | collective-permute-start | bytes 3145736 | tf_op jit(solution)/shard_map/ppermute | solution.py:50
  393.6 94.1 %all-to-all-start.1 = ((bf16[4,256,256]{1,2,0:T(8,128)(2,1)}), bf16[4,256,256]{1,2,0:T(8,128)(2,1)S(1)}, u32[]{:S(2)}, u32[]{:S(2)}) async-start(bf16[4,256,256]{1,2,0:T(8,128)(2,1)} %copy.58), calls=%async_computation.1 | async-start | bytes 1048576 | tf_op jit(solution)/shard_map/all_to_all | solution.py:145
  397.1 699.5 %all-gather.16.cloned.1.call-start = ((), (), s32[]{:S(2)}) async-start(), calls=%async_computation.30 | async-start | bytes 3276800 | tf_op jit(solution)/shard_map/all_gather | solution.py:264
  400.8 91.3 %collective-permute-start.32 = (bf16[4,128,1024]{2,1,0:T(8,128)(2,1)}, bf16[4,128,1024]{2,1,0:T(8,128)(2,1)}, u32[]{:S(2)}, u32[]{:S(2)}) collective-permute-start(bf16[4,128,1024]{2,1,0:T(8,128)(2,1)} %bitcast.23.refs_0_), channel_id=1, source_target_pairs={{0,4},{1,5},{2,6},{3,7},{4,0},{5,1},{6,2},{7,3},{8,12},{9,13},{10,... | collective-permute-start | bytes 3145736 | tf_op jit(solution)/shard_map/ppermute | solution.py:50
  402.3 90.4 %collective-permute-start.28 = (bf16[4,32,4096]{2,1,0:T(8,128)(2,1)}, bf16[4,32,4096]{2,1,0:T(8,128)(2,1)}, u32[]{:S(2)}, u32[]{:S(2)}) collective-permute-start(bf16[4,32,4096]{2,1,0:T(8,128)(2,1)} %collective-permute-done.24.refs_1_), channel_id=1, source_target_pairs={{0,1},{1,0},{2,3},{3,2},{4,5},{5,4},{6,7},{7,6},{8,9},{9,8},{10,11... | collective-permute-start | bytes 3145736 | tf_op jit(solution)/shard_map/ppermute | solution.py:50
  402.4 90.4 %collective-permute-start.29 = (bf16[4,32,4096]{2,1,0:T(8,128)(2,1)}, bf16[4,32,4096]{2,1,0:T(8,128)(2,1)}, u32[]{:S(2)}, u32[]{:S(2)}) collective-permute-start(bf16[4,32,4096]{2,1,0:T(8,128)(2,1)} %collective-permute-done.25.refs_2_), channel_id=1, source_target_pairs={{0,1},{1,0},{2,3},{3,2},{4,5},{5,4},{6,7},{7,6},{8,9},{9,8},{10,11... | collective-permute-start | bytes 3145736 | tf_op jit(solution)/shard_map/ppermute | solution.py:50
  492.1 265.9 %collective-permute-start.34 = (bf16[4,128,1024]{2,1,0:T(8,128)(2,1)}, bf16[4,128,1024]{2,1,0:T(8,128)(2,1)S(1)}, u32[]{:S(2)}, u32[]{:S(2)}) collective-permute-start(bf16[4,128,1024]{2,1,0:T(8,128)(2,1)} %bitcast.23.refs_0_), channel_id=1, source_target_pairs={{0,1},{1,0},{2,3},{3,2},{4,5},{5,4},{6,7},{7,6},{8,9},{9,8},{10,11... | collective-permute-start | bytes 3145736 | tf_op jit(solution)/shard_map/ppermute | solution.py:50
  492.7 265.3 %collective-permute-start.35 = (bf16[4,128,1024]{2,1,0:T(8,128)(2,1)}, bf16[4,128,1024]{2,1,0:T(8,128)(2,1)}, u32[]{:S(2)}, u32[]{:S(2)}) collective-permute-start(bf16[4,128,1024]{2,1,0:T(8,128)(2,1)} %collective-permute-done.31.refs_1_), channel_id=1, source_target_pairs={{0,1},{1,0},{2,3},{3,2},{4,5},{5,4},{6,7},{7,6},{8,9},{9,8},{10,11... | collective-permute-start | bytes 3145736 | tf_op jit(solution)/shard_map/ppermute | solution.py:50
  492.8 265.2 %collective-permute-start.36 = (bf16[4,128,1024]{2,1,0:T(8,128)(2,1)}, bf16[4,128,1024]{2,1,0:T(8,128)(2,1)}, u32[]{:S(2)}, u32[]{:S(2)}) collective-permute-start(bf16[4,128,1024]{2,1,0:T(8,128)(2,1)} %collective-permute-done.32.refs_2_), channel_id=1, source_target_pairs={{0,1},{1,0},{2,3},{3,2},{4,5},{5,4},{6,7},{7,6},{8,9},{9,8},{10,11... | collective-permute-start | bytes 3145736 | tf_op jit(solution)/shard_map/ppermute | solution.py:50
  493.2 264.8 %collective-permute-start.37 = (bf16[4,128,1024]{2,1,0:T(8,128)(2,1)}, bf16[4,128,1024]{2,1,0:T(8,128)(2,1)}, u32[]{:S(2)}, u32[]{:S(2)}) collective-permute-start(bf16[4,128,1024]{2,1,0:T(8,128)(2,1)} %collective-permute-done.33.refs_3_), channel_id=1, source_target_pairs={{0,1},{1,0},{2,3},{3,2},{4,5},{5,4},{6,7},{7,6},{8,9},{9,8},{10,11... | collective-permute-start | bytes 3145736 | tf_op jit(solution)/shard_map/ppermute | solution.py:50
  1097.2 113.1 %all-gather.22.cloned.1.call-start = ((), (), s32[]{:S(2)}) async-start(), calls=%async_computation.34 | async-start | bytes 3276800 | tf_op jit(solution)/shard_map/all_gather | solution.py:264
  1144.0 119.6 %reduce-scatter.14.cloned.1.call-start = ((), (), s32[]{:S(2)}) async-start(), calls=%async_computation.32 | async-start | bytes 3276800 | tf_op jit(solution)/shard_map/reduce_scatter | solution.py:268
  1170.3 147.4 %reduce-scatter.16.cloned.1.call-start = ((), (), s32[]{:S(2)}) async-start(), calls=%async_computation.35 | async-start | bytes 3276800 | tf_op jit(solution)/shard_map/reduce_scatter | solution.py:268
  1225.3 148.3 %all-gather.20.cloned.1.call-start = ((), (), s32[]{:S(2)}) async-start(), calls=%async_computation.33 | async-start | bytes 3276800 | tf_op jit(solution)/shard_map/all_gather | solution.py:264
  1263.6 165.0 %all-gather.24.cloned.1.call-start = ((), (), s32[]{:S(2)}) async-start(), calls=%async_computation.36 | async-start | bytes 3276800 | tf_op jit(solution)/shard_map/all_gather | solution.py:264
  1317.8 164.2 %reduce-scatter.26.cloned.1.call-start = ((), (), s32[]{:S(2)}) async-start(), calls=%async_computation.42 | async-start | bytes 3276800 | tf_op jit(solution)/shard_map/reduce_scatter | solution.py:268
  1392.6 143.3 %reduce-scatter.18.cloned.1.call-start = ((), (), s32[]{:S(2)}) async-start(), calls=%async_computation.37 | async-start | bytes 3276800 | tf_op jit(solution)/shard_map/reduce_scatter | solution.py:268
  1449.3 142.5 %all-gather.28.cloned.1.call-start = ((), (), s32[]{:S(2)}) async-start(), calls=%async_computation.43 | async-start | bytes 3276800 | tf_op jit(solution)/shard_map/all_gather | solution.py:264
  1482.0 164.8 %all-gather.26.cloned.1.call-start = ((), (), s32[]{:S(2)}) async-start(), calls=%async_computation.38 | async-start | bytes 3276800 | tf_op jit(solution)/shard_map/all_gather | solution.py:264
  1536.0 213.8 %reduce-scatter.20.cloned.1.call-start = ((), (), s32[]{:S(2)}) async-start(), calls=%async_computation.39 | async-start | bytes 3276800 | tf_op jit(solution)/shard_map/reduce_scatter | solution.py:268
  1698.6 111.9 %reduce-scatter.24.cloned.1.call-start = ((), (), s32[]{:S(2)}) async-start(), calls=%async_computation.41 | async-start | bytes 3276800 | tf_op jit(solution)/shard_map/reduce_scatter | solution.py:268
  1749.8 108.1 %reduce-scatter.22.cloned.1.call-start = ((), (), s32[]{:S(2)}) async-start(), calls=%async_computation.40 | async-start | bytes 3276800 | tf_op jit(solution)/shard_map/reduce_scatter | solution.py:268
  1750.4 161.5 %reduce-scatter.28.cloned.1.call-start = ((), (), s32[]{:S(2)}) async-start(), calls=%async_computation.44 | async-start | bytes 3276800 | tf_op jit(solution)/shard_map/reduce_scatter | solution.py:268
  2121.7 221.3 %reduce-scatter.34.cloned.1.call-start = ((), (), s32[]{:S(2)}) async-start(), calls=%async_computation.47 | async-start | bytes 327680 | tf_op jit(solution)/shard_map/reduce_scatter | solution.py:139
  2162.8 155.7 %all-to-all-start.9 = ((bf16[8,40,1024]{2,1,0:T(8,128)(2,1)}), bf16[8,40,1024]{2,1,0:T(8,128)(2,1)S(1)}, u32[]{:S(2)}, u32[]{:S(2)}) async-start(bf16[8,40,1024]{2,1,0:T(8,128)(2,1)} %bitcast.59), calls=%async_computation.15 | async-start | bytes 1310720 | tf_op jit(solution)/shard_map/all_to_all | solution.py:151
  2166.4 193.8 %reduce-scatter.30.cloned.1.call-start = ((), (), s32[]{:S(2)}) async-start(), calls=%async_computation.45 | async-start | bytes 491520 | tf_op jit(solution)/shard_map/reduce_scatter | solution.py:139
  2193.4 86.9 %collective-permute-start.57 = (bf16[4,2,128,1024]{3,2,1,0:T(8,128)(2,1)}, bf16[4,2,128,1024]{3,2,1,0:T(8,128)(2,1)}, u32[]{:S(2)}, u32[]{:S(2)}) collective-permute-start(bf16[4,2,128,1024]{3,2,1,0:T(8,128)(2,1)} %dynamic-slice_bitcast_fusion.2), channel_id=1, source_target_pairs={{0,2},{1,3},{2,0},{3,1},{4,6},{5,7},{6,4},{7,5},{8,10},{9,11},{10,... | collective-permute-start | bytes 6291464 | tf_op jit(solution)/shard_map/ppermute | solution.py:50
  2209.4 79.9 %collective-permute-start.54 = (bf16[4,2,32,4096]{3,2,1,0:T(8,128)(2,1)}, bf16[4,2,32,4096]{3,2,1,0:T(8,128)(2,1)}, u32[]{:S(2)}, u32[]{:S(2)}) collective-permute-start(bf16[4,2,32,4096]{3,2,1,0:T(8,128)(2,1)} %dynamic-slice_bitcast_fusion.3), channel_id=1, source_target_pairs={{0,4},{1,5},{2,6},{3,7},{4,0},{5,1},{6,2},{7,3},{8,12},{9,13},{10,... | collective-permute-start | bytes 6291464 | tf_op jit(solution)/shard_map/ppermute | solution.py:50
  2280.0 80.2 %reduce-scatter.32.cloned.1.call-start = ((), (), s32[]{:S(2)}) async-start(), calls=%async_computation.46 | async-start | bytes 491520 | tf_op jit(solution)/shard_map/reduce_scatter | solution.py:139
  (243 other events, 9406.7 us)
Sparse Core Ops, SparseCore 0:
  9.6 39.4 all-gather.29
  50.6 29.3 all-gather.31
  81.6 54.1 all-gather.13
  423.0 52.0 all-gather.15
  1098.6 56.6 all-gather.17
  1156.7 53.4 all-gather.21
  1212.6 51.0 reduce-scatter.13
  1265.9 51.7 reduce-scatter.15
  1319.3 54.2 all-gather.19
  1375.1 53.5 all-gather.23
  1430.9 51.0 reduce-scatter.25
  1484.1 51.7 reduce-scatter.17
  1537.6 54.2 all-gather.27
  1593.3 53.5 all-gather.25
  1698.7 51.0 reduce-scatter.19
  1751.9 51.7 reduce-scatter.23
  1805.9 51.9 reduce-scatter.21
  1860.0 51.8 reduce-scatter.27
  2137.4 26.6 reduce-scatter.33
  2280.2 19.0 reduce-scatter.29
  2302.1 19.1 reduce-scatter.31
  2323.6 25.7 reduce-scatter.37
  2351.7 26.1 reduce-scatter.35

commit v3 on v2

--- a/solution.py
+++ b/solution.py
@@ -71,17 +71,29 @@
 
 
 def assemble_kernel(masks, *refs):
-    pieces, full, sems = refs[: len(masks)], refs[-2], refs[-1]
+    count = len(masks)
+    pieces, full, held, in_sems, out_sems = (
+        refs[:count],
+        refs[count],
+        refs[count + 1],
+        refs[count + 2],
+        refs[count + 3],
+    )
     own = lax.axis_index("expert")
-    copies = []
-    for i, mask in enumerate(masks):
-        copies.append(
-            pltpu.make_async_copy(pieces[i], full.at[:, jnp.bitwise_xor(own, mask)], sems.at[i])
+    loads = [pltpu.make_async_copy(pieces[i], held.at[i], in_sems.at[i]) for i in range(count)]
+    stores = [
+        pltpu.make_async_copy(
+            held.at[i], full.at[:, jnp.bitwise_xor(own, mask)], out_sems.at[i]
         )
-    for copy in copies:
-        copy.start()
-    for copy in copies:
-        copy.wait()
+        for i, mask in enumerate(masks)
+    ]
+    for load in loads:
+        load.start()
+    for load, store in zip(loads, stores):
+        load.wait()
+        store.start()
+    for store in stores:
+        store.wait()
 
 
 def assemble(pieces):
@@ -93,7 +105,11 @@
         out_shape=jax.ShapeDtypeStruct((dp_count, len(masks), rows, cols), arrays[0].dtype),
         in_specs=[pl.BlockSpec(memory_space=pl.ANY)] * len(masks),
         out_specs=pl.BlockSpec(memory_space=pl.ANY),
-        scratch_shapes=[pltpu.SemaphoreType.DMA((len(masks),))],
+        scratch_shapes=[
+            pltpu.VMEM((len(masks), dp_count, rows, cols), arrays[0].dtype),
+            pltpu.SemaphoreType.DMA((len(masks),)),
+            pltpu.SemaphoreType.DMA((len(masks),)),
+        ],
         name="assemble",
     )(*arrays)
     return full.reshape(dp_count * len(masks) * rows, cols)
@@ -258,6 +274,10 @@
         ],
         name="attend_back",
     )(prefix, whole, grads)
+
+
+def after(value, *others):
+    return lax.optimization_barrier((value,) + others)[0]
 
 
 def gather_slots(rows):
@@ -338,15 +358,9 @@
     )
     full_gain = assemble([(mask, piece[:, :, half:]) for mask, piece in part_b])
     gains = full_gain[:, :2].T.astype(f32)
-    tie, by_dp_mix, by_dp_up, by_dp_down = (
-        None,
-        gather_dp(mix_weight),
-        gather_dp(up_weight),
-        gather_dp(down_weight),
-    )
-    full_mix = assemble(spread(by_dp_mix, order_a))
-    full_up = assemble(spread(by_dp_up, order_a))
-    full_down = assemble(spread(by_dp_down, order_b))
+    full_mix = assemble(spread(turn_gather(mix_weight), order_a))
+    full_up = assemble(spread(gather_dp(up_weight), order_a))
+    full_down = assemble(spread(gather_dp(down_weight), order_b))
     for micro in micros:
         grad_rows.append(gather_slots(grad_slots[micro]))
 
@@ -355,7 +369,7 @@
     for micro in micros:
         source = tokens[micro, 0]
         if micro > 0:
-            source, _ = lax.optimization_barrier((source, dense[micro - 1][6]))
+            source = after(source, slots_in[micro - 1])
         inputs = source.astype(f32)
         normed = layer_norm(inputs, gains[0]).astype(low)
         qkv = jnp.dot(normed, full_qkv, preferred_element_type=f32).astype(low)
@@ -369,9 +383,9 @@
         pre = jnp.dot(normed2, full_up, preferred_element_type=f32)
         hidden = gelu(pre).astype(low)
         ffn = jnp.dot(hidden, full_down, preferred_element_type=f32)
-        after = resid + ffn
-        sent = jnp.dot(places[micro], after.astype(low), preferred_element_type=f32).astype(low)
-        dense.append((inputs, normed, whole, mixed, attn, resid, ffn, normed2, pre, hidden, after))
+        dense_out = resid + ffn
+        sent = jnp.dot(places[micro], dense_out.astype(low), preferred_element_type=f32).astype(low)
+        dense.append((inputs, normed, whole, mixed, attn, resid, ffn, normed2, pre, hidden, dense_out))
         slots_in.append(swap_experts(sent))
 
     own_in, *grad_rows = lax.optimization_barrier((slots_in[0], *grad_rows))
@@ -379,43 +393,67 @@
     up_sum = [None, None]
     down_sum = [None, None]
     gain_one = jnp.zeros((width,), f32)
-    state = []
+
+    first_stage = []
     for micro in micros:
         rows = gather_slots(slots_in[micro])
+        if micro > 0:
+            rows = after(rows, first_stage[micro - 1][-1])
         sig = jax.nn.sigmoid(jnp.dot(rows, centroid, preferred_element_type=f32))[:, None]
         state0 = rows.astype(f32)
         z0 = layer_norm(state0, gain_ex[0]).astype(low)
         pre0 = jnp.dot(z0, up_ex[0], preferred_element_type=f32)
         h0 = gelu(pre0).astype(low)
         out0 = jnp.dot(h0, down_ex[0], preferred_element_type=f32).astype(low)
-        state1 = state0 + sum_slots(out0).astype(f32)
+        first_stage.append((rows, sig, z0, pre0, h0, out0))
+    summed0 = [sum_slots(first_stage[micro][-1]) for micro in micros]
+    second_stage = []
+    for micro in micros:
+        rows, sig = first_stage[micro][:2]
+        total = summed0[micro]
+        if micro > 0:
+            total = after(total, second_stage[micro - 1][-1])
+        state1 = rows.astype(f32) + total.astype(f32)
         z1 = layer_norm(state1, gain_ex[1]).astype(low)
         pre1 = jnp.dot(z1, up_ex[1], preferred_element_type=f32)
         h1 = gelu(pre1).astype(low)
         out1 = jnp.dot(h1, down_ex[1], preferred_element_type=f32).astype(low)
-        state.append((rows, sig, z0, pre0, h0, state1, z1, pre1, h1, out1))
-
-    own_grads = []
-    for micro in micros:
-        rows, sig, z0, pre0, h0, state1, z1, pre1, h1, out1 = state[micro]
         incoming = grad_rows[micro].astype(f32)
         score_part = jnp.sum(incoming * out1.astype(f32), 1)
         grad2 = incoming * sig
         grad_y = grad2.astype(low)
         pre_grad = gelu_back(pre1, contract_cols(grad_y, down_ex[1])).astype(low)
-        normed_grad = sum_slots(contract_cols(pre_grad, up_ex[1]).astype(low)).astype(f32)
-        down_part, up_part = (contract_rows(h1, grad_y), contract_rows(z1, pre_grad))
-        down_sum[1] = down_part if micro == 0 else down_sum[1] + down_part
-        up_sum[1] = up_part if micro == 0 else up_sum[1] + up_part
-        state_grad, gain_grad = norm_back(state1, gain_ex[1], normed_grad)
+        normed_part = contract_cols(pre_grad, up_ex[1]).astype(low)
+        second_stage.append(
+            (state1, out1, incoming, score_part, grad2, z1, h1, grad_y, pre_grad, normed_part)
+        )
+    summed1 = [sum_slots(second_stage[micro][-1]) for micro in micros]
+    third_stage = []
+    for micro in micros:
+        rows, sig, z0, pre0, h0, _ = first_stage[micro]
+        state1, _, _, _, grad2, z1, h1, grad_y1, pre_grad1, _ = second_stage[micro]
+        total = summed1[micro]
+        if micro > 0:
+            total = after(total, third_stage[micro - 1][-1])
+        state_grad, gain_grad = norm_back(state1, gain_ex[1], total.astype(f32))
         gain_one = gain_one + gain_grad
         grad1 = grad2 + state_grad
         grad_y = grad1.astype(low)
         pre_grad = gelu_back(pre0, contract_cols(grad_y, down_ex[0])).astype(low)
-        normed_grad = scatter_slots(contract_cols(pre_grad, up_ex[0]).astype(low)).astype(f32)
+        normed_part = contract_cols(pre_grad, up_ex[0]).astype(low)
+        down_part, up_part = (contract_rows(h1, grad_y1), contract_rows(z1, pre_grad1))
+        down_sum[1] = down_part if micro == 0 else down_sum[1] + down_part
+        up_sum[1] = up_part if micro == 0 else up_sum[1] + up_part
         down_part, up_part = (contract_rows(h0, grad_y), contract_rows(z0, pre_grad))
         down_sum[0] = down_part if micro == 0 else down_sum[0] + down_part
         up_sum[0] = up_part if micro == 0 else up_sum[0] + up_part
+        third_stage.append((grad1, normed_part))
+    own_grads = []
+    for micro in micros:
+        rows, sig = first_stage[micro][:2]
+        state1, _, incoming, score_part = second_stage[micro][:4]
+        grad1, normed_part = third_stage[micro]
+        normed_grad = scatter_slots(normed_part).astype(f32)
         own_rows = own_slots(rows).astype(f32)
         state_grad, gain_grad = norm_back(own_rows, gain_ex[0], normed_grad)
         own_sig = own_slots(sig)[:, 0]
@@ -431,7 +469,7 @@
     input_grads = []
     kept = []
     for micro in micros:
-        inputs, normed, whole, mixed, attn, resid, ffn, normed2, pre, hidden, after = dense[micro]
+        inputs, normed, whole, mixed, attn, resid, ffn, normed2, pre, hidden, _ = dense[micro]
         grad_back = swap_experts(own_grads[micro][0])
         after_grad = cotangent[micro, 0] + contract_rows(places[micro], grad_back)
         ffn_low = after_grad.astype(low)
@@ -470,13 +508,14 @@
     output_list = []
     stat_list = []
     for micro in micros:
-        rows, sig, state1, out1 = (state[micro][i] for i in (0, 1, 5, 9))
-        attn, ffn, after = (dense[micro][i] for i in (4, 6, 10))
-        late, _ = lax.optimization_barrier((out1, own_grads[-1][3]))
-        state2 = own_slots(state1) + scatter_slots(late).astype(f32)
+        sig = first_stage[micro][1]
+        state1, out1 = second_stage[micro][:2]
+        attn, ffn, dense_out = (dense[micro][i] for i in (4, 6, 10))
+        late = scatter_slots(after(out1, own_grads[-1][3]))
+        state2 = own_slots(state1) + after(late, kept[-1][1]).astype(f32)
         returned = swap_experts((own_slots(sig) * state2).astype(low))
         branch = contract_rows(places[micro], returned)
-        final = after + branch
+        final = dense_out + branch
         output_list.append(final.astype(low))
         stat_list.append(jnp.stack([jnp.sum(v * v) for v in (final, attn, ffn, branch)]))
 

time: 2400 us -> 1600 us (0.67)
  Pallas kernels: 855 us -> 102 us
  waiting for transfers between devices: 818 us -> 756 us
  blocking collectives: 59 us -> 90.3 us
    pallas_call x5, Pallas kernels: 776 us -> 22.7 us  [assemble(): pl.pallas_call(functools.partial(assemble_kernel, masks), out_shape=jax.S...]
    reduce_scatter x8, waiting for transfers between devices: 320 us -> 219 us  [scatter_slots(): return lax.psum_scatter(partial_sums, 'dp', scatter_dimension=0, tiled=True)]
    all_to_all x0 -> x1, blocking collectives: none -> 74.3 us  [swap_heads(): return lax.all_to_all(blocks, 'dp', split_axis=0, concat_axis=0, tiled=True)]
    ppermute x15 -> x18, waiting for transfers between devices: 13.8 us -> 65.1 us  [turn(): lax.ppermute(values, 'dp', [(i, (i + shift) % count) for i in range(count)])]
    all_gather x1 -> x0, blocking collectives: 44.1 us -> none  [gather_dp(): return lax.all_gather(shard, 'dp', axis=0)]
    all_gather x8, waiting for transfers between devices: 246 us -> 218 us  [gather_slots(): return lax.all_gather(rows, 'dp', axis=0, tiled=True)]
    all_to_all x8 -> x7, waiting for transfers between devices: 79.8 us -> 91.3 us  [swap_heads(): return lax.all_to_all(blocks, 'dp', split_axis=0, concat_axis=0, tiled=True)]
  transfers between devices with their start and end apart: 106 -> 108, of which waited for: 37 -> 48; matrix products, arithmetic and copies ran while one was open for 18% -> 27% of each run, Pallas kernels for 36% -> 6%
where the time goes in v3:
time: 1600 us; the launch traced here: 1590 us
  waiting for transfers between devices  756 us (47%)
  matrix products  278 us (17%)
  other arithmetic  145 us (9%)
  starting transfers between devices  137 us (9%)
  Pallas kernels  102 us (6%)
  blocking collectives  90.3 us (6%)
  local copies, waits for them, and re-layouts  66.5 us (4%)
  between operations  17.2 us (1%)
    reduce_scatter x8, waiting for transfers between devices, scatter_slots(): return lax.psum_scatter(partial_sums, 'dp', scatter_dimension=0, tiled=True)  219 us
    all_gather x8, waiting for transfers between devices, gather_slots(): return lax.all_gather(rows, 'dp', axis=0, tiled=True)  218 us
    ppermute x53, waiting for transfers between devices, swap(): return lax.ppermute(values, 'expert', [(i, i ^ bit) for i in range(count)])  141 us
    dot_general x16, matrix products, contract_cols(): lax.dot_general(left, right, (((1,), (1,)), ((), ())), preferred_element_...  99.3 us
    all_to_all x7, waiting for transfers between devices, swap_heads(): return lax.all_to_all(blocks, 'dp', split_axis=0, concat_axis=0, tiled=True)  91.3 us
    dot_general x16, matrix products, contract_rows(): lax.dot_general(left, right, (((0,), (0,)), ((), ())), preferred_element_...  89.2 us
    all_to_all x1, blocking collectives, swap_heads(): return lax.all_to_all(blocks, 'dp', split_axis=0, concat_axis=0, tiled=True)  74.3 us
    ppermute x18, waiting for transfers between devices, turn(): lax.ppermute(values, 'dp', [(i, (i + shift) % count) for i in range(count)])  65.1 us
  transfers between devices with their start and end apart: 108, of which 48 were waited for; matrix products, arithmetic and copies ran while one was open for 27% of the time, Pallas kernels for 6%

profile of v3, /device:TPU:0, one launch (start us, length us, event | category | flops | bytes accessed | tf_op | source)
XLA Modules:
  0.0 1591.6 jit_solution(16642258266426219569)
XLA Ops:
  85.9 21.4 %all-to-all-start = ((bf16[4,256,768]{2,1,0:T(8,128)(2,1)}), bf16[4,256,768]{2,1,0:T(8,128)(2,1)S(1)}, u32[]{:S(2)}, u32[]{:S(2)}) async-start(bf16[4,256,768]{2,1,0:T(8,128)(2,1)} %bitcast.424), calls=%async_computation | async-start | bytes 3145728 | tf_op jit(solution)/shard_map/all_to_all | solution.py:161
  112.3 27.3 %collective-permute-done.17 = bf16[32,1024]{1,0:T(8,128)(2,1)S(1)} collective-permute-done((bf16[32,1024]{1,0:T(8,128)(2,1)S(1)}, bf16[32,1024]{1,0:T(8,128)(2,1)S(1)}, u32[]{:S(2)}, u32[]{:S(2)}) %collective-permute-start.17) | collective-permute-done | bytes 65568 | tf_op jit(solution)/shard_map/ppermute | solution.py:55
  173.5 19.4 %collective-permute-done.22.refs_3_ = bf16[4,32,1024]{2,1,0:T(8,128)(2,1)} collective-permute-done((bf16[4,32,1024]{2,1,0:T(8,128)(2,1)}, bf16[4,32,1024]{2,1,0:T(8,128)(2,1)}, u32[]{:S(2)}, u32[]{:S(2)}) %collective-permute-start.22) | collective-permute-done | bytes 262176 | tf_op jit(solution)/shard_map/ppermute | solution.py:50
  197.2 14.5 collective-permute-done.27.refs_1_
  214.6 15.0 attend.2
  290.8 10.5 all-to-all-done.2
  307.2 74.3 %all_to_all.80 = bf16[4,256,768]{2,1,0:T(8,128)(2,1)} all-to-all(bf16[4,256,768]{2,1,0:T(8,128)(2,1)S(1)} %bitcast.425), channel_id=1, replica_groups=mesh['dp'=4,'expert'=8] {'dp'}, dimensions={0} | all-to-all | bytes 3145728 | tf_op jit(solution)/shard_map/all_to_all | solution.py:161
  381.5 15.0 attend.3
  402.7 12.6 all-to-all-done.6
  430.8 16.0 %all_to_all.81 = bf16[8,40,1024]{2,1,0:T(8,128)(2,1)} all-to-all(bf16[8,40,1024]{2,1,0:T(8,128)(2,1)S(1)} %bitcast.436), channel_id=1, replica_groups=mesh['dp'=4,'expert'=8] {'expert'}, dimensions={0} | all-to-all | bytes 1310720 | tf_op jit(solution)/shard_map/all_to_all | solution.py:167
  447.1 13.3 all-gather.17.cloned.1.call-done
  475.5 39.8 %all-gather.21.cloned.1.call-done = bf16[1280,1024]{1,0:T(8,128)(2,1)} async-done(((bf16[320,1024]{1,0:T(8,128)(2,1)}), bf16[1280,1024]{1,0:T(8,128)(2,1)}) %all-gather.21.cloned.1.call-update) | async-done | bytes 2621456 | tf_op jit(solution)/shard_map/all_gather | solution.py:284
  531.0 37.7 %reduce-scatter.14.cloned.1.call-done = bf16[320,1024]{1,0:T(8,128)(2,1)} async-done(((bf16[1280,1024]{1,0:T(8,128)(2,1)}), bf16[320,1024]{1,0:T(8,128)(2,1)}) %reduce-scatter.14.cloned.1.call-update) | async-done | bytes 655376 | tf_op jit(solution)/shard_map/reduce_scatter | solution.py:288
  569.6 53.8 %reduce-scatter.16.cloned.1.call-done = bf16[320,1024]{1,0:T(8,128)(2,1)} async-done(((bf16[1280,1024]{1,0:T(8,128)(2,1)}), bf16[320,1024]{1,0:T(8,128)(2,1)}) %reduce-scatter.16.cloned.1.call-update) | async-done | bytes 655376 | tf_op jit(solution)/shard_map/reduce_scatter | solution.py:288
  623.7 55.6 %all-gather.19.cloned.1.call-done = bf16[1280,1024]{1,0:T(8,128)(2,1)} async-done(((bf16[320,1024]{1,0:T(8,128)(2,1)}), bf16[1280,1024]{1,0:T(8,128)(2,1)}) %all-gather.19.cloned.1.call-update) | async-done | bytes 2621456 | tf_op jit(solution)/shard_map/all_gather | solution.py:284
  701.3 33.0 %all-gather.23.cloned.1.call-done = bf16[1280,1024]{1,0:T(8,128)(2,1)} async-done(((bf16[320,1024]{1,0:T(8,128)(2,1)}), bf16[1280,1024]{1,0:T(8,128)(2,1)}) %all-gather.23.cloned.1.call-update) | async-done | bytes 2621456 | tf_op jit(solution)/shard_map/all_gather | solution.py:284
  754.9 32.7 %reduce-scatter.20.cloned.1.call-done = bf16[320,1024]{1,0:T(8,128)(2,1)} async-done(((bf16[1280,1024]{1,0:T(8,128)(2,1)}), bf16[320,1024]{1,0:T(8,128)(2,1)}) %reduce-scatter.20.cloned.1.call-update) | async-done | bytes 655376 | tf_op jit(solution)/shard_map/reduce_scatter | solution.py:288
  787.7 53.9 %reduce-scatter.18.cloned.1.call-done = bf16[320,1024]{1,0:T(8,128)(2,1)} async-done(((bf16[1280,1024]{1,0:T(8,128)(2,1)}), bf16[320,1024]{1,0:T(8,128)(2,1)}) %reduce-scatter.18.cloned.1.call-update) | async-done | bytes 655376 | tf_op jit(solution)/shard_map/reduce_scatter | solution.py:288
  841.7 55.8 %all-gather.27.cloned.1.call-done = bf16[1280,1024]{1,0:T(8,128)(2,1)} async-done(((bf16[320,1024]{1,0:T(8,128)(2,1)}), bf16[1280,1024]{1,0:T(8,128)(2,1)}) %all-gather.27.cloned.1.call-update) | async-done | bytes 2621456 | tf_op jit(solution)/shard_map/all_gather | solution.py:284
  931.9 20.6 %all-gather.25.cloned.1.call-done = bf16[1280,1024]{1,0:T(8,128)(2,1)} async-done(((bf16[320,1024]{1,0:T(8,128)(2,1)}), bf16[1280,1024]{1,0:T(8,128)(2,1)}) %all-gather.25.cloned.1.call-update) | async-done | bytes 2621456 | tf_op jit(solution)/shard_map/all_gather | solution.py:284
  997.9 41.1 %reduce-scatter.22.cloned.1.call-done = bf16[320,1024]{1,0:T(8,128)(2,1)} async-done(((bf16[1280,1024]{1,0:T(8,128)(2,1)}), bf16[320,1024]{1,0:T(8,128)(2,1)}) %reduce-scatter.22.cloned.1.call-update) | async-done | bytes 655376 | tf_op jit(solution)/shard_map/reduce_scatter | solution.py:288
  1095.5 11.8 fusion.61
  1131.6 20.0 %all-to-all-done.9 = bf16[4,256,256]{2,1,0:T(8,128)(2,1)S(1)} async-done(((bf16[4,256,256]{2,1,0:T(8,128)(2,1)}), bf16[4,256,256]{2,1,0:T(8,128)(2,1)S(1)}, u32[]{:S(2)}, u32[]{:S(2)}) %all-to-all-start.9) | async-done | bytes 524320 | tf_op jit(solution)/shard_map/all_to_all | solution.py:161
  1152.5 24.9 %attend_back.2 = bf16[1024,768]{1,0:T(8,128)(2,1)} custom-call(s32[1]{0:T(128)} %bitcast.51.prefix_ref, bf16[1024,768]{1,0:T(8,128)(2,1)} %bitcast.401, bf16[1024,256]{1,0:T(8,128)(2,1)} %bitcast.451), custom_call_target="tpu_custom_call" | custom-call | tf_op jit(solution)/shard_map/attend_back/pallas_call | solution.py:261
  1204.1 36.6 %all-to-all-done.10 = bf16[4,256,768]{1,2,0:T(8,128)(2,1)} async-done(((bf16[4,256,768]{1,2,0:T(8,128)(2,1)}), bf16[4,256,768]{1,2,0:T(8,128)(2,1)}, u32[]{:S(2)}, u32[]{:S(2)}) %all-to-all-start.10) | async-done | bytes 1572896 | tf_op jit(solution)/shard_map/all_to_all | solution.py:161
  1267.8 11.8 fusion.54
  1296.1 10.5 convolution_convert_fusion.1
  1312.3 24.7 %attend_back.3 = bf16[1024,768]{1,0:T(8,128)(2,1)} custom-call(s32[1]{0:T(128)} %bitcast.1.prefix_ref, bf16[1024,768]{1,0:T(8,128)(2,1)} %bitcast.399, bf16[1024,256]{1,0:T(8,128)(2,1)} %bitcast.450), custom_call_target="tpu_custom_call" | custom-call | tf_op jit(solution)/shard_map/attend_back/pallas_call | solution.py:261
  1370.8 11.6 all-to-all-done.15
  1419.3 12.7 collective-permute-done.48
  1434.3 33.7 %collective-permute-done.51 = bf16[4,2,32,1536]{3,2,1,0:T(8,128)(2,1)S(1)} collective-permute-done((bf16[4,2,32,1536]{3,2,1,0:T(8,128)(2,1)S(1)}, bf16[4,2,32,1536]{3,2,1,0:T(8,128)(2,1)S(1)}, u32[]{:S(2)}, u32[]{:S(2)}) %collective-permute-start.51) | collective-permute-done | bytes 786464 | tf_op jit(solution)/shard_map/ppermute | solution.py:50
  1490.2 17.8 %collective-permute-done.58 = bf16[4,32,4096]{2,1,0:T(8,128)(2,1)} collective-permute-done((bf16[4,32,4096]{2,1,0:T(8,128)(2,1)}, bf16[4,32,4096]{2,1,0:T(8,128)(2,1)}, u32[]{:S(2)}, u32[]{:S(2)}) %collective-permute-start.58) | collective-permute-done | bytes 1048608 | tf_op jit(solution)/shard_map/ppermute | solution.py:50
  (798 shorter events, 695.1 us)
Async XLA Ops:
  7.2 151.6 %all-gather.31.cloned.1.call-start = ((), (), s32[]{:S(2)}) async-start(), calls=%async_computation.51 | async-start | bytes 1310720 | tf_op jit(solution)/shard_map/all_gather | solution.py:126
  7.9 154.5 %all-gather.29.cloned.1.call-start = ((), (), s32[]{:S(2)}) async-start(), calls=%async_computation.50 | async-start | bytes 1310720 | tf_op jit(solution)/shard_map/all_gather | solution.py:126
  85.9 83.8 %all-to-all-start = ((bf16[4,256,768]{2,1,0:T(8,128)(2,1)}), bf16[4,256,768]{2,1,0:T(8,128)(2,1)S(1)}, u32[]{:S(2)}, u32[]{:S(2)}) async-start(bf16[4,256,768]{2,1,0:T(8,128)(2,1)} %bitcast.424), calls=%async_computation | async-start | bytes 3145728 | tf_op jit(solution)/shard_map/all_to_all | solution.py:161
  169.7 61.8 %all-to-all-start.3 = ((bf16[8,40,1024]{2,1,0:T(8,128)(2,1)}), bf16[8,40,1024]{2,1,0:T(8,128)(2,1)S(1)}, u32[]{:S(2)}, u32[]{:S(2)}) async-start(bf16[8,40,1024]{2,1,0:T(8,128)(2,1)} %bitcast.433), calls=%async_computation.3 | async-start | bytes 1310720 | tf_op jit(solution)/shard_map/all_to_all | solution.py:167
  194.7 56.8 %collective-permute-start.28 = (bf16[4,32,4096]{2,1,0:T(8,128)(2,1)}, bf16[4,32,4096]{2,1,0:T(8,128)(2,1)}, u32[]{:S(2)}, u32[]{:S(2)}) collective-permute-start(bf16[4,32,4096]{2,1,0:T(8,128)(2,1)} %bitcast.24.refs_0_), channel_id=1, source_target_pairs={{0,2},{1,3},{2,0},{3,1},{4,6},{5,7},{6,4},{7,5},{8,10},{9,11},{10,... | collective-permute-start | bytes 3145736 | tf_op jit(solution)/shard_map/ppermute | solution.py:50
  235.0 167.1 %all-gather.13.cloned.1.call-start = ((), (), s32[]{:S(2)}) async-start(), calls=%async_computation.29 | async-start | bytes 3276800 | tf_op jit(solution)/shard_map/all_gather | solution.py:284
  290.2 112.0 %all-gather.15.cloned.1.call-start = ((), (), s32[]{:S(2)}) async-start(), calls=%async_computation.30 | async-start | bytes 3276800 | tf_op jit(solution)/shard_map/all_gather | solution.py:284
  402.1 58.3 %all-gather.17.cloned.1.call-start = ((), (), s32[]{:S(2)}) async-start(), calls=%async_computation.31 | async-start | bytes 3276800 | tf_op jit(solution)/shard_map/all_gather | solution.py:284
  402.7 112.6 %all-gather.21.cloned.1.call-start = ((), (), s32[]{:S(2)}) async-start(), calls=%async_computation.34 | async-start | bytes 3276800 | tf_op jit(solution)/shard_map/all_gather | solution.py:284
  446.8 121.9 %reduce-scatter.14.cloned.1.call-start = ((), (), s32[]{:S(2)}) async-start(), calls=%async_computation.32 | async-start | bytes 3276800 | tf_op jit(solution)/shard_map/reduce_scatter | solution.py:288
  475.5 147.9 %reduce-scatter.16.cloned.1.call-start = ((), (), s32[]{:S(2)}) async-start(), calls=%async_computation.35 | async-start | bytes 3276800 | tf_op jit(solution)/shard_map/reduce_scatter | solution.py:288
  531.0 148.3 %all-gather.19.cloned.1.call-start = ((), (), s32[]{:S(2)}) async-start(), calls=%async_computation.33 | async-start | bytes 3276800 | tf_op jit(solution)/shard_map/all_gather | solution.py:284
  568.7 165.6 %all-gather.23.cloned.1.call-start = ((), (), s32[]{:S(2)}) async-start(), calls=%async_computation.36 | async-start | bytes 3276800 | tf_op jit(solution)/shard_map/all_gather | solution.py:284
  623.4 164.2 %reduce-scatter.20.cloned.1.call-start = ((), (), s32[]{:S(2)}) async-start(), calls=%async_computation.39 | async-start | bytes 3276800 | tf_op jit(solution)/shard_map/reduce_scatter | solution.py:288
  698.2 143.4 %reduce-scatter.18.cloned.1.call-start = ((), (), s32[]{:S(2)}) async-start(), calls=%async_computation.37 | async-start | bytes 3276800 | tf_op jit(solution)/shard_map/reduce_scatter | solution.py:288
  754.8 142.7 %all-gather.27.cloned.1.call-start = ((), (), s32[]{:S(2)}) async-start(), calls=%async_computation.40 | async-start | bytes 3276800 | tf_op jit(solution)/shard_map/all_gather | solution.py:284
  787.6 164.8 %all-gather.25.cloned.1.call-start = ((), (), s32[]{:S(2)}) async-start(), calls=%async_computation.38 | async-start | bytes 3276800 | tf_op jit(solution)/shard_map/all_gather | solution.py:284
  841.6 197.4 %reduce-scatter.22.cloned.1.call-start = ((), (), s32[]{:S(2)}) async-start(), calls=%async_computation.41 | async-start | bytes 3276800 | tf_op jit(solution)/shard_map/reduce_scatter | solution.py:288
  987.8 252.9 %reduce-scatter.24.cloned.1.call-start = ((), (), s32[]{:S(2)}) async-start(), calls=%async_computation.42 | async-start | bytes 3276800 | tf_op jit(solution)/shard_map/reduce_scatter | solution.py:288
  1080.6 163.3 %reduce-scatter.28.cloned.1.call-start = ((), (), s32[]{:S(2)}) async-start(), calls=%async_computation.44 | async-start | bytes 3276800 | tf_op jit(solution)/shard_map/reduce_scatter | solution.py:288
  1090.6 153.1 %collective-permute-start.46 = (f32[1280]{0:T(1024)S(1)}, f32[1280]{0:T(1024)S(1)}, u32[]{:S(2)}, u32[]{:S(2)}) collective-permute-start(f32[1280]{0:T(1024)S(1)} %get-tuple-element.113), channel_id=1, source_target_pairs={{0,24},{8,0},{16,8},{24,16},{1,25},{9,1},{17,9},{25,17},{2,26},{10... | collective-permute-start | bytes 15368 | tf_op jit(solution)/shard_map/ppermute | solution.py:55
  1092.4 151.3 %collective-permute-start.45 = (f32[1280]{0:T(1024)S(1)}, f32[1280]{0:T(1024)S(1)}, u32[]{:S(2)}, u32[]{:S(2)}) collective-permute-start(f32[1280]{0:T(1024)S(1)} %get-tuple-element.113), channel_id=1, source_target_pairs={{0,16},{8,24},{16,0},{24,8},{1,17},{9,25},{17,1},{25,9},{2,18},{10... | collective-permute-start | bytes 15368 | tf_op jit(solution)/shard_map/ppermute | solution.py:55
  1092.4 151.3 %collective-permute-start.44 = (f32[1280]{0:T(1024)S(1)}, f32[1280]{0:T(1024)S(1)}, u32[]{:S(2)}, u32[]{:S(2)}) collective-permute-start(f32[1280]{0:T(1024)S(1)} %get-tuple-element.113), channel_id=1, source_target_pairs={{0,8},{8,16},{16,24},{24,0},{1,9},{9,17},{17,25},{25,1},{2,10},{10... | collective-permute-start | bytes 15368 | tf_op jit(solution)/shard_map/ppermute | solution.py:55
  1180.0 60.7 %all-to-all-start.10 = ((bf16[4,256,768]{1,2,0:T(8,128)(2,1)}), bf16[4,256,768]{1,2,0:T(8,128)(2,1)}, u32[]{:S(2)}, u32[]{:S(2)}) async-start(bf16[4,256,768]{1,2,0:T(8,128)(2,1)} %copy.64), calls=%async_computation.16 | async-start | bytes 3145728 | tf_op jit(solution)/shard_map/all_to_all | solution.py:161
  1184.4 300.6 %reduce-scatter.26.cloned.1.call-start = ((), (), s32[]{:S(2)}) async-start(), calls=%async_computation.43 | async-start | bytes 3276800 | tf_op jit(solution)/shard_map/reduce_scatter | solution.py:288
  1343.9 214.0 %reduce-scatter.34.cloned.1.call-start = ((), (), s32[]{:S(2)}) async-start(), calls=%async_computation.47 | async-start | bytes 327680 | tf_op jit(solution)/shard_map/reduce_scatter | solution.py:155
  1370.8 206.2 %reduce-scatter.30.cloned.1.call-start = ((), (), s32[]{:S(2)}) async-start(), calls=%async_computation.45 | async-start | bytes 491520 | tf_op jit(solution)/shard_map/reduce_scatter | solution.py:155
  1402.6 65.8 %collective-permute-start.57 = (bf16[4,2,32,4096]{3,2,1,0:T(8,128)(2,1)S(1)}, bf16[4,2,32,4096]{3,2,1,0:T(8,128)(2,1)S(1)}, u32[]{:S(2)}, u32[]{:S(2)}) collective-permute-start(bf16[4,2,32,4096]{3,2,1,0:T(8,128)(2,1)S(1)} %dynamic-slice_bitcast_fusion.3), channel_id=1, source_target_pairs={{0,4},{1,5},{2,6},{3,7},{4,0},{5,1},{6,2},{7,3},{8,12},{9,13},{10,... | collective-permute-start | bytes 6291464 | tf_op jit(solution)/shard_map/ppermute | solution.py:50
  1417.3 104.7 %collective-permute-start.60 = (bf16[4,2,128,1024]{3,2,1,0:T(8,128)(2,1)}, bf16[4,2,128,1024]{3,2,1,0:T(8,128)(2,1)}, u32[]{:S(2)}, u32[]{:S(2)}) collective-permute-start(bf16[4,2,128,1024]{3,2,1,0:T(8,128)(2,1)} %dynamic-slice_bitcast_fusion.2), channel_id=1, source_target_pairs={{0,2},{1,3},{2,0},{3,1},{4,6},{5,7},{6,4},{7,5},{8,10},{9,11},{10,... | collective-permute-start | bytes 6291464 | tf_op jit(solution)/shard_map/ppermute | solution.py:50
  1489.2 87.7 %reduce-scatter.32.cloned.1.call-start = ((), (), s32[]{:S(2)}) async-start(), calls=%async_computation.46 | async-start | bytes 491520 | tf_op jit(solution)/shard_map/reduce_scatter | solution.py:155
  1490.1 89.1 %reduce-scatter.36.cloned.1.call-start = ((), (), s32[]{:S(2)}) async-start(), calls=%async_computation.48 | async-start | bytes 1310720 | tf_op jit(solution)/shard_map/reduce_scatter | solution.py:155
  1519.4 63.7 %reduce-scatter.38.cloned.1.call-start = ((), (), s32[]{:S(2)}) async-start(), calls=%async_computation.49 | async-start | bytes 1310720 | tf_op jit(solution)/shard_map/reduce_scatter | solution.py:155
  (231 other events, 4196.0 us)
Sparse Core Ops, SparseCore 0:
  9.6 39.7 all-gather.30
  51.0 29.5 all-gather.28
  238.0 55.2 all-gather.12
  295.3 86.8 all-gather.14
  404.2 56.1 all-gather.16
  461.8 53.5 all-gather.20
  517.6 51.0 reduce-scatter.13
  571.5 51.7 reduce-scatter.15
  625.0 54.2 all-gather.18
  680.7 53.5 all-gather.22
  736.6 51.0 reduce-scatter.19
  789.8 51.7 reduce-scatter.17
  843.2 54.2 all-gather.26
  898.9 53.5 all-gather.24
  987.9 51.0 reduce-scatter.21
  1041.1 52.2 reduce-scatter.23
  1095.6 60.1 reduce-scatter.27
  1204.2 59.9 reduce-scatter.25
  1370.9 20.1 reduce-scatter.33
  1476.5 17.9 reduce-scatter.29
  1497.4 18.9 reduce-scatter.31
  1518.7 25.8 reduce-scatter.35
  1556.7 26.3 reduce-scatter.37

commit v4 on v3

--- a/solution.py
+++ b/solution.py
@@ -136,14 +136,18 @@
     return full
 
 
-def scatter_rows(total, order):
+def scatter_start(total, order):
     count = lax.axis_size("expert")
     dp_count = lax.axis_size("dp")
-    own = lax.axis_index("expert")
     rows = total.shape[0] // (count * dp_count)
     bits = sorted(order)
     current = total.reshape((dp_count,) + (2,) * len(bits) + (rows, total.shape[1]))
     left = sorted(bits, reverse=True)
+    return scatter_bits(current, order[:1], left), order[1:], left
+
+
+def scatter_bits(current, order, left):
+    own = lax.axis_index("expert")
     for bit in order:
         axis = 1 + left.index(bit)
         mine = (own // bit) % 2
@@ -152,9 +156,19 @@
         received = swap(send, bit)
         current = (keep.astype(jnp.float32) + received.astype(jnp.float32)).astype(jnp.bfloat16)
         left.remove(bit)
+    return current
+
+
+def scatter_end(started):
+    current, order, left = started
+    current = scatter_bits(current, order, left)
     return lax.psum_scatter(
-        current.reshape(dp_count * rows, -1), "dp", scatter_dimension=0, tiled=True
+        current.reshape(-1, current.shape[-1]), "dp", scatter_dimension=0, tiled=True
     ).astype(jnp.float32)
+
+
+def scatter_rows(total, order):
+    return scatter_end(scatter_start(total, order))
 
 
 def swap_heads(blocks):
@@ -198,6 +212,14 @@
     out_ref[...] = jnp.concatenate(parts, 0).T.astype(out_ref.dtype)
 
 
+def attend_cost(length, cols, products):
+    return pl.CostEstimate(
+        flops=products * length * length * cols // 3,
+        transcendentals=length * length * cols // (3 * HEAD_DIM),
+        bytes_accessed=products * length * cols,
+    )
+
+
 def attend(whole, prefix, block):
     length, cols = whole.shape
     width = cols // 3
@@ -210,6 +232,7 @@
             pl.BlockSpec((length, cols), lambda i: (0, 0)),
         ],
         out_specs=pl.BlockSpec((block, width), lambda i: (i, 0)),
+        cost_estimate=attend_cost(length, cols, 4),
         name="attend",
     )(prefix, whole)
 
@@ -272,6 +295,7 @@
             pltpu.VMEM((heads, length, HEAD_DIM), jnp.float32),
             pltpu.VMEM((heads, length, HEAD_DIM), jnp.float32),
         ],
+        cost_estimate=attend_cost(length, cols, 10),
         name="attend_back",
     )(prefix, whole, grads)
 
@@ -280,22 +304,40 @@
     return lax.optimization_barrier((value,) + others)[0]
 
 
-def gather_slots(rows):
-    return lax.all_gather(rows, "dp", axis=0, tiled=True)
-
-
-def scatter_slots(partial_sums):
-    return lax.psum_scatter(partial_sums, "dp", scatter_dimension=0, tiled=True)
-
-
-def sum_slots(partial_sums):
-    return gather_slots(scatter_slots(partial_sums))
-
-
-def own_slots(values):
+def flip(values, bit):
     count = lax.axis_size("dp")
-    size = values.shape[0] // count
-    return lax.dynamic_slice_in_dim(values, lax.axis_index("dp") * size, size, 0)
+    return lax.ppermute(values, "dp", [(i, i ^ bit) for i in range(count)])
+
+
+def near_groups():
+    count = lax.axis_size("dp")
+    return [[i, i ^ 1] for i in range(count) if not i & 1]
+
+
+def gather_near(shard):
+    return lax.all_gather(shard, "dp", axis=0, axis_index_groups=near_groups())
+
+
+def scatter_near(parts):
+    return lax.psum_scatter(parts, "dp", scatter_dimension=0, axis_index_groups=near_groups())
+
+
+def both_rows(own):
+    return jnp.concatenate([own, flip(own, 2)], 0)
+
+
+def sum_pair(partial_sums):
+    size = partial_sums.shape[0] // 2
+    received = flip(partial_sums, 2)
+    return partial_sums.astype(jnp.float32) + jnp.concatenate(
+        [received[size:], received[:size]], 0
+    ).astype(jnp.float32)
+
+
+def sum_own(partial_sums):
+    size = partial_sums.shape[0] // 2
+    received = flip(partial_sums[size:], 2)
+    return partial_sums[:size].astype(jnp.float32) + received.astype(jnp.float32)
 
 
 def shards(
@@ -327,7 +369,7 @@
     up_ex, down_ex, centroid = (expert_up[0], expert_down[0], centroids[0])
     gain_ex = expert_gain[0].astype(f32)
 
-    places, grad_slots, grad_rows = ([], [], [])
+    places, grad_rows = ([], [])
     for micro in micros:
         route = routes[micro, 0, :, 0]
         onehot = (route[:, None] == expert_ids[None, :]).astype(jnp.int32)
@@ -338,7 +380,7 @@
         grad_sent = jnp.dot(
             place, cotangent[micro, 0].astype(low), preferred_element_type=f32
         ).astype(low)
-        grad_slots.append(swap_experts(grad_sent))
+        grad_rows.append(both_rows(swap_experts(grad_sent)))
 
     order_a, order_b = bit_orders()
     rows_qkv = qkv_weight.shape[0]
@@ -361,8 +403,12 @@
     full_mix = assemble(spread(turn_gather(mix_weight), order_a))
     full_up = assemble(spread(gather_dp(up_weight), order_a))
     full_down = assemble(spread(gather_dp(down_weight), order_b))
-    for micro in micros:
-        grad_rows.append(gather_slots(grad_slots[micro]))
+
+    up_both, down_both = ([], [])
+    for layer in range(2):
+        up_near = gather_near(after(up_ex[layer], first))
+        up_both.append(jnp.concatenate([up_near[0], up_near[1]], 1))
+        down_both.append(gather_near(after(down_ex[layer], first)).reshape(-1, width))
 
     dense = []
     slots_in = []
@@ -388,86 +434,97 @@
         dense.append((inputs, normed, whole, mixed, attn, resid, ffn, normed2, pre, hidden, dense_out))
         slots_in.append(swap_experts(sent))
 
-    own_in, *grad_rows = lax.optimization_barrier((slots_in[0], *grad_rows))
-    slots_in[0] = own_in
-    up_sum = [None, None]
-    down_sum = [None, None]
+    slot_count = experts * capacity
     gain_one = jnp.zeros((width,), f32)
-
     first_stage = []
     for micro in micros:
-        rows = gather_slots(slots_in[micro])
+        rows = both_rows(slots_in[micro])
         if micro > 0:
             rows = after(rows, first_stage[micro - 1][-1])
         sig = jax.nn.sigmoid(jnp.dot(rows, centroid, preferred_element_type=f32))[:, None]
         state0 = rows.astype(f32)
         z0 = layer_norm(state0, gain_ex[0]).astype(low)
-        pre0 = jnp.dot(z0, up_ex[0], preferred_element_type=f32)
+        pre0 = jnp.dot(z0, up_both[0], preferred_element_type=f32)
         h0 = gelu(pre0).astype(low)
-        out0 = jnp.dot(h0, down_ex[0], preferred_element_type=f32).astype(low)
+        out0 = jnp.dot(h0, down_both[0], preferred_element_type=f32).astype(low)
         first_stage.append((rows, sig, z0, pre0, h0, out0))
-    summed0 = [sum_slots(first_stage[micro][-1]) for micro in micros]
     second_stage = []
     for micro in micros:
         rows, sig = first_stage[micro][:2]
-        total = summed0[micro]
+        total = sum_pair(first_stage[micro][-1])
         if micro > 0:
             total = after(total, second_stage[micro - 1][-1])
-        state1 = rows.astype(f32) + total.astype(f32)
+        state1 = rows.astype(f32) + total
         z1 = layer_norm(state1, gain_ex[1]).astype(low)
-        pre1 = jnp.dot(z1, up_ex[1], preferred_element_type=f32)
+        pre1 = jnp.dot(z1, up_both[1], preferred_element_type=f32)
         h1 = gelu(pre1).astype(low)
-        out1 = jnp.dot(h1, down_ex[1], preferred_element_type=f32).astype(low)
+        out1 = jnp.dot(h1, down_both[1], preferred_element_type=f32).astype(low)
         incoming = grad_rows[micro].astype(f32)
-        score_part = jnp.sum(incoming * out1.astype(f32), 1)
         grad2 = incoming * sig
         grad_y = grad2.astype(low)
-        pre_grad = gelu_back(pre1, contract_cols(grad_y, down_ex[1])).astype(low)
-        normed_part = contract_cols(pre_grad, up_ex[1]).astype(low)
-        second_stage.append(
-            (state1, out1, incoming, score_part, grad2, z1, h1, grad_y, pre_grad, normed_part)
-        )
-    summed1 = [sum_slots(second_stage[micro][-1]) for micro in micros]
+        pre_grad = gelu_back(pre1, contract_cols(grad_y, down_both[1])).astype(low)
+        normed_part = contract_cols(pre_grad, up_both[1]).astype(low)
+        second_stage.append((state1, out1, incoming, grad2, z1, h1, grad_y, pre_grad, normed_part))
+    hidden_dev = up_ex.shape[2]
+    hidden_halves = (slice(0, hidden_dev), slice(hidden_dev, 2 * hidden_dev))
+
+    def grad_halves(lefts, rights, split_left):
+        left, right = (jnp.concatenate(parts, 0) for parts in (lefts, rights))
+        return jnp.stack(
+            [
+                contract_rows(left[:, half] if split_left else left, right if split_left else right[:, half])
+                for half in hidden_halves
+            ]
+        ).astype(low)
+
+    up_grads, down_grads = ([None, None], [None, None])
+    by_stage = list(zip(*second_stage))
+    down_grads[1] = grad_halves(by_stage[5], by_stage[6], True)
+    up_grads[1] = grad_halves(by_stage[4], by_stage[7], False)
     third_stage = []
     for micro in micros:
         rows, sig, z0, pre0, h0, _ = first_stage[micro]
-        state1, _, _, _, grad2, z1, h1, grad_y1, pre_grad1, _ = second_stage[micro]
-        total = summed1[micro]
+        state1, out1, incoming, grad2 = second_stage[micro][:4]
+        total = sum_pair(second_stage[micro][-1])
         if micro > 0:
-            total = after(total, third_stage[micro - 1][-1])
-        state_grad, gain_grad = norm_back(state1, gain_ex[1], total.astype(f32))
+            total = after(total, third_stage[micro - 1][-1], up_grads[1], down_grads[1])
+        state_grad, gain_grad = norm_back(state1, gain_ex[1], total)
         gain_one = gain_one + gain_grad
         grad1 = grad2 + state_grad
         grad_y = grad1.astype(low)
-        pre_grad = gelu_back(pre0, contract_cols(grad_y, down_ex[0])).astype(low)
-        normed_part = contract_cols(pre_grad, up_ex[0]).astype(low)
-        down_part, up_part = (contract_rows(h1, grad_y1), contract_rows(z1, pre_grad1))
-        down_sum[1] = down_part if micro == 0 else down_sum[1] + down_part
-        up_sum[1] = up_part if micro == 0 else up_sum[1] + up_part
-        down_part, up_part = (contract_rows(h0, grad_y), contract_rows(z0, pre_grad))
-        down_sum[0] = down_part if micro == 0 else down_sum[0] + down_part
-        up_sum[0] = up_part if micro == 0 else up_sum[0] + up_part
-        third_stage.append((grad1, normed_part))
+        pre_grad = gelu_back(pre0, contract_cols(grad_y, down_both[0])).astype(low)
+        normed_part = contract_cols(pre_grad, up_both[0]).astype(low)
+        third_stage.append((grad1, grad_y, pre_grad, normed_part))
+    by_first, by_third = (list(zip(*first_stage)), list(zip(*third_stage)))
+    down_grads[0] = grad_halves(by_first[4], by_third[1], True)
+    up_grads[0] = grad_halves(by_first[2], by_third[2], False)
+    down_sum, up_sum = ([None, None], [None, None])
+    for layer in (1, 0):
+        down_sum[layer] = scatter_near(down_grads[layer]).astype(f32)
+        up_sum[layer] = scatter_near(up_grads[layer]).astype(f32)
     own_grads = []
+    branches = []
     for micro in micros:
         rows, sig = first_stage[micro][:2]
-        state1, _, incoming, score_part = second_stage[micro][:4]
-        grad1, normed_part = third_stage[micro]
-        normed_grad = scatter_slots(normed_part).astype(f32)
-        own_rows = own_slots(rows).astype(f32)
+        state1, out1, incoming = second_stage[micro][:3]
+        grad1, normed_part = (third_stage[micro][i] for i in (0, 3))
+        normed_grad = sum_own(normed_part)
+        own_rows = rows[:slot_count].astype(f32)
         state_grad, gain_grad = norm_back(own_rows, gain_ex[0], normed_grad)
-        own_sig = own_slots(sig)[:, 0]
-        score_grad = own_slots(sum_small(score_part)) + jnp.sum(
-            own_slots(incoming) * own_slots(state1), 1
-        )
+        own_sig = sig[:slot_count]
+        state2 = state1[:slot_count] + sum_own(out1)
+        branches.append((own_sig * state2).astype(low))
+        score_grad = jnp.sum(incoming[:slot_count] * state2, 1, keepdims=True)
         score_grad = score_grad * own_sig * (1.0 - own_sig)
-        row_grad = own_slots(grad1) + state_grad + score_grad[:, None] * centroid.astype(f32)
-        cent_grad = jnp.sum(score_grad[:, None] * own_rows, 0)
-        own_grads.append((row_grad.astype(low), gain_grad, cent_grad, normed_grad))
+        row_grad = grad1[:slot_count] + state_grad + score_grad * centroid.astype(f32)
+        cent_grad = jnp.sum(score_grad * own_rows, 0)
+        own_grads.append((row_grad.astype(low), gain_grad, cent_grad))
 
     gain_acc = jnp.zeros((2, width), f32)
     input_grads = []
     kept = []
+    kept_dense = []
+    order_c, order_d = (order_a[::-1], order_b[::-1])
     for micro in micros:
         inputs, normed, whole, mixed, attn, resid, ffn, normed2, pre, hidden, _ = dense[micro]
         grad_back = swap_experts(own_grads[micro][0])
@@ -482,18 +539,27 @@
         mixed_grad = contract_cols(attn_low, full_mix).astype(low)
         mixed_grad = mixed_grad.reshape(rows_dev, dp_count, mine).transpose(1, 0, 2)
         mixed_grad = swap_heads(mixed_grad).reshape(length, mine)
+        kept_dense.append((normed2, pre_grad, hidden, ffn_low))
+        if micro == 0:
+            mixed_grad = after(mixed_grad, up_grads[0], down_grads[0], down_sum[1])
+        if micro == micro_count - 1:
+            joined = [jnp.concatenate(parts, 0) for parts in zip(*kept_dense)]
+            down_start = scatter_start(contract_rows(joined[2], joined[3]).astype(low), order_c)
+            up_low = contract_rows(joined[0], joined[1]).astype(low)
+            mixed_grad = after(mixed_grad, down_start[0], up_low, up_sum[1])
         whole_grad = attend_back(whole, mixed_grad, prefix[micro], block)
         qkv_grad = swap_heads(whole_grad.reshape(dp_count, rows_dev, 3 * mine))
         qkv_grad = qkv_grad.transpose(1, 0, 2).reshape(rows_dev, 3 * width)
+        if micro == micro_count - 1:
+            qkv_grad = after(qkv_grad, down_sum[0])
         normed_grad = contract_cols(qkv_grad, full_qkv)
         input_part, gain1_grad = norm_back(inputs, gains[0], normed_grad)
         input_grads.append(resid_grad + input_part)
         gain_acc = gain_acc + jnp.stack([gain1_grad, gain2_grad])
-        kept.append((normed, qkv_grad, mixed, attn_low, normed2, pre_grad, hidden, ffn_low))
+        kept.append((normed, qkv_grad, mixed, attn_low))
     joined = [jnp.concatenate(parts, 0) for parts in zip(*kept)]
-    order_c, order_d = (order_a[::-1], order_b[::-1])
-    down_out = scatter_rows(contract_rows(joined[6], joined[7]).astype(low), order_c)
-    up_out = scatter_rows(contract_rows(joined[4], joined[5]).astype(low), order_d)
+    down_out = scatter_end(down_start)
+    up_out = scatter_rows(up_low, order_d)
     mix_out = scatter_rows(contract_rows(joined[2], joined[3]).astype(low), order_d)
     qkv_low = contract_rows(joined[0], joined[1]).astype(low)
     qkv_out = jnp.concatenate(
@@ -508,12 +574,8 @@
     output_list = []
     stat_list = []
     for micro in micros:
-        sig = first_stage[micro][1]
-        state1, out1 = second_stage[micro][:2]
         attn, ffn, dense_out = (dense[micro][i] for i in (4, 6, 10))
-        late = scatter_slots(after(out1, own_grads[-1][3]))
-        state2 = own_slots(state1) + after(late, kept[-1][1]).astype(f32)
-        returned = swap_experts((own_slots(sig) * state2).astype(low))
+        returned = swap_experts(branches[micro])
         branch = contract_rows(places[micro], returned)
         final = dense_out + branch
         output_list.append(final.astype(low))
@@ -524,12 +586,13 @@
             jnp.stack(stat_list, 1).reshape(-1),
             sum(part[1] for part in own_grads),
             sum(part[2] for part in own_grads),
+            0.5 * gain_one,
         ]
     )
     small = sum_small(small)
     stats = 4 * micro_count
     branch_rms = jnp.sqrt(small[:stats] / (length * width)).reshape(4, micro_count, 1)
-    ex_gain = jnp.stack([small[stats : stats + width], gain_one])
+    ex_gain = jnp.stack([small[stats : stats + width], small[stats + 2 * width :]])
     gain_sum = sum_small(gain_acc)
     for bit in order_a:
         gain_sum = gain_sum + swap(gain_sum, bit)
@@ -548,7 +611,7 @@
         jnp.stack(up_sum)[None],
         jnp.stack(down_sum)[None],
         ex_gain[None],
-        small[None, stats + width :],
+        small[None, stats + width : stats + 2 * width],
         branch_rms,
     )
 

time: 1600 us -> 1470 us (0.919)
  waiting for transfers between devices: 756 us -> 691 us
  blocking collectives: 90.3 us -> 27.2 us
  matrix products: 278 us -> 238 us
  local copies, waits for them, and re-layouts: 66.5 us -> 103 us
    ppermute x0 -> x12, waiting for transfers between devices: none -> 349 us  [flip(): return lax.ppermute(values, 'dp', [(i, i ^ bit) for i in range(count)])]
    all_gather x8 -> x4, waiting for transfers between devices: 218 us -> 0.04 us  [gather_near(): return lax.all_gather(shard, 'dp', axis=0, axis_index_groups=near_groups())]
    reduce_scatter x13 -> x9, waiting for transfers between devices: 221 us -> 27.1 us  [the longest x5 27.1 us: scatter_end(): lax.psum_scatter(current.reshape(-1, current.shape[-1]), 'dp', scatter_di...]
    all_to_all x1 -> x0, blocking collectives: 74.3 us -> none  [swap_heads(): return lax.all_to_all(blocks, 'dp', split_axis=0, concat_axis=0, tiled=True)]
    all_to_all x7 -> x6, waiting for transfers between devices: 17.2 us -> 77.6 us  [swap_experts(): lax.all_to_all(blocks, 'expert', split_axis=0, concat_axis=0, tiled=True)]
    all_to_all x7 -> x8, waiting for transfers between devices: 91.3 us -> 38.1 us  [swap_heads(): return lax.all_to_all(blocks, 'dp', split_axis=0, concat_axis=0, tiled=True)]
    dot_general x16, matrix products: 89.2 us -> 63.5 us  [contract_rows(): lax.dot_general(left, right, (((0,), (0,)), ((), ())), preferred_element_...]
    slice x1 -> x14, local copies, waits for them, and re-layouts: 0.67 us -> 17 us  [the longest x2 9.38 us: shards(): up_both.append(jnp.concatenate([up_near[0], up_near[1]], 1))]
  transfers between devices with their start and end apart: 108 -> 106, of which waited for: 48 -> 38; matrix products, arithmetic and copies ran while one was open for 27% -> 24% of each run, Pallas kernels for 6% -> 7%
where the time goes in v4:
time: 1470 us; the launch traced here: 1460 us
  waiting for transfers between devices  691 us (47%)
  matrix products  238 us (16%)
  starting transfers between devices  141 us (10%)
  other arithmetic  137 us (9%)
  local copies, waits for them, and re-layouts  103 us (7%)
  Pallas kernels  103 us (7%)
  blocking collectives  27.2 us (2%)
  between operations  17.4 us (1%)
    ppermute x12, waiting for transfers between devices, flip(): return lax.ppermute(values, 'dp', [(i, i ^ bit) for i in range(count)])  349 us
    ppermute x53, waiting for transfers between devices, swap(): return lax.ppermute(values, 'expert', [(i, i ^ bit) for i in range(count)])  138 us
    dot_general x16, matrix products, contract_cols(): lax.dot_general(left, right, (((1,), (1,)), ((), ())), preferred_element_...  89.9 us
    all_to_all x6, waiting for transfers between devices, swap_experts(): lax.all_to_all(blocks, 'expert', split_axis=0, concat_axis=0, tiled=True)  77.6 us
    dot_general x16, matrix products, contract_rows(): lax.dot_general(left, right, (((0,), (0,)), ((), ())), preferred_element_...  63.5 us
    ppermute x12, waiting for transfers between devices, turn(): lax.ppermute(values, 'dp', [(i, (i + shift) % count) for i in range(count)])  58.9 us
    pallas_call x2, Pallas kernels, attend_back(): pl.pallas_call(attend_back_kernel, out_shape=jax.ShapeDtypeStruct((length...  49.4 us
    all_to_all x8, starting transfers between devices, swap_heads(): return lax.all_to_all(blocks, 'dp', split_axis=0, concat_axis=0, tiled=True)  43.9 us
  transfers between devices with their start and end apart: 106, of which 38 were waited for; matrix products, arithmetic and copies ran while one was open for 24% of the time, Pallas kernels for 7%

profile of v4, /device:TPU:0, one launch (start us, length us, event | category | flops | bytes accessed | tf_op | source)
XLA Modules:
  0.0 1457.9 jit_solution(10444826343639488161)
XLA Ops:
  22.2 15.7 %collective-permute-done.1 = bf16[32,3200]{1,0:T(8,128)(2,1)S(1)} collective-permute-done((bf16[32,3200]{1,0:T(8,128)(2,1)S(1)}, bf16[32,3200]{1,0:T(8,128)(2,1)S(1)}, u32[]{:S(2)}, u32[]{:S(2)}) %collective-permute-start.1) | collective-permute-done | bytes 204832 | tf_op jit(solution)/shard_map/ppermute | solution.py:55
  51.1 14.3 collective-permute-done.10
  104.3 13.5 all-to-all-start
  123.7 42.7 %collective-permute-done.17 = bf16[32,1024]{1,0:T(8,128)(2,1)S(1)} collective-permute-done((bf16[32,1024]{1,0:T(8,128)(2,1)S(1)}, bf16[32,1024]{1,0:T(8,128)(2,1)S(1)}, u32[]{:S(2)}, u32[]{:S(2)}) %collective-permute-start.17) | collective-permute-done | bytes 65568 | tf_op jit(solution)/shard_map/ppermute | solution.py:55
  171.3 25.5 %collective-permute-done.20.refs_1_ = bf16[4,32,1024]{2,1,0:T(8,128)(2,1)S(1)} collective-permute-done((bf16[4,32,1024]{2,1,0:T(8,128)(2,1)S(1)}, bf16[4,32,1024]{2,1,0:T(8,128)(2,1)S(1)}, u32[]{:S(2)}, u32[]{:S(2)}) %collective-permute-start.20) | collective-permute-done | bytes 262176 | tf_op jit(solution)/shard_map/ppermute | solution.py:50
  208.2 15.0 %attend.2 = bf16[1024,256]{1,0:T(8,128)(2,1)} custom-call(s32[1]{0:T(128)} %bitcast.1.prefix_ref, bf16[1024,768]{1,0:T(8,128)(2,1)} %bitcast.14.x_ref), custom_call_target="tpu_custom_call" | custom-call | flops 1073741824 | bytes 3145728 | tf_op jit(solution)/shard_map/attend/pallas_call | solution.py:226
  235.7 14.7 %collective-permute-done.34.refs_1_ = bf16[4,128,1024]{2,1,0:T(8,128)(2,1)} collective-permute-done((bf16[4,128,1024]{2,1,0:T(8,128)(2,1)}, bf16[4,128,1024]{2,1,0:T(8,128)(2,1)}, u32[]{:S(2)}, u32[]{:S(2)}) %collective-permute-start.34) | collective-permute-done | bytes 1048608 | tf_op jit(solution)/shard_map/ppermute | solution.py:50
  258.4 14.4 collective-permute-done.29.refs_3_
  299.2 9.2 multiply_convert_fusion.5
  351.7 28.3 %collective-permute-done.41 = bf16[320,1024]{1,0:T(8,128)(2,1)S(1)} collective-permute-done((bf16[320,1024]{1,0:T(8,128)(2,1)S(1)}, bf16[320,1024]{1,0:T(8,128)(2,1)S(1)}, u32[]{:S(2)}, u32[]{:S(2)}) %collective-permute-start.41) | collective-permute-done | bytes 655392 | tf_op jit(solution)/shard_map/ppermute | solution.py:309
  401.6 58.2 %collective-permute-done.42 = bf16[640,1024]{1,0:T(8,128)(2,1)} collective-permute-done((bf16[640,1024]{1,0:T(8,128)(2,1)}, bf16[640,1024]{1,0:T(8,128)(2,1)}, u32[]{:S(2)}, u32[]{:S(2)}) %collective-permute-start.42) | collective-permute-done | bytes 1310752 | tf_op jit(solution)/shard_map/ppermute | solution.py:309
  488.6 14.9 %attend.3 = bf16[1024,256]{1,0:T(8,128)(2,1)} custom-call(s32[1]{0:T(128)} %bitcast.44.prefix_ref, bf16[1024,768]{1,0:T(8,128)(2,1)} %bitcast.46.x_ref), custom_call_target="tpu_custom_call" | custom-call | flops 1073741824 | bytes 3145728 | tf_op jit(solution)/shard_map/attend/pallas_call | solution.py:226
  510.1 31.4 %collective-permute-done.43 = bf16[320,1024]{1,0:T(8,128)(2,1)} collective-permute-done((bf16[320,1024]{1,0:T(8,128)(2,1)}, bf16[320,1024]{1,0:T(8,128)(2,1)}, u32[]{:S(2)}, u32[]{:S(2)}) %collective-permute-start.43) | collective-permute-done | bytes 655392 | tf_op jit(solution)/shard_map/ppermute | solution.py:309
  544.4 25.1 %collective-permute-done.48 = bf16[640,1024]{1,0:T(8,128)(2,1)} collective-permute-done((bf16[640,1024]{1,0:T(8,128)(2,1)}, bf16[640,1024]{1,0:T(8,128)(2,1)}, u32[]{:S(2)}, u32[]{:S(2)}) %collective-permute-start.48) | collective-permute-done | bytes 1310752 | tf_op jit(solution)/shard_map/ppermute | solution.py:309
  595.7 26.6 %collective-permute-done.49 = bf16[320,1024]{1,0:T(8,128)(2,1)} collective-permute-done((bf16[320,1024]{1,0:T(8,128)(2,1)}, bf16[320,1024]{1,0:T(8,128)(2,1)}, u32[]{:S(2)}, u32[]{:S(2)}) %collective-permute-start.49) | collective-permute-done | bytes 655392 | tf_op jit(solution)/shard_map/ppermute | solution.py:309
  634.5 10.9 all-to-all-done.9
  648.8 12.1 fusion.36
  678.5 13.7 all_to_all.80
  692.5 13.5 all_to_all.81
  709.0 27.7 %collective-permute-done.44 = bf16[320,1024]{1,0:T(8,128)(2,1)S(1)} collective-permute-done((bf16[320,1024]{1,0:T(8,128)(2,1)S(1)}, bf16[320,1024]{1,0:T(8,128)(2,1)S(1)}, u32[]{:S(2)}, u32[]{:S(2)}) %collective-permute-start.44) | collective-permute-done | bytes 655392 | tf_op jit(solution)/shard_map/ppermute | solution.py:309
  753.4 53.5 %collective-permute-done.45 = bf16[640,1024]{1,0:T(8,128)(2,1)S(1)} collective-permute-done((bf16[640,1024]{1,0:T(8,128)(2,1)S(1)}, bf16[640,1024]{1,0:T(8,128)(2,1)S(1)}, u32[]{:S(2)}, u32[]{:S(2)}) %collective-permute-start.45) | collective-permute-done | bytes 1310752 | tf_op jit(solution)/shard_map/ppermute | solution.py:309
  852.5 67.1 %collective-permute-done.51 = bf16[640,1024]{1,0:T(8,128)(2,1)} collective-permute-done((bf16[640,1024]{1,0:T(8,128)(2,1)}, bf16[640,1024]{1,0:T(8,128)(2,1)}, u32[]{:S(2)}, u32[]{:S(2)}) %collective-permute-start.51) | collective-permute-done | bytes 1310752 | tf_op jit(solution)/shard_map/ppermute | solution.py:309
  939.6 28.4 %collective-permute-done.52 = bf16[320,1024]{1,0:T(8,128)(2,1)S(1)} collective-permute-done((bf16[320,1024]{1,0:T(8,128)(2,1)S(1)}, bf16[320,1024]{1,0:T(8,128)(2,1)S(1)}, u32[]{:S(2)}, u32[]{:S(2)}) %collective-permute-start.52) | collective-permute-done | bytes 655392 | tf_op jit(solution)/shard_map/ppermute | solution.py:309
  988.5 11.7 fusion.43
  1017.4 13.4 collective-permute-done.61
  1080.5 11.1 all-to-all-done.3
  1131.5 24.6 %attend_back.3 = bf16[1024,768]{1,0:T(8,128)(2,1)} custom-call(s32[1]{0:T(128)} %bitcast.44.prefix_ref, bf16[1024,768]{1,0:T(8,128)(2,1)} %bitcast.46.x_ref, bf16[1024,256]{1,0:T(8,128)(2,1)} %bitcast.460), custom_call_target="tpu_custom_call" | custom-call | flops 2684354560 | bytes 7864320 | tf_op jit(solution)/shard_map/attend_back/pallas_call | solution.py:284
  1173.2 42.6 %all-to-all-done.8 = bf16[8,40,1024]{2,1,0:T(8,128)(2,1)S(1)} async-done(((bf16[8,40,1024]{2,1,0:T(8,128)(2,1)}), bf16[8,40,1024]{2,1,0:T(8,128)(2,1)S(1)}, u32[]{:S(2)}, u32[]{:S(2)}) %all-to-all-start.8) | async-done | bytes 655392 | tf_op jit(solution)/shard_map/all_to_all | solution.py:181
  1236.1 24.7 %attend_back.2 = bf16[1024,768]{1,0:T(8,128)(2,1)} custom-call(s32[1]{0:T(128)} %bitcast.1.prefix_ref, bf16[1024,768]{1,0:T(8,128)(2,1)} %bitcast.14.x_ref, bf16[1024,256]{1,0:T(8,128)(2,1)} %bitcast.459), custom_call_target="tpu_custom_call" | custom-call | flops 2684354560 | bytes 7864320 | tf_op jit(solution)/shard_map/attend_back/pallas_call | solution.py:284
  1289.8 36.5 %all-to-all-done.12 = bf16[4,256,768]{1,2,0:T(8,128)(2,1)} async-done(((bf16[4,256,768]{1,2,0:T(8,128)(2,1)}), bf16[4,256,768]{1,2,0:T(8,128)(2,1)}, u32[]{:S(2)}, u32[]{:S(2)}) %all-to-all-start.12) | async-done | bytes 1572896 | tf_op jit(solution)/shard_map/all_to_all | solution.py:175
  1369.3 15.1 %collective-permute-done.55 = bf16[4,2,32,1536]{3,2,1,0:T(8,128)(2,1)S(1)} collective-permute-done((bf16[4,2,32,1536]{3,2,1,0:T(8,128)(2,1)S(1)}, bf16[4,2,32,1536]{3,2,1,0:T(8,128)(2,1)S(1)}, u32[]{:S(2)}, u32[]{:S(2)}) %collective-permute-start.55) | collective-permute-done | bytes 786464 | tf_op jit(solution)/shard_map/ppermute | solution.py:50
  1427.1 21.7 %reduce-scatter.12.cloned.1.call-done = bf16[32,1536]{1,0:T(8,128)(2,1)} async-done(((bf16[128,1536]{1,0:T(8,128)(2,1)}), bf16[32,1536]{1,0:T(8,128)(2,1)}) %reduce-scatter.12.cloned.1.call-update) | async-done | bytes 98320 | tf_op jit(solution)/shard_map/reduce_scatter | solution.py:165
  (875 shorter events, 662.5 us)
Async XLA Ops:
  7.2 159.2 %all-gather.13.cloned.1.call-start = ((), (), s32[]{:S(2)}) async-start(), calls=%async_computation.34 | async-start | bytes 1310720 | tf_op jit(solution)/shard_map/all_gather | solution.py:126
  7.9 197.4 %all-gather.15.cloned.1.call-start = ((), (), s32[]{:S(2)}) async-start(), calls=%async_computation.35 | async-start | bytes 1310720 | tf_op jit(solution)/shard_map/all_gather | solution.py:126
  17.2 311.1 %all-gather.17.cloned.1.call-start = ((), (), s32[]{:S(2)}) async-start(), calls=%async_computation.36 | async-start | bytes 6291456 | tf_op jit(solution)/shard_map/all_gather | solution.py:318
  37.9 295.1 %all-gather.21.cloned.1.call-start = ((), (), s32[]{:S(2)}) async-start(), calls=%async_computation.38 | async-start | bytes 6291456 | tf_op jit(solution)/shard_map/all_gather | solution.py:318
  38.5 350.1 %all-gather.19.cloned.1.call-start = ((), (), s32[]{:S(2)}) async-start(), calls=%async_computation.37 | async-start | bytes 6291456 | tf_op jit(solution)/shard_map/all_gather | solution.py:318
  104.3 103.9 %all-to-all-start = ((bf16[4,256,768]{2,1,0:T(8,128)(2,1)}), bf16[4,256,768]{2,1,0:T(8,128)(2,1)}, u32[]{:S(2)}, u32[]{:S(2)}) async-start(bf16[4,256,768]{2,1,0:T(8,128)(2,1)} %bitcast.428), calls=%async_computation | async-start | bytes 3145728 | tf_op jit(solution)/shard_map/all_to_all | solution.py:175
  207.5 65.3 %collective-permute-start.29 = (bf16[4,32,4096]{2,1,0:T(8,128)(2,1)}, bf16[4,32,4096]{2,1,0:T(8,128)(2,1)}, u32[]{:S(2)}, u32[]{:S(2)}) collective-permute-start(bf16[4,32,4096]{2,1,0:T(8,128)(2,1)} %collective-permute-done.27.refs_1_), channel_id=1, source_target_pairs={{0,2},{1,3},{2,0},{3,1},{4,6},{5,7},{6,4},{7,5},{8,10},{9,11},{10,... | collective-permute-start | bytes 3145736 | tf_op jit(solution)/shard_map/ppermute | solution.py:50
  228.8 167.6 %all-gather.23.cloned.1.call-start = ((), (), s32[]{:S(2)}) async-start(), calls=%async_computation.39 | async-start | bytes 6291456 | tf_op jit(solution)/shard_map/all_gather | solution.py:318
  288.8 107.2 %collective-permute-start.46 = (bf16[320,1024]{1,0:T(8,128)(2,1)S(1)}, bf16[320,1024]{1,0:T(8,128)(2,1)S(1)}, u32[]{:S(2)}, u32[]{:S(2)}) collective-permute-start(bf16[320,1024]{1,0:T(8,128)(2,1)S(1)} %bitcast.400), channel_id=1, source_target_pairs={{0,16},{8,24},{16,0},{24,8},{1,17},{9,25},{17,1},{25,9},{2,18},{10... | collective-permute-start | bytes 1966088 | tf_op jit(solution)/shard_map/ppermute | solution.py:309
  346.8 141.8 %all-to-all-start.4 = ((bf16[4,256,768]{2,1,0:T(8,128)(2,1)}), bf16[4,256,768]{2,1,0:T(8,128)(2,1)}, u32[]{:S(2)}, u32[]{:S(2)}) async-start(bf16[4,256,768]{2,1,0:T(8,128)(2,1)} %bitcast.429), calls=%async_computation.4 | async-start | bytes 3145728 | tf_op jit(solution)/shard_map/all_to_all | solution.py:175
  395.5 64.3 %collective-permute-start.42 = (bf16[640,1024]{1,0:T(8,128)(2,1)}, bf16[640,1024]{1,0:T(8,128)(2,1)}, u32[]{:S(2)}, u32[]{:S(2)}) collective-permute-start(bf16[640,1024]{1,0:T(8,128)(2,1)} %convolution_convert_fusion.13), channel_id=1, source_target_pairs={{0,16},{8,24},{16,0},{24,8},{1,17},{9,25},{17,1},{25,9},{2,18},{10... | collective-permute-start | bytes 3932168 | tf_op jit(solution)/shard_map/ppermute | solution.py:309
  478.2 63.2 %collective-permute-start.43 = (bf16[320,1024]{1,0:T(8,128)(2,1)}, bf16[320,1024]{1,0:T(8,128)(2,1)}, u32[]{:S(2)}, u32[]{:S(2)}) collective-permute-start(bf16[320,1024]{1,0:T(8,128)(2,1)} %slice.401), channel_id=1, source_target_pairs={{0,16},{8,24},{16,0},{24,8},{1,17},{9,25},{17,1},{25,9},{2,18},{10... | collective-permute-start | bytes 1966088 | tf_op jit(solution)/shard_map/ppermute | solution.py:309
  482.2 87.3 %collective-permute-start.48 = (bf16[640,1024]{1,0:T(8,128)(2,1)}, bf16[640,1024]{1,0:T(8,128)(2,1)}, u32[]{:S(2)}, u32[]{:S(2)}) collective-permute-start(bf16[640,1024]{1,0:T(8,128)(2,1)} %convolution_convert_fusion.10), channel_id=1, source_target_pairs={{0,16},{8,24},{16,0},{24,8},{1,17},{9,25},{17,1},{25,9},{2,18},{10... | collective-permute-start | bytes 3932168 | tf_op jit(solution)/shard_map/ppermute | solution.py:309
  505.6 86.6 %all-to-all-start.5 = ((bf16[4,256,256]{1,2,0:T(8,128)(2,1)}), bf16[4,256,256]{1,2,0:T(8,128)(2,1)}, u32[]{:S(2)}, u32[]{:S(2)}) async-start(bf16[4,256,256]{1,2,0:T(8,128)(2,1)} %copy.56), calls=%async_computation.5 | async-start | bytes 1048576 | tf_op jit(solution)/shard_map/all_to_all | solution.py:175
  747.9 59.0 %collective-permute-start.45 = (bf16[640,1024]{1,0:T(8,128)(2,1)S(1)}, bf16[640,1024]{1,0:T(8,128)(2,1)S(1)}, u32[]{:S(2)}, u32[]{:S(2)}) collective-permute-start(bf16[640,1024]{1,0:T(8,128)(2,1)S(1)} %convolution_convert_fusion.11), channel_id=1, source_target_pairs={{0,16},{8,24},{16,0},{24,8},{1,17},{9,25},{17,1},{25,9},{2,18},{10... | collective-permute-start | bytes 3932168 | tf_op jit(solution)/shard_map/ppermute | solution.py:309
  832.1 105.2 %collective-permute-start.47 = (bf16[320,1024]{1,0:T(8,128)(2,1)}, bf16[320,1024]{1,0:T(8,128)(2,1)}, u32[]{:S(2)}, u32[]{:S(2)}) collective-permute-start(bf16[320,1024]{1,0:T(8,128)(2,1)} %slice.407), channel_id=1, source_target_pairs={{0,16},{8,24},{16,0},{24,8},{1,17},{9,25},{17,1},{25,9},{2,18},{10... | collective-permute-start | bytes 1966088 | tf_op jit(solution)/shard_map/ppermute | solution.py:309
  836.1 83.5 %collective-permute-start.51 = (bf16[640,1024]{1,0:T(8,128)(2,1)}, bf16[640,1024]{1,0:T(8,128)(2,1)}, u32[]{:S(2)}, u32[]{:S(2)}) collective-permute-start(bf16[640,1024]{1,0:T(8,128)(2,1)} %convolution_convert_fusion.7), channel_id=1, source_target_pairs={{0,16},{8,24},{16,0},{24,8},{1,17},{9,25},{17,1},{25,9},{2,18},{10... | collective-permute-start | bytes 3932168 | tf_op jit(solution)/shard_map/ppermute | solution.py:309
  974.7 291.3 %reduce-scatter.14.cloned.1.call-start = ((), (), s32[]{:S(2)}) async-start(), calls=%async_computation.27 | async-start | bytes 327680 | tf_op jit(solution)/shard_map/reduce_scatter | solution.py:165
  1039.4 366.4 %reduce-scatter.26.cloned.1.call-start = ((), (), s32[]{:S(2)}) async-start(), calls=%async_computation.33 | async-start | bytes 6291456 | tf_op jit(solution)/shard_map/reduce_scatter | solution.py:322
  1040.2 365.7 %reduce-scatter.24.cloned.1.call-start = ((), (), s32[]{:S(2)}) async-start(), calls=%async_computation.32 | async-start | bytes 6291456 | tf_op jit(solution)/shard_map/reduce_scatter | solution.py:322
  1051.7 360.3 %reduce-scatter.22.cloned.1.call-start = ((), (), s32[]{:S(2)}) async-start(), calls=%async_computation.31 | async-start | bytes 6291456 | tf_op jit(solution)/shard_map/reduce_scatter | solution.py:322
  1066.0 57.9 %collective-permute-start.53 = (bf16[4,2,2,128,1024]{4,3,2,1,0:T(8,128)(2,1)}, bf16[4,2,2,128,1024]{4,3,2,1,0:T(8,128)(2,1)}, u32[]{:S(2)}, u32[]{:S(2)}) collective-permute-start(bf16[4,2,2,128,1024]{4,3,2,1,0:T(8,128)(2,1)} %dynamic-slice_bitcast_fusion.1), channel_id=1, source_target_pairs={{0,1},{1,0},{2,3},{3,2},{4,5},{5,4},{6,7},{7,6},{8,9},{9,8},{10,11... | collective-permute-start | bytes 12582920 | tf_op jit(solution)/shard_map/ppermute | solution.py:50
  1075.9 90.0 %collective-permute-start.63 = (bf16[4,2,2,32,4096]{4,3,2,1,0:T(8,128)(2,1)}, bf16[4,2,2,32,4096]{4,3,2,1,0:T(8,128)(2,1)}, u32[]{:S(2)}, u32[]{:S(2)}) collective-permute-start(bf16[4,2,2,32,4096]{4,3,2,1,0:T(8,128)(2,1)} %dynamic-slice_bitcast_fusion), channel_id=1, source_target_pairs={{0,1},{1,0},{2,3},{3,2},{4,5},{5,4},{6,7},{7,6},{8,9},{9,8},{10,11... | collective-permute-start | bytes 12582920 | tf_op jit(solution)/shard_map/ppermute | solution.py:50
  1105.4 306.6 %reduce-scatter.20.cloned.1.call-start = ((), (), s32[]{:S(2)}) async-start(), calls=%async_computation.30 | async-start | bytes 6291456 | tf_op jit(solution)/shard_map/reduce_scatter | solution.py:322
  1160.9 106.6 %collective-permute-start.66 = (bf16[4,2,128,1024]{3,2,1,0:T(8,128)(2,1)}, bf16[4,2,128,1024]{3,2,1,0:T(8,128)(2,1)}, u32[]{:S(2)}, u32[]{:S(2)}) collective-permute-start(bf16[4,2,128,1024]{3,2,1,0:T(8,128)(2,1)} %dynamic-slice_bitcast_fusion.2), channel_id=1, source_target_pairs={{0,2},{1,3},{2,0},{3,1},{4,6},{5,7},{6,4},{7,5},{8,10},{9,11},{10,... | collective-permute-start | bytes 6291464 | tf_op jit(solution)/shard_map/ppermute | solution.py:50
  1215.8 55.0 %all-to-all-start.15 = ((bf16[4,256,768]{1,2,0:T(8,128)(2,1)}), bf16[4,256,768]{1,2,0:T(8,128)(2,1)}, u32[]{:S(2)}, u32[]{:S(2)}) async-start(bf16[4,256,768]{1,2,0:T(8,128)(2,1)} %copy.60), calls=%async_computation.15 | async-start | bytes 3145728 | tf_op jit(solution)/shard_map/all_to_all | solution.py:175
  1270.8 55.6 %all-to-all-start.12 = ((bf16[4,256,768]{1,2,0:T(8,128)(2,1)}), bf16[4,256,768]{1,2,0:T(8,128)(2,1)}, u32[]{:S(2)}, u32[]{:S(2)}) async-start(bf16[4,256,768]{1,2,0:T(8,128)(2,1)} %copy.58), calls=%async_computation.12 | async-start | bytes 3145728 | tf_op jit(solution)/shard_map/all_to_all | solution.py:175
  1275.1 143.0 %reduce-scatter.18.cloned.1.call-start = ((), (), s32[]{:S(2)}) async-start(), calls=%async_computation.29 | async-start | bytes 1310720 | tf_op jit(solution)/shard_map/reduce_scatter | solution.py:165
  1276.4 71.4 %collective-permute-start.67 = (bf16[4,128,1024]{2,1,0:T(8,128)(2,1)}, bf16[4,128,1024]{2,1,0:T(8,128)(2,1)}, u32[]{:S(2)}, u32[]{:S(2)}) collective-permute-start(bf16[4,128,1024]{2,1,0:T(8,128)(2,1)} %dynamic-slice_bitcast_fusion.6), channel_id=1, source_target_pairs={{0,4},{1,5},{2,6},{3,7},{4,0},{5,1},{6,2},{7,3},{8,12},{9,13},{10,... | collective-permute-start | bytes 3145736 | tf_op jit(solution)/shard_map/ppermute | solution.py:50
  1282.1 77.2 %collective-permute-start.65 = (bf16[4,32,4096]{2,1,0:T(8,128)(2,1)}, bf16[4,32,4096]{2,1,0:T(8,128)(2,1)}, u32[]{:S(2)}, u32[]{:S(2)}) collective-permute-start(bf16[4,32,4096]{2,1,0:T(8,128)(2,1)} %dynamic-slice_bitcast_fusion.7), channel_id=1, source_target_pairs={{0,2},{1,3},{2,0},{3,1},{4,6},{5,7},{6,4},{7,5},{8,10},{9,11},{10,... | collective-permute-start | bytes 3145736 | tf_op jit(solution)/shard_map/ppermute | solution.py:50
  1350.4 69.5 %reduce-scatter.16.cloned.1.call-start = ((), (), s32[]{:S(2)}) async-start(), calls=%async_computation.28 | async-start | bytes 1310720 | tf_op jit(solution)/shard_map/reduce_scatter | solution.py:165
  1361.8 65.3 %reduce-scatter.10.cloned.1.call-start = ((), (), s32[]{:S(2)}) async-start(), calls=%async_computation.25 | async-start | bytes 491520 | tf_op jit(solution)/shard_map/reduce_scatter | solution.py:165
  (257 other events, 4399.8 us)
Sparse Core Ops, SparseCore 0:
  9.6 39.4 all-gather.12
  50.7 29.2 all-gather.14
  81.6 85.5 all-gather.16
  168.6 55.6 all-gather.20
  225.6 57.3 all-gather.18
  284.4 100.6 all-gather.22
  1039.5 17.7 reduce-scatter.13
  1059.7 61.0 reduce-scatter.25
  1123.0 57.7 reduce-scatter.23
  1183.0 80.6 reduce-scatter.21
  1265.9 80.3 reduce-scatter.19
  1350.6 26.9 reduce-scatter.17
  1379.8 25.7 reduce-scatter.15
  1407.8 19.2 reduce-scatter.9
  1429.8 18.9 reduce-scatter.11

commit v5 on v4

--- a/solution.py
+++ b/solution.py
@@ -398,11 +398,18 @@
     full_qkv = assemble(
         [(mask, jnp.concatenate([piece, qkv_pieces[mask][:, :, :half]], 2)) for mask, piece in part_a]
     )
+    mix_dp = turn_gather(mix_weight)
+    full_qkv = after(full_qkv, mix_dp)
     full_gain = assemble([(mask, piece[:, :, half:]) for mask, piece in part_b])
     gains = full_gain[:, :2].T.astype(f32)
-    full_mix = assemble(spread(turn_gather(mix_weight), order_a))
-    full_up = assemble(spread(gather_dp(up_weight), order_a))
-    full_down = assemble(spread(gather_dp(down_weight), order_b))
+    full_mix = assemble(spread(mix_dp, order_a))
+    up_pieces = spread(gather_dp(up_weight), order_a)
+    down_pieces = spread(gather_dp(down_weight), order_b)
+    full_up, full_down = (assemble(up_pieces), assemble(down_pieces))
+    hops = [
+        [piece for pieces in (up_pieces, down_pieces) for _, piece in pieces[start : 2 * start]]
+        for start in (1, 2)
+    ]
 
     up_both, down_both = ([], [])
     for layer in range(2):
@@ -412,6 +419,7 @@
 
     dense = []
     slots_in = []
+    sends, mixes = ([], [])
     for micro in micros:
         source = tokens[micro, 0]
         if micro > 0:
@@ -421,8 +429,14 @@
         qkv = jnp.dot(normed, full_qkv, preferred_element_type=f32).astype(low)
         blocks = qkv.reshape(rows_dev, dp_count, 3 * mine).transpose(1, 0, 2)
         whole = swap_heads(blocks).reshape(length, 3 * mine)
+        if micro == 0:
+            whole = after(whole, *hops[0])
         mixed = attend(whole, prefix[micro], block).reshape(dp_count, rows_dev, mine)
-        mixed = swap_heads(mixed).transpose(1, 0, 2).reshape(rows_dev, width)
+        mixed = swap_heads(mixed)
+        mixes.append(mixed)
+        if micro == 0:
+            mixed = after(mixed, *hops[1])
+        mixed = mixed.transpose(1, 0, 2).reshape(rows_dev, width)
         attn = jnp.dot(mixed, full_mix, preferred_element_type=f32)
         resid = inputs + attn
         normed2 = layer_norm(resid, gains[1]).astype(low)
@@ -432,10 +446,10 @@
         dense_out = resid + ffn
         sent = jnp.dot(places[micro], dense_out.astype(low), preferred_element_type=f32).astype(low)
         dense.append((inputs, normed, whole, mixed, attn, resid, ffn, normed2, pre, hidden, dense_out))
+        sends.append(sent)
         slots_in.append(swap_experts(sent))
 
     slot_count = experts * capacity
-    gain_one = jnp.zeros((width,), f32)
     first_stage = []
     for micro in micros:
         rows = both_rows(slots_in[micro])
@@ -449,11 +463,11 @@
         out0 = jnp.dot(h0, down_both[0], preferred_element_type=f32).astype(low)
         first_stage.append((rows, sig, z0, pre0, h0, out0))
     second_stage = []
-    for micro in micros:
+
+    def run_second(micro, *others):
         rows, sig = first_stage[micro][:2]
         total = sum_pair(first_stage[micro][-1])
-        if micro > 0:
-            total = after(total, second_stage[micro - 1][-1])
+        total = after(total, *others)
         state1 = rows.astype(f32) + total
         z1 = layer_norm(state1, gain_ex[1]).astype(low)
         pre1 = jnp.dot(z1, up_both[1], preferred_element_type=f32)
@@ -465,6 +479,7 @@
         pre_grad = gelu_back(pre1, contract_cols(grad_y, down_both[1])).astype(low)
         normed_part = contract_cols(pre_grad, up_both[1]).astype(low)
         second_stage.append((state1, out1, incoming, grad2, z1, h1, grad_y, pre_grad, normed_part))
+
     hidden_dev = up_ex.shape[2]
     hidden_halves = (slice(0, hidden_dev), slice(hidden_dev, 2 * hidden_dev))
 
@@ -477,38 +492,29 @@
             ]
         ).astype(low)
 
-    up_grads, down_grads = ([None, None], [None, None])
-    by_stage = list(zip(*second_stage))
-    down_grads[1] = grad_halves(by_stage[5], by_stage[6], True)
-    up_grads[1] = grad_halves(by_stage[4], by_stage[7], False)
+    gain_ones = []
     third_stage = []
-    for micro in micros:
+
+    def run_third(micro, *others):
         rows, sig, z0, pre0, h0, _ = first_stage[micro]
         state1, out1, incoming, grad2 = second_stage[micro][:4]
         total = sum_pair(second_stage[micro][-1])
-        if micro > 0:
-            total = after(total, third_stage[micro - 1][-1], up_grads[1], down_grads[1])
+        total = after(total, *others)
         state_grad, gain_grad = norm_back(state1, gain_ex[1], total)
-        gain_one = gain_one + gain_grad
         grad1 = grad2 + state_grad
         grad_y = grad1.astype(low)
         pre_grad = gelu_back(pre0, contract_cols(grad_y, down_both[0])).astype(low)
         normed_part = contract_cols(pre_grad, up_both[0]).astype(low)
         third_stage.append((grad1, grad_y, pre_grad, normed_part))
-    by_first, by_third = (list(zip(*first_stage)), list(zip(*third_stage)))
-    down_grads[0] = grad_halves(by_first[4], by_third[1], True)
-    up_grads[0] = grad_halves(by_first[2], by_third[2], False)
-    down_sum, up_sum = ([None, None], [None, None])
-    for layer in (1, 0):
-        down_sum[layer] = scatter_near(down_grads[layer]).astype(f32)
-        up_sum[layer] = scatter_near(up_grads[layer]).astype(f32)
+        gain_ones.append(gain_grad)
     own_grads = []
     branches = []
-    for micro in micros:
+
+    def run_own(micro, *others):
         rows, sig = first_stage[micro][:2]
         state1, out1, incoming = second_stage[micro][:3]
         grad1, normed_part = (third_stage[micro][i] for i in (0, 3))
-        normed_grad = sum_own(normed_part)
+        normed_grad = after(sum_own(normed_part), *others)
         own_rows = rows[:slot_count].astype(f32)
         state_grad, gain_grad = norm_back(own_rows, gain_ex[0], normed_grad)
         own_sig = sig[:slot_count]
@@ -520,43 +526,81 @@
         cent_grad = jnp.sum(score_grad * own_rows, 0)
         own_grads.append((row_grad.astype(low), gain_grad, cent_grad))
 
-    gain_acc = jnp.zeros((2, width), f32)
+    gain_sums, resid_grads, late = ([], [], [])
     input_grads = []
     kept = []
     kept_dense = []
     order_c, order_d = (order_a[::-1], order_b[::-1])
-    for micro in micros:
+    whole_grads = []
+
+    def run_ffn_back(micro):
         inputs, normed, whole, mixed, attn, resid, ffn, normed2, pre, hidden, _ = dense[micro]
         grad_back = swap_experts(own_grads[micro][0])
         after_grad = cotangent[micro, 0] + contract_rows(places[micro], grad_back)
         ffn_low = after_grad.astype(low)
+        if micro == micro_count - 1:
+            ffn_low = after(ffn_low, up_sum[1])
         hidden_grad = contract_cols(ffn_low, full_down)
         pre_grad = gelu_back(pre, hidden_grad).astype(low)
         normed2_grad = contract_cols(pre_grad, full_up)
         resid_part, gain2_grad = norm_back(resid, gains[1], normed2_grad)
         resid_grad = after_grad + resid_part
         attn_low = resid_grad.astype(low)
+        kept_dense.append((normed2, pre_grad, hidden, ffn_low))
+        resid_grads.append((resid_grad, attn_low, gain2_grad))
+
+    def run_attend_back(micro):
+        inputs, normed, whole, mixed = dense[micro][:4]
+        resid_grad, attn_low, gain2_grad = resid_grads[micro]
         mixed_grad = contract_cols(attn_low, full_mix).astype(low)
         mixed_grad = mixed_grad.reshape(rows_dev, dp_count, mine).transpose(1, 0, 2)
         mixed_grad = swap_heads(mixed_grad).reshape(length, mine)
-        kept_dense.append((normed2, pre_grad, hidden, ffn_low))
-        if micro == 0:
-            mixed_grad = after(mixed_grad, up_grads[0], down_grads[0], down_sum[1])
         if micro == micro_count - 1:
             joined = [jnp.concatenate(parts, 0) for parts in zip(*kept_dense)]
             down_start = scatter_start(contract_rows(joined[2], joined[3]).astype(low), order_c)
             up_low = contract_rows(joined[0], joined[1]).astype(low)
-            mixed_grad = after(mixed_grad, down_start[0], up_low, up_sum[1])
+            mixed_grad = after(mixed_grad, down_start[0], up_low, down_sum[0])
+            late.extend((down_start, up_low))
         whole_grad = attend_back(whole, mixed_grad, prefix[micro], block)
+        whole_grads.append(whole_grad)
         qkv_grad = swap_heads(whole_grad.reshape(dp_count, rows_dev, 3 * mine))
         qkv_grad = qkv_grad.transpose(1, 0, 2).reshape(rows_dev, 3 * width)
         if micro == micro_count - 1:
-            qkv_grad = after(qkv_grad, down_sum[0])
+            qkv_grad = after(qkv_grad, up_sum[0])
         normed_grad = contract_cols(qkv_grad, full_qkv)
         input_part, gain1_grad = norm_back(inputs, gains[0], normed_grad)
         input_grads.append(resid_grad + input_part)
-        gain_acc = gain_acc + jnp.stack([gain1_grad, gain2_grad])
+        gain_sums.append(jnp.stack([gain1_grad, gain2_grad]))
         kept.append((normed, qkv_grad, mixed, attn_low))
+
+    last = micro_count - 1
+    for micro in micros:
+        if micro < last:
+            run_second(micro, mixes[micro + 1])
+            run_third(micro, sends[micro + 1])
+            run_own(micro)
+            run_ffn_back(micro)
+        else:
+            run_second(micro, *(resid_grads[-1][1:2] if micro else ()))
+    for micro in micros[:-1]:
+        run_attend_back(micro)
+    up_grads, down_grads = ([None, None], [None, None])
+    by_stage = list(zip(*second_stage))
+    down_grads[1] = grad_halves(by_stage[5], by_stage[6], True)
+    up_grads[1] = grad_halves(by_stage[4], by_stage[7], False)
+    run_third(last, up_grads[1], down_grads[1], *whole_grads)
+    by_first, by_third = (list(zip(*first_stage)), list(zip(*third_stage)))
+    down_grads[0] = grad_halves(by_first[4], by_third[1], True)
+    up_grads[0] = grad_halves(by_first[2], by_third[2], False)
+    down_sum, up_sum = ([None, None], [None, None])
+    for layer in (1, 0):
+        down_sum[layer] = scatter_near(down_grads[layer]).astype(f32)
+        up_sum[layer] = scatter_near(up_grads[layer]).astype(f32)
+    run_own(last, down_sum[1])
+    run_ffn_back(last)
+    run_attend_back(last)
+    down_start, up_low = late
+    gain_acc, gain_one = (sum(gain_sums), sum(gain_ones))
     joined = [jnp.concatenate(parts, 0) for parts in zip(*kept)]
     down_out = scatter_end(down_start)
     up_out = scatter_rows(up_low, order_d)

time: 1470 us -> 1370 us (0.932)
  waiting for transfers between devices: 691 us -> 570 us
  blocking collectives: 27.2 us -> 0 us
  starting transfers between devices: 141 us -> 165 us
  matrix products: 238 us -> 253 us
    ppermute x12, waiting for transfers between devices: 349 us -> 200 us  [flip(): return lax.ppermute(values, 'dp', [(i, i ^ bit) for i in range(count)])]
    all_to_all x8, waiting for transfers between devices: 38.1 us -> 110 us  [swap_heads(): return lax.all_to_all(blocks, 'dp', split_axis=0, concat_axis=0, tiled=True)]
    ppermute x53, waiting for transfers between devices: 138 us -> 69.9 us  [swap(): return lax.ppermute(values, 'expert', [(i, i ^ bit) for i in range(count)])]
    reduce_scatter x5, waiting for transfers between devices: 27.1 us -> 75 us  [scatter_end(): lax.psum_scatter(current.reshape(-1, current.shape[-1]), 'dp', scatter_di...]
    all_gather x4, waiting for transfers between devices: 0.04 us -> 37.5 us  [gather_near(): return lax.all_gather(shard, 'dp', axis=0, axis_index_groups=near_groups())]
    all_to_all x6 -> x8, waiting for transfers between devices: 77.6 us -> 41.7 us  [swap_experts(): lax.all_to_all(blocks, 'expert', split_axis=0, concat_axis=0, tiled=True)]
    all_to_all x2 -> x0, blocking collectives: 27.2 us -> none  [swap_experts(): lax.all_to_all(blocks, 'expert', split_axis=0, concat_axis=0, tiled=True)]
    ppermute x12, waiting for transfers between devices: 58.9 us -> 32.8 us  [turn(): lax.ppermute(values, 'dp', [(i, (i + shift) % count) for i in range(count)])]
  transfers between devices with their start and end apart: 106 -> 108, of which waited for: 38 -> 38; matrix products, arithmetic and copies ran while one was open for 24% -> 28% of each run, Pallas kernels for 7% -> 8%
where the time goes in v5:
time: 1370 us; the launch traced here: 1360 us
  waiting for transfers between devices  570 us (42%)
  matrix products  253 us (18%)
  starting transfers between devices  165 us (12%)
  other arithmetic  141 us (10%)
  local copies, waits for them, and re-layouts  110 us (8%)
  Pallas kernels  103 us (8%)
  between operations  17.6 us (1%)
    ppermute x12, waiting for transfers between devices, flip(): return lax.ppermute(values, 'dp', [(i, i ^ bit) for i in range(count)])  200 us
    all_to_all x8, waiting for transfers between devices, swap_heads(): return lax.all_to_all(blocks, 'dp', split_axis=0, concat_axis=0, tiled=True)  110 us
    dot_general x16, matrix products, contract_cols(): lax.dot_general(left, right, (((1,), (1,)), ((), ())), preferred_element_...  94.7 us
    reduce_scatter x5, waiting for transfers between devices, scatter_end(): lax.psum_scatter(current.reshape(-1, current.shape[-1]), 'dp', scatter_di...  75 us
    ppermute x53, waiting for transfers between devices, swap(): return lax.ppermute(values, 'expert', [(i, i ^ bit) for i in range(count)])  69.9 us
    dot_general x16, matrix products, contract_rows(): lax.dot_general(left, right, (((0,), (0,)), ((), ())), preferred_element_...  65.2 us
    pallas_call x2, Pallas kernels, attend_back(): pl.pallas_call(attend_back_kernel, out_shape=jax.ShapeDtypeStruct((length...  49.6 us
    all_to_all x8, waiting for transfers between devices, swap_experts(): lax.all_to_all(blocks, 'expert', split_axis=0, concat_axis=0, tiled=True)  41.7 us
  transfers between devices with their start and end apart: 108, of which 38 were waited for; matrix products, arithmetic and copies ran while one was open for 28% of the time, Pallas kernels for 8%

profile of v5, /device:TPU:0, one launch (start us, length us, event | category | flops | bytes accessed | tf_op | source)
XLA Modules:
  0.0 1359.6 jit_solution(14664434205612892506)
XLA Ops:
  22.3 15.6 %collective-permute-done.1 = bf16[32,3200]{1,0:T(8,128)(2,1)S(1)} collective-permute-done((bf16[32,3200]{1,0:T(8,128)(2,1)S(1)}, bf16[32,3200]{1,0:T(8,128)(2,1)S(1)}, u32[]{:S(2)}, u32[]{:S(2)}) %collective-permute-start.1) | collective-permute-done | bytes 204832 | tf_op jit(solution)/shard_map/ppermute | solution.py:55
  38.5 13.5 collective-permute-start.17
  81.9 9.0 collective-permute-done.4
  153.1 23.6 %all-to-all-done = bf16[4,256,768]{2,1,0:T(8,128)(2,1)} async-done(((bf16[4,256,768]{2,1,0:T(8,128)(2,1)}), bf16[4,256,768]{2,1,0:T(8,128)(2,1)}, u32[]{:S(2)}, u32[]{:S(2)}) %all-to-all-start) | async-done | bytes 1572896 | tf_op jit(solution)/shard_map/all_to_all | solution.py:175
  192.9 11.2 collective-permute-done.46
  207.5 15.0 %attend.2 = bf16[1024,256]{1,0:T(8,128)(2,1)} custom-call(s32[1]{0:T(128)} %bitcast.1.prefix_ref, bf16[1024,768]{1,0:T(8,128)(2,1)} %bitcast.17.x_ref), custom_call_target="tpu_custom_call" | custom-call | flops 1073741824 | bytes 3145728 | tf_op jit(solution)/shard_map/attend/pallas_call | solution.py:226
  255.0 9.8 multiply_convert_fusion.5
  311.6 26.2 %collective-permute-done.41 = bf16[320,1024]{1,0:T(8,128)(2,1)S(1)} collective-permute-done((bf16[320,1024]{1,0:T(8,128)(2,1)S(1)}, bf16[320,1024]{1,0:T(8,128)(2,1)S(1)}, u32[]{:S(2)}, u32[]{:S(2)}) %collective-permute-start.41) | collective-permute-done | bytes 655392 | tf_op jit(solution)/shard_map/ppermute | solution.py:309
  355.9 8.4 all-to-all-done.3
  365.4 15.0 %attend.3 = bf16[1024,256]{1,0:T(8,128)(2,1)} custom-call(s32[1]{0:T(128)} %bitcast.36.prefix_ref, bf16[1024,768]{1,0:T(8,128)(2,1)} %bitcast.435), custom_call_target="tpu_custom_call" | custom-call | flops 1073741824 | bytes 3145728 | tf_op jit(solution)/shard_map/attend/pallas_call | solution.py:226
  388.4 37.5 %all-gather.23.cloned.1.call-done = bf16[2048,1024]{1,0:T(8,128)(2,1)} async-done(((bf16[1024,1024]{1,0:T(8,128)(2,1)}), bf16[2048,1024]{1,0:T(8,128)(2,1)}) %all-gather.23.cloned.1.call-update) | async-done | bytes 4194320 | tf_op jit(solution)/shard_map/all_gather | solution.py:318
  425.8 7.9 fusion.235
  444.4 10.1 multiply_convert_fusion.2
  498.5 80.3 %collective-permute-done.44 = bf16[320,1024]{1,0:T(8,128)(2,1)} collective-permute-done((bf16[320,1024]{1,0:T(8,128)(2,1)}, bf16[320,1024]{1,0:T(8,128)(2,1)}, u32[]{:S(2)}, u32[]{:S(2)}) %collective-permute-start.44) | collective-permute-done | bytes 655392 | tf_op jit(solution)/shard_map/ppermute | solution.py:309
  615.9 53.0 %collective-permute-done.48 = bf16[320,1024]{1,0:T(8,128)(2,1)S(1)} collective-permute-done((bf16[320,1024]{1,0:T(8,128)(2,1)S(1)}, bf16[320,1024]{1,0:T(8,128)(2,1)S(1)}, u32[]{:S(2)}, u32[]{:S(2)}) %collective-permute-start.48) | collective-permute-done | bytes 655392 | tf_op jit(solution)/shard_map/ppermute | solution.py:309
  679.2 9.3 all-to-all-done.8
  690.3 11.8 fusion.36
  769.9 36.1 %all-to-all-done.10 = bf16[4,256,256]{2,1,0:T(8,128)(2,1)} async-done(((bf16[4,256,256]{2,1,0:T(8,128)(2,1)}), bf16[4,256,256]{2,1,0:T(8,128)(2,1)}, u32[]{:S(2)}, u32[]{:S(2)}) %all-to-all-start.10) | async-done | bytes 524320 | tf_op jit(solution)/shard_map/all_to_all | solution.py:175
  806.1 24.9 %attend_back.2 = bf16[1024,768]{1,0:T(8,128)(2,1)} custom-call(s32[1]{0:T(128)} %bitcast.1.prefix_ref, bf16[1024,768]{1,0:T(8,128)(2,1)} %bitcast.17.x_ref, bf16[1024,256]{1,0:T(8,128)(2,1)} %bitcast.66.grad_ref), custom_call_target="tpu_custom_call" | custom-call | flops 2684354560 | bytes 7864320 | tf_op jit(solution)/shard_map/attend_back/pallas_call | solution.py:284
  854.0 24.4 %collective-permute-done.52 = bf16[320,1024]{1,0:T(8,128)(2,1)S(1)} collective-permute-done((bf16[320,1024]{1,0:T(8,128)(2,1)S(1)}, bf16[320,1024]{1,0:T(8,128)(2,1)S(1)}, u32[]{:S(2)}, u32[]{:S(2)}) %collective-permute-start.52) | collective-permute-done | bytes 655392 | tf_op jit(solution)/shard_map/ppermute | solution.py:309
  886.8 11.1 all-to-all-done.13
  899.6 12.0 fusion.43
  928.7 13.3 collective-permute-done.61
  990.8 11.0 all-to-all-done.5
  1022.9 7.6 fusion.1
  1034.3 24.7 %attend_back.3 = bf16[1024,768]{1,0:T(8,128)(2,1)} custom-call(s32[1]{0:T(128)} %bitcast.36.prefix_ref, bf16[1024,768]{1,0:T(8,128)(2,1)} %bitcast.436, bf16[1024,256]{1,0:T(8,128)(2,1)} %bitcast.81.grad_ref), custom_call_target="tpu_custom_call" | custom-call | flops 2684354560 | bytes 7864320 | tf_op jit(solution)/shard_map/attend_back/pallas_call | solution.py:284
  1099.9 15.4 %collective-permute-done.74 = f32[3080]{0:T(1024)S(1)} collective-permute-done((f32[3080]{0:T(1024)S(1)}, f32[3080]{0:T(1024)S(1)}, u32[]{:S(2)}, u32[]{:S(2)}) %collective-permute-start.74) | collective-permute-done | bytes 12352 | tf_op jit(solution)/shard_map/ppermute | solution.py:55
  1141.6 38.1 %all-to-all-done.11 = bf16[4,256,768]{1,2,0:T(8,128)(2,1)} async-done(((bf16[4,256,768]{1,2,0:T(8,128)(2,1)}), bf16[4,256,768]{1,2,0:T(8,128)(2,1)}, u32[]{:S(2)}, u32[]{:S(2)}) %all-to-all-start.11) | async-done | bytes 1572896 | tf_op jit(solution)/shard_map/all_to_all | solution.py:175
  1222.9 15.0 %collective-permute-done.55 = bf16[4,2,32,1536]{3,2,1,0:T(8,128)(2,1)S(1)} collective-permute-done((bf16[4,2,32,1536]{3,2,1,0:T(8,128)(2,1)S(1)}, bf16[4,2,32,1536]{3,2,1,0:T(8,128)(2,1)S(1)}, u32[]{:S(2)}, u32[]{:S(2)}) %collective-permute-start.55) | collective-permute-done | bytes 786464 | tf_op jit(solution)/shard_map/ppermute | solution.py:50
  1280.7 26.3 %reduce-scatter.16.cloned.1.call-done = bf16[32,4096]{1,0:T(8,128)(2,1)} async-done(((bf16[128,4096]{1,0:T(8,128)(2,1)}), bf16[32,4096]{1,0:T(8,128)(2,1)}) %reduce-scatter.16.cloned.1.call-update) | async-done | bytes 262160 | tf_op jit(solution)/shard_map/reduce_scatter | solution.py:165
  1308.8 19.7 %reduce-scatter.10.cloned.1.call-done = bf16[32,1536]{1,0:T(8,128)(2,1)} async-done(((bf16[128,1536]{1,0:T(8,128)(2,1)}), bf16[32,1536]{1,0:T(8,128)(2,1)}) %reduce-scatter.10.cloned.1.call-update) | async-done | bytes 98320 | tf_op jit(solution)/shard_map/reduce_scatter | solution.py:165
  1328.5 21.8 %reduce-scatter.12.cloned.1.call-done = bf16[32,1536]{1,0:T(8,128)(2,1)} async-done(((bf16[128,1536]{1,0:T(8,128)(2,1)}), bf16[32,1536]{1,0:T(8,128)(2,1)}) %reduce-scatter.12.cloned.1.call-update) | async-done | bytes 98320 | tf_op jit(solution)/shard_map/reduce_scatter | solution.py:165
  (871 shorter events, 683.5 us)
Async XLA Ops:
  7.2 131.1 %all-gather.13.cloned.1.call-start = ((), (), s32[]{:S(2)}) async-start(), calls=%async_computation.34 | async-start | bytes 1310720 | tf_op jit(solution)/shard_map/all_gather | solution.py:126
  7.9 131.9 %all-gather.15.cloned.1.call-start = ((), (), s32[]{:S(2)}) async-start(), calls=%async_computation.35 | async-start | bytes 1310720 | tf_op jit(solution)/shard_map/all_gather | solution.py:126
  17.2 268.2 %all-gather.17.cloned.1.call-start = ((), (), s32[]{:S(2)}) async-start(), calls=%async_computation.36 | async-start | bytes 6291456 | tf_op jit(solution)/shard_map/all_gather | solution.py:318
  38.0 252.1 %all-gather.21.cloned.1.call-start = ((), (), s32[]{:S(2)}) async-start(), calls=%async_computation.38 | async-start | bytes 6291456 | tf_op jit(solution)/shard_map/all_gather | solution.py:318
  58.4 73.3 %all-to-all-start.7 = ((bf16[8,40,1024]{2,1,0:T(8,128)(2,1)}), bf16[8,40,1024]{2,1,0:T(8,128)(2,1)S(1)}, u32[]{:S(2)}, u32[]{:S(2)}) async-start(bf16[8,40,1024]{2,1,0:T(8,128)(2,1)} %bitcast.427), calls=%async_computation.7 | async-start | bytes 1310720 | tf_op jit(solution)/shard_map/all_to_all | solution.py:181
  62.1 284.2 %all-gather.19.cloned.1.call-start = ((), (), s32[]{:S(2)}) async-start(), calls=%async_computation.37 | async-start | bytes 6291456 | tf_op jit(solution)/shard_map/all_gather | solution.py:318
  147.8 56.3 %collective-permute-start.46 = (bf16[320,1024]{1,0:T(8,128)(2,1)S(1)}, bf16[320,1024]{1,0:T(8,128)(2,1)S(1)}, u32[]{:S(2)}, u32[]{:S(2)}) collective-permute-start(bf16[320,1024]{1,0:T(8,128)(2,1)S(1)} %bitcast.398), channel_id=1, source_target_pairs={{0,16},{8,24},{16,0},{24,8},{1,17},{9,25},{17,1},{25,9},{2,18},{10... | collective-permute-start | bytes 1966088 | tf_op jit(solution)/shard_map/ppermute | solution.py:309
  229.6 196.2 %all-gather.23.cloned.1.call-start = ((), (), s32[]{:S(2)}) async-start(), calls=%async_computation.39 | async-start | bytes 6291456 | tf_op jit(solution)/shard_map/all_gather | solution.py:318
  306.5 57.7 %all-to-all-start.3 = ((bf16[4,256,768]{2,1,0:T(8,128)(2,1)}), bf16[4,256,768]{2,1,0:T(8,128)(2,1)S(1)}, u32[]{:S(2)}, u32[]{:S(2)}) async-start(bf16[4,256,768]{2,1,0:T(8,128)(2,1)} %bitcast.375), calls=%async_computation.3 | async-start | bytes 3145728 | tf_op jit(solution)/shard_map/all_to_all | solution.py:175
  353.2 80.5 %collective-permute-start.42 = (bf16[640,1024]{1,0:T(8,128)(2,1)}, bf16[640,1024]{1,0:T(8,128)(2,1)}, u32[]{:S(2)}, u32[]{:S(2)}) collective-permute-start(bf16[640,1024]{1,0:T(8,128)(2,1)} %convolution_convert_fusion.13), channel_id=1, source_target_pairs={{0,16},{8,24},{16,0},{24,8},{1,17},{9,25},{17,1},{25,9},{2,18},{10... | collective-permute-start | bytes 3932168 | tf_op jit(solution)/shard_map/ppermute | solution.py:309
  382.5 56.0 %all-to-all-start.4 = ((bf16[4,256,256]{1,2,0:T(8,128)(2,1)}), bf16[4,256,256]{1,2,0:T(8,128)(2,1)}, u32[]{:S(2)}, u32[]{:S(2)}) async-start(bf16[4,256,256]{1,2,0:T(8,128)(2,1)} %copy.56), calls=%async_computation.4 | async-start | bytes 1048576 | tf_op jit(solution)/shard_map/all_to_all | solution.py:175
  490.3 98.1 %collective-permute-start.47 = (bf16[640,1024]{1,0:T(8,128)(2,1)}, bf16[640,1024]{1,0:T(8,128)(2,1)}, u32[]{:S(2)}, u32[]{:S(2)}) collective-permute-start(bf16[640,1024]{1,0:T(8,128)(2,1)} %convolution_convert_fusion.10), channel_id=1, source_target_pairs={{0,16},{8,24},{16,0},{24,8},{1,17},{9,25},{17,1},{25,9},{2,18},{10... | collective-permute-start | bytes 3932168 | tf_op jit(solution)/shard_map/ppermute | solution.py:309
  494.4 84.4 %collective-permute-start.44 = (bf16[320,1024]{1,0:T(8,128)(2,1)}, bf16[320,1024]{1,0:T(8,128)(2,1)}, u32[]{:S(2)}, u32[]{:S(2)}) collective-permute-start(bf16[320,1024]{1,0:T(8,128)(2,1)} %bitcast.54), channel_id=1, source_target_pairs={{0,16},{8,24},{16,0},{24,8},{1,17},{9,25},{17,1},{25,9},{2,18},{10... | collective-permute-start | bytes 1966088 | tf_op jit(solution)/shard_map/ppermute | solution.py:309
  608.5 60.4 %collective-permute-start.48 = (bf16[320,1024]{1,0:T(8,128)(2,1)S(1)}, bf16[320,1024]{1,0:T(8,128)(2,1)S(1)}, u32[]{:S(2)}, u32[]{:S(2)}) collective-permute-start(bf16[320,1024]{1,0:T(8,128)(2,1)S(1)} %slice.409), channel_id=1, source_target_pairs={{0,16},{8,24},{16,0},{24,8},{1,17},{9,25},{17,1},{25,9},{2,18},{10... | collective-permute-start | bytes 1966088 | tf_op jit(solution)/shard_map/ppermute | solution.py:309
  612.5 99.7 %collective-permute-start.45 = (bf16[640,1024]{1,0:T(8,128)(2,1)}, bf16[640,1024]{1,0:T(8,128)(2,1)}, u32[]{:S(2)}, u32[]{:S(2)}) collective-permute-start(bf16[640,1024]{1,0:T(8,128)(2,1)} %convolution_convert_fusion.11), channel_id=1, source_target_pairs={{0,16},{8,24},{16,0},{24,8},{1,17},{9,25},{17,1},{25,9},{2,18},{10... | collective-permute-start | bytes 3932168 | tf_op jit(solution)/shard_map/ppermute | solution.py:309
  744.9 61.2 %all-to-all-start.10 = ((bf16[4,256,256]{2,1,0:T(8,128)(2,1)}), bf16[4,256,256]{2,1,0:T(8,128)(2,1)}, u32[]{:S(2)}, u32[]{:S(2)}) async-start(bf16[4,256,256]{2,1,0:T(8,128)(2,1)} %bitcast.381), calls=%async_computation.10 | async-start | bytes 1048576 | tf_op jit(solution)/shard_map/all_to_all | solution.py:175
  749.4 84.8 %collective-permute-start.51 = (bf16[640,1024]{1,0:T(8,128)(2,1)S(1)}, bf16[640,1024]{1,0:T(8,128)(2,1)}, u32[]{:S(2)}, u32[]{:S(2)}) collective-permute-start(bf16[640,1024]{1,0:T(8,128)(2,1)S(1)} %convolution_convert_fusion.7), channel_id=1, source_target_pairs={{0,16},{8,24},{16,0},{24,8},{1,17},{9,25},{17,1},{25,9},{2,18},{10... | collective-permute-start | bytes 3932168 | tf_op jit(solution)/shard_map/ppermute | solution.py:309
  759.5 92.2 %collective-permute-start.49 = (bf16[320,1024]{1,0:T(8,128)(2,1)S(1)}, bf16[320,1024]{1,0:T(8,128)(2,1)}, u32[]{:S(2)}, u32[]{:S(2)}) collective-permute-start(bf16[320,1024]{1,0:T(8,128)(2,1)S(1)} %slice.413), channel_id=1, source_target_pairs={{0,16},{8,24},{16,0},{24,8},{1,17},{9,25},{17,1},{25,9},{2,18},{10... | collective-permute-start | bytes 1966088 | tf_op jit(solution)/shard_map/ppermute | solution.py:309
  886.7 232.4 %reduce-scatter.14.cloned.1.call-start = ((), (), s32[]{:S(2)}) async-start(), calls=%async_computation.27 | async-start | bytes 327680 | tf_op jit(solution)/shard_map/reduce_scatter | solution.py:165
  950.6 308.7 %reduce-scatter.26.cloned.1.call-start = ((), (), s32[]{:S(2)}) async-start(), calls=%async_computation.33 | async-start | bytes 6291456 | tf_op jit(solution)/shard_map/reduce_scatter | solution.py:322
  951.4 308.0 %reduce-scatter.24.cloned.1.call-start = ((), (), s32[]{:S(2)}) async-start(), calls=%async_computation.32 | async-start | bytes 6291456 | tf_op jit(solution)/shard_map/reduce_scatter | solution.py:322
  962.6 303.0 %reduce-scatter.22.cloned.1.call-start = ((), (), s32[]{:S(2)}) async-start(), calls=%async_computation.31 | async-start | bytes 6291456 | tf_op jit(solution)/shard_map/reduce_scatter | solution.py:322
  986.9 79.8 %collective-permute-start.63 = (bf16[4,2,2,32,4096]{4,3,2,1,0:T(8,128)(2,1)}, bf16[4,2,2,32,4096]{4,3,2,1,0:T(8,128)(2,1)}, u32[]{:S(2)}, u32[]{:S(2)}) collective-permute-start(bf16[4,2,2,32,4096]{4,3,2,1,0:T(8,128)(2,1)} %dynamic-slice_bitcast_fusion), channel_id=1, source_target_pairs={{0,1},{1,0},{2,3},{3,2},{4,5},{5,4},{6,7},{7,6},{8,9},{9,8},{10,11... | collective-permute-start | bytes 12582920 | tf_op jit(solution)/shard_map/ppermute | solution.py:50
  1015.4 250.1 %reduce-scatter.20.cloned.1.call-start = ((), (), s32[]{:S(2)}) async-start(), calls=%async_computation.30 | async-start | bytes 6291456 | tf_op jit(solution)/shard_map/reduce_scatter | solution.py:322
  1064.7 56.0 %collective-permute-start.66 = (bf16[4,2,128,1024]{3,2,1,0:T(8,128)(2,1)}, bf16[4,2,128,1024]{3,2,1,0:T(8,128)(2,1)}, u32[]{:S(2)}, u32[]{:S(2)}) collective-permute-start(bf16[4,2,128,1024]{3,2,1,0:T(8,128)(2,1)} %dynamic-slice_bitcast_fusion.2), channel_id=1, source_target_pairs={{0,2},{1,3},{2,0},{3,1},{4,6},{5,7},{6,4},{7,5},{8,10},{9,11},{10,... | collective-permute-start | bytes 6291464 | tf_op jit(solution)/shard_map/ppermute | solution.py:50
  1124.0 55.7 %all-to-all-start.11 = ((bf16[4,256,768]{1,2,0:T(8,128)(2,1)}), bf16[4,256,768]{1,2,0:T(8,128)(2,1)}, u32[]{:S(2)}, u32[]{:S(2)}) async-start(bf16[4,256,768]{1,2,0:T(8,128)(2,1)} %copy.58), calls=%async_computation.11 | async-start | bytes 3145728 | tf_op jit(solution)/shard_map/all_to_all | solution.py:175
  1128.3 150.6 %reduce-scatter.18.cloned.1.call-start = ((), (), s32[]{:S(2)}) async-start(), calls=%async_computation.29 | async-start | bytes 1310720 | tf_op jit(solution)/shard_map/reduce_scatter | solution.py:165
  1128.8 72.6 %collective-permute-start.67 = (bf16[4,128,1024]{2,1,0:T(8,128)(2,1)S(1)}, bf16[4,128,1024]{2,1,0:T(8,128)(2,1)}, u32[]{:S(2)}, u32[]{:S(2)}) collective-permute-start(bf16[4,128,1024]{2,1,0:T(8,128)(2,1)S(1)} %dynamic-slice_bitcast_fusion.6), channel_id=1, source_target_pairs={{0,4},{1,5},{2,6},{3,7},{4,0},{5,1},{6,2},{7,3},{8,12},{9,13},{10,... | collective-permute-start | bytes 3145736 | tf_op jit(solution)/shard_map/ppermute | solution.py:50
  1134.5 78.7 %collective-permute-start.65 = (bf16[4,32,4096]{2,1,0:T(8,128)(2,1)}, bf16[4,32,4096]{2,1,0:T(8,128)(2,1)}, u32[]{:S(2)}, u32[]{:S(2)}) collective-permute-start(bf16[4,32,4096]{2,1,0:T(8,128)(2,1)} %dynamic-slice_bitcast_fusion.7), channel_id=1, source_target_pairs={{0,2},{1,3},{2,0},{3,1},{4,6},{5,7},{6,4},{7,5},{8,10},{9,11},{10,... | collective-permute-start | bytes 3145736 | tf_op jit(solution)/shard_map/ppermute | solution.py:50
  1204.1 102.9 %reduce-scatter.16.cloned.1.call-start = ((), (), s32[]{:S(2)}) async-start(), calls=%async_computation.28 | async-start | bytes 1310720 | tf_op jit(solution)/shard_map/reduce_scatter | solution.py:165
  1215.6 112.9 %reduce-scatter.10.cloned.1.call-start = ((), (), s32[]{:S(2)}) async-start(), calls=%async_computation.25 | async-start | bytes 491520 | tf_op jit(solution)/shard_map/reduce_scatter | solution.py:165
  1249.6 100.7 %reduce-scatter.12.cloned.1.call-start = ((), (), s32[]{:S(2)}) async-start(), calls=%async_computation.26 | async-start | bytes 491520 | tf_op jit(solution)/shard_map/reduce_scatter | solution.py:165
  (253 other events, 4924.5 us)
Sparse Core Ops, SparseCore 0:
  9.6 40.9 all-gather.12
  52.2 28.1 all-gather.14
  81.9 56.0 all-gather.16
  139.5 106.4 all-gather.20
  247.4 60.7 all-gather.18
  309.6 116.1 all-gather.22
  950.8 18.1 reduce-scatter.13
  971.3 61.0 reduce-scatter.25
  1034.7 75.2 reduce-scatter.23
  1112.1 80.4 reduce-scatter.21
  1194.9 54.5 reduce-scatter.19
  1251.6 27.2 reduce-scatter.17
  1281.2 25.7 reduce-scatter.15
  1309.1 19.3 reduce-scatter.9
  1331.2 19.0 reduce-scatter.11

commit v6 on v5

--- a/solution.py
+++ b/solution.py
@@ -159,12 +159,18 @@
     return current
 
 
-def scatter_end(started):
+def scatter_middle(started):
     current, order, left = started
     current = scatter_bits(current, order, left)
-    return lax.psum_scatter(
-        current.reshape(-1, current.shape[-1]), "dp", scatter_dimension=0, tiled=True
-    ).astype(jnp.float32)
+    return current.reshape(-1, current.shape[-1])
+
+
+def scatter_dp(total):
+    return lax.psum_scatter(total, "dp", scatter_dimension=0, tiled=True).astype(jnp.float32)
+
+
+def scatter_end(started):
+    return scatter_dp(scatter_middle(started))
 
 
 def scatter_rows(total, order):
@@ -319,7 +325,15 @@
 
 
 def scatter_near(parts):
-    return lax.psum_scatter(parts, "dp", scatter_dimension=0, axis_index_groups=near_groups())
+    shape = parts.shape[1:]
+    total = lax.psum_scatter(
+        parts.reshape(-1, shape[-1]),
+        "dp",
+        scatter_dimension=0,
+        axis_index_groups=near_groups(),
+        tiled=True,
+    )
+    return total.reshape(shape)
 
 
 def both_rows(own):
@@ -485,12 +499,13 @@
 
     def grad_halves(lefts, rights, split_left):
         left, right = (jnp.concatenate(parts, 0) for parts in (lefts, rights))
-        return jnp.stack(
-            [
-                contract_rows(left[:, half] if split_left else left, right if split_left else right[:, half])
-                for half in hidden_halves
-            ]
-        ).astype(low)
+        return [
+            contract_rows(left[:, half] if split_left else left, right if split_left else right[:, half])
+            for half in hidden_halves
+        ]
+
+    def join_halves(down_parts, up_parts):
+        return jnp.stack([jnp.stack(parts) for parts in zip(down_parts, up_parts)]).astype(low)
 
     gain_ones = []
     third_stage = []
@@ -539,7 +554,8 @@
         after_grad = cotangent[micro, 0] + contract_rows(places[micro], grad_back)
         ffn_low = after_grad.astype(low)
         if micro == micro_count - 1:
-            ffn_low = after(ffn_low, up_sum[1])
+            ffn_low, layer_sums[1] = lax.optimization_barrier((ffn_low, layer_sums[1]))
+            ffn_low = after(ffn_low, *(terms[1] for terms in kept))
         hidden_grad = contract_cols(ffn_low, full_down)
         pre_grad = gelu_back(pre, hidden_grad).astype(low)
         normed2_grad = contract_cols(pre_grad, full_up)
@@ -559,14 +575,14 @@
             joined = [jnp.concatenate(parts, 0) for parts in zip(*kept_dense)]
             down_start = scatter_start(contract_rows(joined[2], joined[3]).astype(low), order_c)
             up_low = contract_rows(joined[0], joined[1]).astype(low)
-            mixed_grad = after(mixed_grad, down_start[0], up_low, down_sum[0])
+            mixed_grad = after(mixed_grad, down_start[0], up_low)
             late.extend((down_start, up_low))
         whole_grad = attend_back(whole, mixed_grad, prefix[micro], block)
         whole_grads.append(whole_grad)
         qkv_grad = swap_heads(whole_grad.reshape(dp_count, rows_dev, 3 * mine))
         qkv_grad = qkv_grad.transpose(1, 0, 2).reshape(rows_dev, 3 * width)
         if micro == micro_count - 1:
-            qkv_grad = after(qkv_grad, up_sum[0])
+            qkv_grad, layer_sums[0] = lax.optimization_barrier((qkv_grad, layer_sums[0]))
         normed_grad = contract_cols(qkv_grad, full_qkv)
         input_part, gain1_grad = norm_back(inputs, gains[0], normed_grad)
         input_grads.append(resid_grad + input_part)
@@ -584,33 +600,45 @@
             run_second(micro, *(resid_grads[-1][1:2] if micro else ()))
     for micro in micros[:-1]:
         run_attend_back(micro)
-    up_grads, down_grads = ([None, None], [None, None])
+    layer_grads, layer_sums = ([None, None], [None, None])
     by_stage = list(zip(*second_stage))
-    down_grads[1] = grad_halves(by_stage[5], by_stage[6], True)
-    up_grads[1] = grad_halves(by_stage[4], by_stage[7], False)
-    run_third(last, up_grads[1], down_grads[1], *whole_grads)
+    layer_grads[1] = join_halves(
+        grad_halves(by_stage[5], by_stage[6], True), grad_halves(by_stage[4], by_stage[7], False)
+    )
+    run_third(last, layer_grads[1], *whole_grads)
     by_first, by_third = (list(zip(*first_stage)), list(zip(*third_stage)))
-    down_grads[0] = grad_halves(by_first[4], by_third[1], True)
-    up_grads[0] = grad_halves(by_first[2], by_third[2], False)
-    down_sum, up_sum = ([None, None], [None, None])
+    layer_grads[0] = join_halves(
+        grad_halves(by_first[4], by_third[1], True), grad_halves(by_first[2], by_third[2], False)
+    )
     for layer in (1, 0):
-        down_sum[layer] = scatter_near(down_grads[layer]).astype(f32)
-        up_sum[layer] = scatter_near(up_grads[layer]).astype(f32)
-    run_own(last, down_sum[1])
+        layer_sums[layer] = scatter_near(layer_grads[layer])
+    run_own(last)
     run_ffn_back(last)
     run_attend_back(last)
     down_start, up_low = late
+    down_sum, up_sum = ([total[i].astype(f32) for total in layer_sums] for i in range(2))
     gain_acc, gain_one = (sum(gain_sums), sum(gain_ones))
     joined = [jnp.concatenate(parts, 0) for parts in zip(*kept)]
     down_out = scatter_end(down_start)
     up_out = scatter_rows(up_low, order_d)
-    mix_out = scatter_rows(contract_rows(joined[2], joined[3]).astype(low), order_d)
+    mix_low = contract_rows(joined[2], joined[3]).astype(low)
     qkv_low = contract_rows(joined[0], joined[1]).astype(low)
-    qkv_out = jnp.concatenate(
-        [scatter_rows(qkv_low[:, :half], order_c), scatter_rows(qkv_low[:, half:], order_d)], 1
-    )
+    qkv_mix = scatter_dp(
+        jnp.concatenate(
+            [
+                scatter_middle(scatter_start(part, order))
+                for part, order in (
+                    (qkv_low[:, :half], order_c),
+                    (qkv_low[:, half:], order_d),
+                    (mix_low, order_d),
+                )
+            ],
+            1,
+        )
+    )
+    mix_out = qkv_mix[:, 3 * width :]
     qkv_out = (
-        qkv_out.reshape(rows_qkv, dp_count, 3, mine)
+        qkv_mix[:, : 3 * width].reshape(rows_qkv, dp_count, 3, mine)
         .transpose(0, 2, 1, 3)
         .reshape(rows_qkv, 3 * width)
     )

time: 1370 us -> 1330 us (0.971)
  waiting for transfers between devices: 570 us -> 535 us
  matrix products: 253 us -> 237 us
    reduce_scatter x9 -> x5, waiting for transfers between devices: 75 us -> 21 us  [the longest x3 21 us: scatter_dp(): lax.psum_scatter(total, 'dp', scatter_dimension=0, tiled=True)]
    all_to_all x8, waiting for transfers between devices: 110 us -> 133 us  [swap_heads(): return lax.all_to_all(blocks, 'dp', split_axis=0, concat_axis=0, tiled=True)]
    ppermute x12, waiting for transfers between devices: 200 us -> 223 us  [flip(): return lax.ppermute(values, 'dp', [(i, i ^ bit) for i in range(count)])]
    another operation x8 -> x10, other arithmetic: 10.7 us -> 25.9 us  [the longest x6 24.6 us: join_halves(): jnp.stack([jnp.stack(parts) for parts in zip(down_parts, up_parts)])]
    ppermute x12, waiting for transfers between devices: 32.8 us -> 18.5 us  [turn(): lax.ppermute(values, 'dp', [(i, (i + shift) % count) for i in range(count)])]
    unnamed x355 -> x391, local copies, waits for them, and re-layouts: 33.3 us -> 34.5 us
  transfers between devices with their start and end apart: 108 -> 104, of which waited for: 38 -> 34; matrix products, arithmetic and copies ran while one was open for 28% -> 33% of each run, Pallas kernels for 8% -> 8%
where the time goes in v6:
time: 1330 us; the launch traced here: 1320 us
  waiting for transfers between devices  535 us (40%)
  matrix products  237 us (18%)
  starting transfers between devices  156 us (12%)
  other arithmetic  151 us (11%)
  local copies, waits for them, and re-layouts  119 us (9%)
  Pallas kernels  102 us (8%)
  between operations  17.4 us (1%)
    ppermute x12, waiting for transfers between devices, flip(): return lax.ppermute(values, 'dp', [(i, i ^ bit) for i in range(count)])  223 us
    all_to_all x8, waiting for transfers between devices, swap_heads(): return lax.all_to_all(blocks, 'dp', split_axis=0, concat_axis=0, tiled=True)  133 us
    dot_general x16, matrix products, contract_cols(): lax.dot_general(left, right, (((1,), (1,)), ((), ())), preferred_element_...  88.9 us
    ppermute x53, waiting for transfers between devices, swap(): return lax.ppermute(values, 'expert', [(i, i ^ bit) for i in range(count)])  66.4 us
    dot_general x16, matrix products, contract_rows(): lax.dot_general(left, right, (((0,), (0,)), ((), ())), preferred_element_...  57.6 us
    pallas_call x2, Pallas kernels, attend_back(): pl.pallas_call(attend_back_kernel, out_shape=jax.ShapeDtypeStruct((length...  49.6 us
    all_to_all x8, starting transfers between devices, swap_heads(): return lax.all_to_all(blocks, 'dp', split_axis=0, concat_axis=0, tiled=True)  38.9 us
    all_gather x4, waiting for transfers between devices, gather_near(): return lax.all_gather(shard, 'dp', axis=0, axis_index_groups=near_groups())  37.2 us
  transfers between devices with their start and end apart: 104, of which 34 were waited for; matrix products, arithmetic and copies ran while one was open for 33% of the time, Pallas kernels for 8%

profile of v6, /device:TPU:0, one launch (start us, length us, event | category | flops | bytes accessed | tf_op | source)
XLA Modules:
  0.0 1317.8 jit_solution(5400235172738175866)
XLA Ops:
  22.2 15.6 %collective-permute-done.1 = bf16[32,3200]{1,0:T(8,128)(2,1)S(1)} collective-permute-done((bf16[32,3200]{1,0:T(8,128)(2,1)S(1)}, bf16[32,3200]{1,0:T(8,128)(2,1)S(1)}, u32[]{:S(2)}, u32[]{:S(2)}) %collective-permute-start.1) | collective-permute-done | bytes 204832 | tf_op jit(solution)/shard_map/ppermute | solution.py:55
  38.6 13.5 %collective-permute-start.17 = (bf16[32,1024]{1,0:T(8,128)(2,1)S(1)}, bf16[32,1024]{1,0:T(8,128)(2,1)S(1)}, u32[]{:S(2)}, u32[]{:S(2)}) collective-permute-start(bf16[32,1024]{1,0:T(8,128)(2,1)S(1)} %copy-done.117), channel_id=1, source_target_pairs={{0,8},{8,16},{16,24},{24,0},{1,9},{9,17},{17,25},{25,1},{2,10},{10... | collective-permute-start | bytes 196616 | tf_op jit(solution)/shard_map/ppermute | solution.py:55
  73.6 7.4 collective-permute-done.4
  129.3 26.0 %collective-permute-done.26.refs_1_ = bf16[4,32,1024]{2,1,0:T(8,128)(2,1)} collective-permute-done((bf16[4,32,1024]{2,1,0:T(8,128)(2,1)S(1)}, bf16[4,32,1024]{2,1,0:T(8,128)(2,1)}, u32[]{:S(2)}, u32[]{:S(2)}) %collective-permute-start.26) | collective-permute-done | bytes 262176 | tf_op jit(solution)/shard_map/ppermute | solution.py:50
  172.8 15.2 %attend.2 = bf16[1024,256]{1,0:T(8,128)(2,1)} custom-call(s32[1]{0:T(128)} %bitcast.1.prefix_ref, bf16[1024,768]{1,0:T(8,128)(2,1)} %bitcast.17.x_ref), custom_call_target="tpu_custom_call" | custom-call | flops 1073741824 | bytes 3145728 | tf_op jit(solution)/shard_map/attend/pallas_call | solution.py:232
  204.4 37.0 %collective-permute-done.46 = bf16[320,1024]{1,0:T(8,128)(2,1)} collective-permute-done((bf16[320,1024]{1,0:T(8,128)(2,1)S(1)}, bf16[320,1024]{1,0:T(8,128)(2,1)}, u32[]{:S(2)}, u32[]{:S(2)}) %collective-permute-start.46) | collective-permute-done | bytes 655392 | tf_op jit(solution)/shard_map/ppermute | solution.py:315
  270.1 9.1 multiply_convert_fusion.5
  286.6 7.1 multiply_reduce_fusion.13
  322.3 28.1 %collective-permute-done.41 = bf16[320,1024]{1,0:T(8,128)(2,1)S(1)} collective-permute-done((bf16[320,1024]{1,0:T(8,128)(2,1)S(1)}, bf16[320,1024]{1,0:T(8,128)(2,1)S(1)}, u32[]{:S(2)}, u32[]{:S(2)}) %collective-permute-start.41) | collective-permute-done | bytes 655392 | tf_op jit(solution)/shard_map/ppermute | solution.py:315
  376.9 14.9 %attend.3 = bf16[1024,256]{1,0:T(8,128)(2,1)} custom-call(s32[1]{0:T(128)} %bitcast.36.prefix_ref, bf16[1024,768]{1,0:T(8,128)(2,1)} %bitcast.458), custom_call_target="tpu_custom_call" | custom-call | flops 1073741824 | bytes 3145728 | tf_op jit(solution)/shard_map/attend/pallas_call | solution.py:232
  400.0 37.1 %all-gather.23.cloned.1.call-done = bf16[2048,1024]{1,0:T(8,128)(2,1)} async-done(((bf16[1024,1024]{1,0:T(8,128)(2,1)}), bf16[2048,1024]{1,0:T(8,128)(2,1)}) %all-gather.23.cloned.1.call-update) | async-done | bytes 4194320 | tf_op jit(solution)/shard_map/all_gather | solution.py:324
  437.1 7.8 fusion.237
  455.5 10.0 multiply_convert_fusion.2
  505.9 79.7 %collective-permute-done.44 = bf16[320,1024]{1,0:T(8,128)(2,1)} collective-permute-done((bf16[320,1024]{1,0:T(8,128)(2,1)}, bf16[320,1024]{1,0:T(8,128)(2,1)}, u32[]{:S(2)}, u32[]{:S(2)}) %collective-permute-start.44) | collective-permute-done | bytes 655392 | tf_op jit(solution)/shard_map/ppermute | solution.py:315
  622.5 52.3 %collective-permute-done.48 = bf16[320,1024]{1,0:T(8,128)(2,1)S(1)} collective-permute-done((bf16[320,1024]{1,0:T(8,128)(2,1)S(1)}, bf16[320,1024]{1,0:T(8,128)(2,1)S(1)}, u32[]{:S(2)}, u32[]{:S(2)}) %collective-permute-start.48) | collective-permute-done | bytes 655392 | tf_op jit(solution)/shard_map/ppermute | solution.py:315
  686.7 8.0 all-to-all-done.8
  696.3 12.0 fusion.36
  708.4 7.3 multiply_reduce_fusion.17
  751.4 7.5 pad_maximum_fusion
  781.3 20.8 %collective-permute-done.49 = bf16[320,1024]{1,0:T(8,128)(2,1)} collective-permute-done((bf16[320,1024]{1,0:T(8,128)(2,1)}, bf16[320,1024]{1,0:T(8,128)(2,1)}, u32[]{:S(2)}, u32[]{:S(2)}) %collective-permute-start.49) | collective-permute-done | bytes 655392 | tf_op jit(solution)/shard_map/ppermute | solution.py:315
  805.4 65.2 %all-to-all-done.10 = bf16[4,256,256]{2,1,0:T(8,128)(2,1)S(1)} async-done(((bf16[4,256,256]{2,1,0:T(8,128)(2,1)}), bf16[4,256,256]{2,1,0:T(8,128)(2,1)S(1)}, u32[]{:S(2)}, u32[]{:S(2)}) %all-to-all-start.10) | async-done | bytes 524320 | tf_op jit(solution)/shard_map/all_to_all | solution.py:181
  875.0 25.0 %attend_back.2 = bf16[1024,768]{1,0:T(8,128)(2,1)} custom-call(s32[1]{0:T(128)} %bitcast.1.prefix_ref, bf16[1024,768]{1,0:T(8,128)(2,1)} %bitcast.17.x_ref, bf16[1024,256]{1,0:T(8,128)(2,1)} %bitcast.477), custom_call_target="tpu_custom_call" | custom-call | flops 2684354560 | bytes 7864320 | tf_op jit(solution)/shard_map/attend_back/pallas_call | solution.py:290
  938.0 7.6 pad_maximum_fusion.1
  960.7 7.7 all-to-all-done.9
  974.7 8.3 all-to-all-done.13
  998.8 40.3 %all-to-all-done.11 = bf16[4,256,768]{1,2,0:T(8,128)(2,1)} async-done(((bf16[4,256,768]{1,2,0:T(8,128)(2,1)}), bf16[4,256,768]{1,2,0:T(8,128)(2,1)}, u32[]{:S(2)}, u32[]{:S(2)}) %all-to-all-start.11) | async-done | bytes 1572896 | tf_op jit(solution)/shard_map/all_to_all | solution.py:181
  1052.0 11.5 fusion.43
  1063.5 7.3 convolution_convert_fusion
  1131.5 24.6 %attend_back.3 = bf16[1024,768]{1,0:T(8,128)(2,1)} custom-call(s32[1]{0:T(128)} %bitcast.36.prefix_ref, bf16[1024,768]{1,0:T(8,128)(2,1)} %bitcast.459, bf16[1024,256]{1,0:T(8,128)(2,1)} %bitcast.86.grad_ref), custom_call_target="tpu_custom_call" | custom-call | flops 2684354560 | bytes 7864320 | tf_op jit(solution)/shard_map/attend_back/pallas_call | solution.py:290
  1179.1 19.3 %all-to-all-done.15 = bf16[4,256,768]{1,2,0:T(8,128)(2,1)} async-done(((bf16[4,256,768]{1,2,0:T(8,128)(2,1)}), bf16[4,256,768]{1,2,0:T(8,128)(2,1)}, u32[]{:S(2)}, u32[]{:S(2)}) %all-to-all-start.15) | async-done | bytes 1572896 | tf_op jit(solution)/shard_map/all_to_all | solution.py:181
  1240.7 11.1 collective-permute-done.55
  1287.0 21.0 %reduce-scatter.10.cloned.1.call-done = bf16[32,4096]{1,0:T(8,128)(2,1)} async-done(((bf16[128,4096]{1,0:T(8,128)(2,1)}), bf16[32,4096]{1,0:T(8,128)(2,1)}) %reduce-scatter.10.cloned.1.call-update) | async-done | bytes 262160 | tf_op jit(solution)/shard_map/reduce_scatter | solution.py:169
  (904 shorter events, 635.3 us)
Async XLA Ops:
  7.2 117.1 %all-gather.13.cloned.1.call-start = ((), (), s32[]{:S(2)}) async-start(), calls=%async_computation.26 | async-start | bytes 1310720 | tf_op jit(solution)/shard_map/all_gather | solution.py:126
  7.9 118.0 %all-gather.15.cloned.1.call-start = ((), (), s32[]{:S(2)}) async-start(), calls=%async_computation.27 | async-start | bytes 1310720 | tf_op jit(solution)/shard_map/all_gather | solution.py:126
  17.2 281.5 %all-gather.17.cloned.1.call-start = ((), (), s32[]{:S(2)}) async-start(), calls=%async_computation.28 | async-start | bytes 6291456 | tf_op jit(solution)/shard_map/all_gather | solution.py:324
  37.9 265.4 %all-gather.21.cloned.1.call-start = ((), (), s32[]{:S(2)}) async-start(), calls=%async_computation.30 | async-start | bytes 6291456 | tf_op jit(solution)/shard_map/all_gather | solution.py:324
  38.5 320.4 %all-gather.19.cloned.1.call-start = ((), (), s32[]{:S(2)}) async-start(), calls=%async_computation.29 | async-start | bytes 6291456 | tf_op jit(solution)/shard_map/all_gather | solution.py:324
  166.5 74.8 %collective-permute-start.22 = (bf16[4,32,4096]{2,1,0:T(8,128)(2,1)}, bf16[4,32,4096]{2,1,0:T(8,128)(2,1)}, u32[]{:S(2)}, u32[]{:S(2)}) collective-permute-start(bf16[4,32,4096]{2,1,0:T(8,128)(2,1)} %bitcast.467), channel_id=1, source_target_pairs={{0,2},{1,3},{2,0},{3,1},{4,6},{5,7},{6,4},{7,5},{8,10},{9,11},{10,... | collective-permute-start | bytes 3145736 | tf_op jit(solution)/shard_map/ppermute | solution.py:50
  168.2 73.7 %collective-permute-start.24 = (bf16[4,128,1024]{2,1,0:T(8,128)(2,1)}, bf16[4,128,1024]{2,1,0:T(8,128)(2,1)}, u32[]{:S(2)}, u32[]{:S(2)}) collective-permute-start(bf16[4,128,1024]{2,1,0:T(8,128)(2,1)} %bitcast.471), channel_id=1, source_target_pairs={{0,4},{1,5},{2,6},{3,7},{4,0},{5,1},{6,2},{7,3},{8,12},{9,13},{10,... | collective-permute-start | bytes 3145736 | tf_op jit(solution)/shard_map/ppermute | solution.py:50
  170.5 78.6 %collective-permute-start.23 = (bf16[4,32,4096]{2,1,0:T(8,128)(2,1)}, bf16[4,32,4096]{2,1,0:T(8,128)(2,1)}, u32[]{:S(2)}, u32[]{:S(2)}) collective-permute-start(bf16[4,32,4096]{2,1,0:T(8,128)(2,1)} %collective-permute-done.20.refs_1_), channel_id=1, source_target_pairs={{0,2},{1,3},{2,0},{3,1},{4,6},{5,7},{6,4},{7,5},{8,10},{9,11},{10,... | collective-permute-start | bytes 3145736 | tf_op jit(solution)/shard_map/ppermute | solution.py:50
  171.1 78.5 %collective-permute-start.25 = (bf16[4,128,1024]{2,1,0:T(8,128)(2,1)}, bf16[4,128,1024]{2,1,0:T(8,128)(2,1)}, u32[]{:S(2)}, u32[]{:S(2)}) collective-permute-start(bf16[4,128,1024]{2,1,0:T(8,128)(2,1)} %collective-permute-done.21.refs_1_), channel_id=1, source_target_pairs={{0,4},{1,5},{2,6},{3,7},{4,0},{5,1},{6,2},{7,3},{8,12},{9,13},{10,... | collective-permute-start | bytes 3145736 | tf_op jit(solution)/shard_map/ppermute | solution.py:50
  190.1 54.8 %all-to-all-start.1 = ((bf16[4,256,256]{1,2,0:T(8,128)(2,1)}), bf16[4,256,256]{1,2,0:T(8,128)(2,1)}, u32[]{:S(2)}, u32[]{:S(2)}) async-start(bf16[4,256,256]{1,2,0:T(8,128)(2,1)} %copy.55), calls=%async_computation.1 | async-start | bytes 1048576 | tf_op jit(solution)/shard_map/all_to_all | solution.py:181
  195.7 241.4 %all-gather.23.cloned.1.call-start = ((), (), s32[]{:S(2)}) async-start(), calls=%async_computation.31 | async-start | bytes 6291456 | tf_op jit(solution)/shard_map/all_gather | solution.py:324
  260.2 423.9 %collective-permute-start.50 = (bf16[320,1024]{1,0:T(8,128)(2,1)}, bf16[320,1024]{1,0:T(8,128)(2,1)}, u32[]{:S(2)}, u32[]{:S(2)}) collective-permute-start(bf16[320,1024]{1,0:T(8,128)(2,1)} %bitcast.73), channel_id=1, source_target_pairs={{0,16},{8,24},{16,0},{24,8},{1,17},{9,25},{17,1},{25,9},{2,18},{10... | collective-permute-start | bytes 1966088 | tf_op jit(solution)/shard_map/ppermute | solution.py:315
  316.6 59.1 %all-to-all-start.3 = ((bf16[4,256,768]{2,1,0:T(8,128)(2,1)}), bf16[4,256,768]{2,1,0:T(8,128)(2,1)S(1)}, u32[]{:S(2)}, u32[]{:S(2)}) async-start(bf16[4,256,768]{2,1,0:T(8,128)(2,1)} %bitcast.387), calls=%async_computation.3 | async-start | bytes 3145728 | tf_op jit(solution)/shard_map/all_to_all | solution.py:181
  365.9 79.0 %collective-permute-start.42 = (bf16[640,1024]{1,0:T(8,128)(2,1)}, bf16[640,1024]{1,0:T(8,128)(2,1)}, u32[]{:S(2)}, u32[]{:S(2)}) collective-permute-start(bf16[640,1024]{1,0:T(8,128)(2,1)} %convolution_convert_fusion.13), channel_id=1, source_target_pairs={{0,16},{8,24},{16,0},{24,8},{1,17},{9,25},{17,1},{25,9},{2,18},{10... | collective-permute-start | bytes 3932168 | tf_op jit(solution)/shard_map/ppermute | solution.py:315
  393.9 55.7 %all-to-all-start.4 = ((bf16[4,256,256]{1,2,0:T(8,128)(2,1)}), bf16[4,256,256]{1,2,0:T(8,128)(2,1)}, u32[]{:S(2)}, u32[]{:S(2)}) async-start(bf16[4,256,256]{1,2,0:T(8,128)(2,1)} %copy.57), calls=%async_computation.4 | async-start | bytes 1048576 | tf_op jit(solution)/shard_map/all_to_all | solution.py:181
  495.6 99.5 %collective-permute-start.47 = (bf16[640,1024]{1,0:T(8,128)(2,1)}, bf16[640,1024]{1,0:T(8,128)(2,1)}, u32[]{:S(2)}, u32[]{:S(2)}) collective-permute-start(bf16[640,1024]{1,0:T(8,128)(2,1)} %convolution_convert_fusion.10), channel_id=1, source_target_pairs={{0,16},{8,24},{16,0},{24,8},{1,17},{9,25},{17,1},{25,9},{2,18},{10... | collective-permute-start | bytes 3932168 | tf_op jit(solution)/shard_map/ppermute | solution.py:315
  499.7 85.8 %collective-permute-start.44 = (bf16[320,1024]{1,0:T(8,128)(2,1)}, bf16[320,1024]{1,0:T(8,128)(2,1)}, u32[]{:S(2)}, u32[]{:S(2)}) collective-permute-start(bf16[320,1024]{1,0:T(8,128)(2,1)} %bitcast.54), channel_id=1, source_target_pairs={{0,16},{8,24},{16,0},{24,8},{1,17},{9,25},{17,1},{25,9},{2,18},{10... | collective-permute-start | bytes 1966088 | tf_op jit(solution)/shard_map/ppermute | solution.py:315
  615.5 59.2 %collective-permute-start.48 = (bf16[320,1024]{1,0:T(8,128)(2,1)S(1)}, bf16[320,1024]{1,0:T(8,128)(2,1)S(1)}, u32[]{:S(2)}, u32[]{:S(2)}) collective-permute-start(bf16[320,1024]{1,0:T(8,128)(2,1)S(1)} %slice.433), channel_id=1, source_target_pairs={{0,16},{8,24},{16,0},{24,8},{1,17},{9,25},{17,1},{25,9},{2,18},{10... | collective-permute-start | bytes 1966088 | tf_op jit(solution)/shard_map/ppermute | solution.py:315
  619.6 96.7 %collective-permute-start.45 = (bf16[640,1024]{1,0:T(8,128)(2,1)}, bf16[640,1024]{1,0:T(8,128)(2,1)}, u32[]{:S(2)}, u32[]{:S(2)}) collective-permute-start(bf16[640,1024]{1,0:T(8,128)(2,1)} %convolution_convert_fusion.11), channel_id=1, source_target_pairs={{0,16},{8,24},{16,0},{24,8},{1,17},{9,25},{17,1},{25,9},{2,18},{10... | collective-permute-start | bytes 3932168 | tf_op jit(solution)/shard_map/ppermute | solution.py:315
  683.6 315.2 %reduce-scatter.6.cloned.1.call-start = ((), (), s32[]{:S(2)}) async-start(), calls=%async_computation.21 | async-start | bytes 12582912 | tf_op jit(solution)/shard_map/reduce_scatter | solution.py:329
  773.2 126.7 %collective-permute-start.51 = (bf16[640,1024]{1,0:T(8,128)(2,1)}, bf16[640,1024]{1,0:T(8,128)(2,1)S(1)}, u32[]{:S(2)}, u32[]{:S(2)}) collective-permute-start(bf16[640,1024]{1,0:T(8,128)(2,1)} %convolution_convert_fusion.7), channel_id=1, source_target_pairs={{0,16},{8,24},{16,0},{24,8},{1,17},{9,25},{17,1},{25,9},{2,18},{10... | collective-permute-start | bytes 3932168 | tf_op jit(solution)/shard_map/ppermute | solution.py:315
  777.7 92.9 %all-to-all-start.10 = ((bf16[4,256,256]{2,1,0:T(8,128)(2,1)}), bf16[4,256,256]{2,1,0:T(8,128)(2,1)S(1)}, u32[]{:S(2)}, u32[]{:S(2)}) async-start(bf16[4,256,256]{2,1,0:T(8,128)(2,1)} %bitcast.393), calls=%async_computation.10 | async-start | bytes 1048576 | tf_op jit(solution)/shard_map/all_to_all | solution.py:181
  871.4 81.7 %all-to-all-start.5 = ((bf16[8,40,1024]{2,1,0:T(8,128)(2,1)}), bf16[8,40,1024]{2,1,0:T(8,128)(2,1)S(1)}, u32[]{:S(2)}, u32[]{:S(2)}) async-start(bf16[8,40,1024]{2,1,0:T(8,128)(2,1)} %bitcast.44), calls=%async_computation.5 | async-start | bytes 1310720 | tf_op jit(solution)/shard_map/all_to_all | solution.py:187
  874.9 304.2 %reduce-scatter.8.cloned.1.call-start = ((), (), s32[]{:S(2)}) async-start(), calls=%async_computation.22 | async-start | bytes 12582912 | tf_op jit(solution)/shard_map/reduce_scatter | solution.py:329
  983.8 55.3 %all-to-all-start.11 = ((bf16[4,256,768]{1,2,0:T(8,128)(2,1)}), bf16[4,256,768]{1,2,0:T(8,128)(2,1)}, u32[]{:S(2)}, u32[]{:S(2)}) async-start(bf16[4,256,768]{1,2,0:T(8,128)(2,1)} %copy.59), calls=%async_computation.11 | async-start | bytes 3145728 | tf_op jit(solution)/shard_map/all_to_all | solution.py:181
  1052.0 57.8 %collective-permute-start.53 = (bf16[4,2,2,128,1024]{4,3,2,1,0:T(8,128)(2,1)}, bf16[4,2,2,128,1024]{4,3,2,1,0:T(8,128)(2,1)}, u32[]{:S(2)}, u32[]{:S(2)}) collective-permute-start(bf16[4,2,2,128,1024]{4,3,2,1,0:T(8,128)(2,1)} %dynamic-slice_bitcast_fusion.1), channel_id=1, source_target_pairs={{0,1},{1,0},{2,3},{3,2},{4,5},{5,4},{6,7},{7,6},{8,9},{9,8},{10,11... | collective-permute-start | bytes 12582920 | tf_op jit(solution)/shard_map/ppermute | solution.py:50
  1117.9 51.6 %collective-permute-start.66 = (bf16[4,2,128,1024]{3,2,1,0:T(8,128)(2,1)}, bf16[4,2,128,1024]{3,2,1,0:T(8,128)(2,1)S(1)}, u32[]{:S(2)}, u32[]{:S(2)}) collective-permute-start(bf16[4,2,128,1024]{3,2,1,0:T(8,128)(2,1)} %dynamic-slice_bitcast_fusion.2), channel_id=1, source_target_pairs={{0,2},{1,3},{2,0},{3,1},{4,6},{5,7},{6,4},{7,5},{8,10},{9,11},{10,... | collective-permute-start | bytes 6291464 | tf_op jit(solution)/shard_map/ppermute | solution.py:50
  1163.8 119.6 %reduce-scatter.14.cloned.1.call-start = ((), (), s32[]{:S(2)}) async-start(), calls=%async_computation.25 | async-start | bytes 1310720 | tf_op jit(solution)/shard_map/reduce_scatter | solution.py:169
  1177.7 59.8 %collective-permute-start.65 = (bf16[4,32,4096]{2,1,0:T(8,128)(2,1)}, bf16[4,32,4096]{2,1,0:T(8,128)(2,1)}, u32[]{:S(2)}, u32[]{:S(2)}) collective-permute-start(bf16[4,32,4096]{2,1,0:T(8,128)(2,1)} %dynamic-slice_bitcast_fusion.7), channel_id=1, source_target_pairs={{0,2},{1,3},{2,0},{3,1},{4,6},{5,7},{6,4},{7,5},{8,10},{9,11},{10,... | collective-permute-start | bytes 3145736 | tf_op jit(solution)/shard_map/ppermute | solution.py:50
  1220.7 51.4 %collective-permute-start.68 = (f32[2,1024]{1,0:T(2,128)S(1)}, f32[2,1024]{1,0:T(2,128)S(1)}, u32[]{:S(2)}, u32[]{:S(2)}) collective-permute-start(f32[2,1024]{1,0:T(2,128)S(1)} %maximum_add_fusion), channel_id=1, source_target_pairs={{0,8},{8,16},{16,24},{24,0},{1,9},{9,17},{17,25},{25,1},{2,10},{10... | collective-permute-start | bytes 24584 | tf_op jit(solution)/shard_map/ppermute | solution.py:55
  1225.5 59.8 %reduce-scatter.12.cloned.1.call-start = ((), (), s32[]{:S(2)}) async-start(), calls=%async_computation.24 | async-start | bytes 1310720 | tf_op jit(solution)/shard_map/reduce_scatter | solution.py:169
  1240.6 67.4 %reduce-scatter.10.cloned.1.call-start = ((), (), s32[]{:S(2)}) async-start(), calls=%async_computation.23 | async-start | bytes 1310720 | tf_op jit(solution)/shard_map/reduce_scatter | solution.py:169
  (268 other events, 5379.2 us)
Sparse Core Ops, SparseCore 0:
  9.6 40.9 all-gather.12
  52.2 28.1 all-gather.14
  81.9 81.3 all-gather.16
  164.7 79.1 all-gather.20
  245.3 76.2 all-gather.18
  323.0 114.0 all-gather.22
  759.0 147.0 reduce-scatter.5
  945.8 124.0 reduce-scatter.7
  1225.6 26.3 reduce-scatter.13
  1254.1 25.7 reduce-scatter.11
  1282.2 25.7 reduce-scatter.9

commit v7 on v6

--- a/solution.py
+++ b/solution.py
@@ -605,14 +605,14 @@
     layer_grads[1] = join_halves(
         grad_halves(by_stage[5], by_stage[6], True), grad_halves(by_stage[4], by_stage[7], False)
     )
-    run_third(last, layer_grads[1], *whole_grads)
+    run_third(last, layer_grads[1])
     by_first, by_third = (list(zip(*first_stage)), list(zip(*third_stage)))
     layer_grads[0] = join_halves(
         grad_halves(by_first[4], by_third[1], True), grad_halves(by_first[2], by_third[2], False)
     )
     for layer in (1, 0):
         layer_sums[layer] = scatter_near(layer_grads[layer])
-    run_own(last)
+    run_own(last, *whole_grads)
     run_ffn_back(last)
     run_attend_back(last)
     down_start, up_low = late

time: 1330 us -> 1330 us (level)
  no operation moved by 1% of the time
where the time goes in v7:
time: 1330 us; the launch traced here: 1320 us
  waiting for transfers between devices  535 us (40%)
  matrix products  237 us (18%)
  starting transfers between devices  156 us (12%)
  other arithmetic  151 us (11%)
  local copies, waits for them, and re-layouts  119 us (9%)
  Pallas kernels  102 us (8%)
  between operations  17.4 us (1%)
    ppermute x12, waiting for transfers between devices, flip(): return lax.ppermute(values, 'dp', [(i, i ^ bit) for i in range(count)])  223 us
    all_to_all x8, waiting for transfers between devices, swap_heads(): return lax.all_to_all(blocks, 'dp', split_axis=0, concat_axis=0, tiled=True)  133 us
    dot_general x16, matrix products, contract_cols(): lax.dot_general(left, right, (((1,), (1,)), ((), ())), preferred_element_...  88.9 us
    ppermute x53, waiting for transfers between devices, swap(): return lax.ppermute(values, 'expert', [(i, i ^ bit) for i in range(count)])  66.4 us
    dot_general x16, matrix products, contract_rows(): lax.dot_general(left, right, (((0,), (0,)), ((), ())), preferred_element_...  57.6 us
    pallas_call x2, Pallas kernels, attend_back(): pl.pallas_call(attend_back_kernel, out_shape=jax.ShapeDtypeStruct((length...  49.6 us
    all_to_all x8, starting transfers between devices, swap_heads(): return lax.all_to_all(blocks, 'dp', split_axis=0, concat_axis=0, tiled=True)  38.9 us
    all_gather x4, waiting for transfers between devices, gather_near(): return lax.all_gather(shard, 'dp', axis=0, axis_index_groups=near_groups())  37.2 us
  transfers between devices with their start and end apart: 104, of which 34 were waited for; matrix products, arithmetic and copies ran while one was open for 33% of the time, Pallas kernels for 8%

profile of v7, /device:TPU:0, one launch (start us, length us, event | category | flops | bytes accessed | tf_op | source)
XLA Modules:
  0.0 1317.8 jit_solution(5400235172738175866)
XLA Ops:
  22.2 15.6 %collective-permute-done.1 = bf16[32,3200]{1,0:T(8,128)(2,1)S(1)} collective-permute-done((bf16[32,3200]{1,0:T(8,128)(2,1)S(1)}, bf16[32,3200]{1,0:T(8,128)(2,1)S(1)}, u32[]{:S(2)}, u32[]{:S(2)}) %collective-permute-start.1) | collective-permute-done | bytes 204832 | tf_op jit(solution)/shard_map/ppermute | solution.py:55
  38.6 13.5 %collective-permute-start.17 = (bf16[32,1024]{1,0:T(8,128)(2,1)S(1)}, bf16[32,1024]{1,0:T(8,128)(2,1)S(1)}, u32[]{:S(2)}, u32[]{:S(2)}) collective-permute-start(bf16[32,1024]{1,0:T(8,128)(2,1)S(1)} %copy-done.117), channel_id=1, source_target_pairs={{0,8},{8,16},{16,24},{24,0},{1,9},{9,17},{17,25},{25,1},{2,10},{10... | collective-permute-start | bytes 196616 | tf_op jit(solution)/shard_map/ppermute | solution.py:55
  73.6 7.4 collective-permute-done.4
  129.3 26.0 %collective-permute-done.26.refs_1_ = bf16[4,32,1024]{2,1,0:T(8,128)(2,1)} collective-permute-done((bf16[4,32,1024]{2,1,0:T(8,128)(2,1)S(1)}, bf16[4,32,1024]{2,1,0:T(8,128)(2,1)}, u32[]{:S(2)}, u32[]{:S(2)}) %collective-permute-start.26) | collective-permute-done | bytes 262176 | tf_op jit(solution)/shard_map/ppermute | solution.py:50
  172.8 15.2 %attend.2 = bf16[1024,256]{1,0:T(8,128)(2,1)} custom-call(s32[1]{0:T(128)} %bitcast.1.prefix_ref, bf16[1024,768]{1,0:T(8,128)(2,1)} %bitcast.17.x_ref), custom_call_target="tpu_custom_call" | custom-call | flops 1073741824 | bytes 3145728 | tf_op jit(solution)/shard_map/attend/pallas_call | solution.py:232
  204.4 37.0 %collective-permute-done.46 = bf16[320,1024]{1,0:T(8,128)(2,1)} collective-permute-done((bf16[320,1024]{1,0:T(8,128)(2,1)S(1)}, bf16[320,1024]{1,0:T(8,128)(2,1)}, u32[]{:S(2)}, u32[]{:S(2)}) %collective-permute-start.46) | collective-permute-done | bytes 655392 | tf_op jit(solution)/shard_map/ppermute | solution.py:315
  270.1 9.1 multiply_convert_fusion.5
  286.6 7.1 multiply_reduce_fusion.13
  322.3 28.1 %collective-permute-done.41 = bf16[320,1024]{1,0:T(8,128)(2,1)S(1)} collective-permute-done((bf16[320,1024]{1,0:T(8,128)(2,1)S(1)}, bf16[320,1024]{1,0:T(8,128)(2,1)S(1)}, u32[]{:S(2)}, u32[]{:S(2)}) %collective-permute-start.41) | collective-permute-done | bytes 655392 | tf_op jit(solution)/shard_map/ppermute | solution.py:315
  376.9 14.9 %attend.3 = bf16[1024,256]{1,0:T(8,128)(2,1)} custom-call(s32[1]{0:T(128)} %bitcast.36.prefix_ref, bf16[1024,768]{1,0:T(8,128)(2,1)} %bitcast.458), custom_call_target="tpu_custom_call" | custom-call | flops 1073741824 | bytes 3145728 | tf_op jit(solution)/shard_map/attend/pallas_call | solution.py:232
  400.0 37.1 %all-gather.23.cloned.1.call-done = bf16[2048,1024]{1,0:T(8,128)(2,1)} async-done(((bf16[1024,1024]{1,0:T(8,128)(2,1)}), bf16[2048,1024]{1,0:T(8,128)(2,1)}) %all-gather.23.cloned.1.call-update) | async-done | bytes 4194320 | tf_op jit(solution)/shard_map/all_gather | solution.py:324
  437.1 7.8 fusion.237
  455.5 10.0 multiply_convert_fusion.2
  505.9 79.7 %collective-permute-done.44 = bf16[320,1024]{1,0:T(8,128)(2,1)} collective-permute-done((bf16[320,1024]{1,0:T(8,128)(2,1)}, bf16[320,1024]{1,0:T(8,128)(2,1)}, u32[]{:S(2)}, u32[]{:S(2)}) %collective-permute-start.44) | collective-permute-done | bytes 655392 | tf_op jit(solution)/shard_map/ppermute | solution.py:315
  622.5 52.3 %collective-permute-done.48 = bf16[320,1024]{1,0:T(8,128)(2,1)S(1)} collective-permute-done((bf16[320,1024]{1,0:T(8,128)(2,1)S(1)}, bf16[320,1024]{1,0:T(8,128)(2,1)S(1)}, u32[]{:S(2)}, u32[]{:S(2)}) %collective-permute-start.48) | collective-permute-done | bytes 655392 | tf_op jit(solution)/shard_map/ppermute | solution.py:315
  686.7 8.0 all-to-all-done.8
  696.3 12.0 fusion.36
  708.4 7.3 multiply_reduce_fusion.17
  751.4 7.5 pad_maximum_fusion
  781.3 20.8 %collective-permute-done.49 = bf16[320,1024]{1,0:T(8,128)(2,1)} collective-permute-done((bf16[320,1024]{1,0:T(8,128)(2,1)}, bf16[320,1024]{1,0:T(8,128)(2,1)}, u32[]{:S(2)}, u32[]{:S(2)}) %collective-permute-start.49) | collective-permute-done | bytes 655392 | tf_op jit(solution)/shard_map/ppermute | solution.py:315
  805.4 65.2 %all-to-all-done.10 = bf16[4,256,256]{2,1,0:T(8,128)(2,1)S(1)} async-done(((bf16[4,256,256]{2,1,0:T(8,128)(2,1)}), bf16[4,256,256]{2,1,0:T(8,128)(2,1)S(1)}, u32[]{:S(2)}, u32[]{:S(2)}) %all-to-all-start.10) | async-done | bytes 524320 | tf_op jit(solution)/shard_map/all_to_all | solution.py:181
  875.0 25.0 %attend_back.2 = bf16[1024,768]{1,0:T(8,128)(2,1)} custom-call(s32[1]{0:T(128)} %bitcast.1.prefix_ref, bf16[1024,768]{1,0:T(8,128)(2,1)} %bitcast.17.x_ref, bf16[1024,256]{1,0:T(8,128)(2,1)} %bitcast.477), custom_call_target="tpu_custom_call" | custom-call | flops 2684354560 | bytes 7864320 | tf_op jit(solution)/shard_map/attend_back/pallas_call | solution.py:290
  938.0 7.6 pad_maximum_fusion.1
  960.7 7.7 all-to-all-done.9
  974.7 8.3 all-to-all-done.13
  998.8 40.3 %all-to-all-done.11 = bf16[4,256,768]{1,2,0:T(8,128)(2,1)} async-done(((bf16[4,256,768]{1,2,0:T(8,128)(2,1)}), bf16[4,256,768]{1,2,0:T(8,128)(2,1)}, u32[]{:S(2)}, u32[]{:S(2)}) %all-to-all-start.11) | async-done | bytes 1572896 | tf_op jit(solution)/shard_map/all_to_all | solution.py:181
  1052.0 11.5 fusion.43
  1063.5 7.3 convolution_convert_fusion
  1131.5 24.6 %attend_back.3 = bf16[1024,768]{1,0:T(8,128)(2,1)} custom-call(s32[1]{0:T(128)} %bitcast.36.prefix_ref, bf16[1024,768]{1,0:T(8,128)(2,1)} %bitcast.459, bf16[1024,256]{1,0:T(8,128)(2,1)} %bitcast.86.grad_ref), custom_call_target="tpu_custom_call" | custom-call | flops 2684354560 | bytes 7864320 | tf_op jit(solution)/shard_map/attend_back/pallas_call | solution.py:290
  1179.1 19.3 %all-to-all-done.15 = bf16[4,256,768]{1,2,0:T(8,128)(2,1)} async-done(((bf16[4,256,768]{1,2,0:T(8,128)(2,1)}), bf16[4,256,768]{1,2,0:T(8,128)(2,1)}, u32[]{:S(2)}, u32[]{:S(2)}) %all-to-all-start.15) | async-done | bytes 1572896 | tf_op jit(solution)/shard_map/all_to_all | solution.py:181
  1240.7 11.1 collective-permute-done.55
  1287.0 21.0 %reduce-scatter.10.cloned.1.call-done = bf16[32,4096]{1,0:T(8,128)(2,1)} async-done(((bf16[128,4096]{1,0:T(8,128)(2,1)}), bf16[32,4096]{1,0:T(8,128)(2,1)}) %reduce-scatter.10.cloned.1.call-update) | async-done | bytes 262160 | tf_op jit(solution)/shard_map/reduce_scatter | solution.py:169
  (904 shorter events, 635.3 us)
Async XLA Ops:
  7.2 117.1 %all-gather.13.cloned.1.call-start = ((), (), s32[]{:S(2)}) async-start(), calls=%async_computation.26 | async-start | bytes 1310720 | tf_op jit(solution)/shard_map/all_gather | solution.py:126
  7.9 118.0 %all-gather.15.cloned.1.call-start = ((), (), s32[]{:S(2)}) async-start(), calls=%async_computation.27 | async-start | bytes 1310720 | tf_op jit(solution)/shard_map/all_gather | solution.py:126
  17.2 281.5 %all-gather.17.cloned.1.call-start = ((), (), s32[]{:S(2)}) async-start(), calls=%async_computation.28 | async-start | bytes 6291456 | tf_op jit(solution)/shard_map/all_gather | solution.py:324
  37.9 265.4 %all-gather.21.cloned.1.call-start = ((), (), s32[]{:S(2)}) async-start(), calls=%async_computation.30 | async-start | bytes 6291456 | tf_op jit(solution)/shard_map/all_gather | solution.py:324
  38.5 320.4 %all-gather.19.cloned.1.call-start = ((), (), s32[]{:S(2)}) async-start(), calls=%async_computation.29 | async-start | bytes 6291456 | tf_op jit(solution)/shard_map/all_gather | solution.py:324
  166.5 74.8 %collective-permute-start.22 = (bf16[4,32,4096]{2,1,0:T(8,128)(2,1)}, bf16[4,32,4096]{2,1,0:T(8,128)(2,1)}, u32[]{:S(2)}, u32[]{:S(2)}) collective-permute-start(bf16[4,32,4096]{2,1,0:T(8,128)(2,1)} %bitcast.467), channel_id=1, source_target_pairs={{0,2},{1,3},{2,0},{3,1},{4,6},{5,7},{6,4},{7,5},{8,10},{9,11},{10,... | collective-permute-start | bytes 3145736 | tf_op jit(solution)/shard_map/ppermute | solution.py:50
  168.2 73.7 %collective-permute-start.24 = (bf16[4,128,1024]{2,1,0:T(8,128)(2,1)}, bf16[4,128,1024]{2,1,0:T(8,128)(2,1)}, u32[]{:S(2)}, u32[]{:S(2)}) collective-permute-start(bf16[4,128,1024]{2,1,0:T(8,128)(2,1)} %bitcast.471), channel_id=1, source_target_pairs={{0,4},{1,5},{2,6},{3,7},{4,0},{5,1},{6,2},{7,3},{8,12},{9,13},{10,... | collective-permute-start | bytes 3145736 | tf_op jit(solution)/shard_map/ppermute | solution.py:50
  170.5 78.6 %collective-permute-start.23 = (bf16[4,32,4096]{2,1,0:T(8,128)(2,1)}, bf16[4,32,4096]{2,1,0:T(8,128)(2,1)}, u32[]{:S(2)}, u32[]{:S(2)}) collective-permute-start(bf16[4,32,4096]{2,1,0:T(8,128)(2,1)} %collective-permute-done.20.refs_1_), channel_id=1, source_target_pairs={{0,2},{1,3},{2,0},{3,1},{4,6},{5,7},{6,4},{7,5},{8,10},{9,11},{10,... | collective-permute-start | bytes 3145736 | tf_op jit(solution)/shard_map/ppermute | solution.py:50
  171.1 78.5 %collective-permute-start.25 = (bf16[4,128,1024]{2,1,0:T(8,128)(2,1)}, bf16[4,128,1024]{2,1,0:T(8,128)(2,1)}, u32[]{:S(2)}, u32[]{:S(2)}) collective-permute-start(bf16[4,128,1024]{2,1,0:T(8,128)(2,1)} %collective-permute-done.21.refs_1_), channel_id=1, source_target_pairs={{0,4},{1,5},{2,6},{3,7},{4,0},{5,1},{6,2},{7,3},{8,12},{9,13},{10,... | collective-permute-start | bytes 3145736 | tf_op jit(solution)/shard_map/ppermute | solution.py:50
  190.1 54.8 %all-to-all-start.1 = ((bf16[4,256,256]{1,2,0:T(8,128)(2,1)}), bf16[4,256,256]{1,2,0:T(8,128)(2,1)}, u32[]{:S(2)}, u32[]{:S(2)}) async-start(bf16[4,256,256]{1,2,0:T(8,128)(2,1)} %copy.55), calls=%async_computation.1 | async-start | bytes 1048576 | tf_op jit(solution)/shard_map/all_to_all | solution.py:181
  195.7 241.4 %all-gather.23.cloned.1.call-start = ((), (), s32[]{:S(2)}) async-start(), calls=%async_computation.31 | async-start | bytes 6291456 | tf_op jit(solution)/shard_map/all_gather | solution.py:324
  260.2 423.9 %collective-permute-start.50 = (bf16[320,1024]{1,0:T(8,128)(2,1)}, bf16[320,1024]{1,0:T(8,128)(2,1)}, u32[]{:S(2)}, u32[]{:S(2)}) collective-permute-start(bf16[320,1024]{1,0:T(8,128)(2,1)} %bitcast.73), channel_id=1, source_target_pairs={{0,16},{8,24},{16,0},{24,8},{1,17},{9,25},{17,1},{25,9},{2,18},{10... | collective-permute-start | bytes 1966088 | tf_op jit(solution)/shard_map/ppermute | solution.py:315
  316.6 59.1 %all-to-all-start.3 = ((bf16[4,256,768]{2,1,0:T(8,128)(2,1)}), bf16[4,256,768]{2,1,0:T(8,128)(2,1)S(1)}, u32[]{:S(2)}, u32[]{:S(2)}) async-start(bf16[4,256,768]{2,1,0:T(8,128)(2,1)} %bitcast.387), calls=%async_computation.3 | async-start | bytes 3145728 | tf_op jit(solution)/shard_map/all_to_all | solution.py:181
  365.9 79.0 %collective-permute-start.42 = (bf16[640,1024]{1,0:T(8,128)(2,1)}, bf16[640,1024]{1,0:T(8,128)(2,1)}, u32[]{:S(2)}, u32[]{:S(2)}) collective-permute-start(bf16[640,1024]{1,0:T(8,128)(2,1)} %convolution_convert_fusion.13), channel_id=1, source_target_pairs={{0,16},{8,24},{16,0},{24,8},{1,17},{9,25},{17,1},{25,9},{2,18},{10... | collective-permute-start | bytes 3932168 | tf_op jit(solution)/shard_map/ppermute | solution.py:315
  393.9 55.7 %all-to-all-start.4 = ((bf16[4,256,256]{1,2,0:T(8,128)(2,1)}), bf16[4,256,256]{1,2,0:T(8,128)(2,1)}, u32[]{:S(2)}, u32[]{:S(2)}) async-start(bf16[4,256,256]{1,2,0:T(8,128)(2,1)} %copy.57), calls=%async_computation.4 | async-start | bytes 1048576 | tf_op jit(solution)/shard_map/all_to_all | solution.py:181
  495.6 99.5 %collective-permute-start.47 = (bf16[640,1024]{1,0:T(8,128)(2,1)}, bf16[640,1024]{1,0:T(8,128)(2,1)}, u32[]{:S(2)}, u32[]{:S(2)}) collective-permute-start(bf16[640,1024]{1,0:T(8,128)(2,1)} %convolution_convert_fusion.10), channel_id=1, source_target_pairs={{0,16},{8,24},{16,0},{24,8},{1,17},{9,25},{17,1},{25,9},{2,18},{10... | collective-permute-start | bytes 3932168 | tf_op jit(solution)/shard_map/ppermute | solution.py:315
  499.7 85.8 %collective-permute-start.44 = (bf16[320,1024]{1,0:T(8,128)(2,1)}, bf16[320,1024]{1,0:T(8,128)(2,1)}, u32[]{:S(2)}, u32[]{:S(2)}) collective-permute-start(bf16[320,1024]{1,0:T(8,128)(2,1)} %bitcast.54), channel_id=1, source_target_pairs={{0,16},{8,24},{16,0},{24,8},{1,17},{9,25},{17,1},{25,9},{2,18},{10... | collective-permute-start | bytes 1966088 | tf_op jit(solution)/shard_map/ppermute | solution.py:315
  615.5 59.2 %collective-permute-start.48 = (bf16[320,1024]{1,0:T(8,128)(2,1)S(1)}, bf16[320,1024]{1,0:T(8,128)(2,1)S(1)}, u32[]{:S(2)}, u32[]{:S(2)}) collective-permute-start(bf16[320,1024]{1,0:T(8,128)(2,1)S(1)} %slice.433), channel_id=1, source_target_pairs={{0,16},{8,24},{16,0},{24,8},{1,17},{9,25},{17,1},{25,9},{2,18},{10... | collective-permute-start | bytes 1966088 | tf_op jit(solution)/shard_map/ppermute | solution.py:315
  619.6 96.7 %collective-permute-start.45 = (bf16[640,1024]{1,0:T(8,128)(2,1)}, bf16[640,1024]{1,0:T(8,128)(2,1)}, u32[]{:S(2)}, u32[]{:S(2)}) collective-permute-start(bf16[640,1024]{1,0:T(8,128)(2,1)} %convolution_convert_fusion.11), channel_id=1, source_target_pairs={{0,16},{8,24},{16,0},{24,8},{1,17},{9,25},{17,1},{25,9},{2,18},{10... | collective-permute-start | bytes 3932168 | tf_op jit(solution)/shard_map/ppermute | solution.py:315
  683.6 315.2 %reduce-scatter.6.cloned.1.call-start = ((), (), s32[]{:S(2)}) async-start(), calls=%async_computation.21 | async-start | bytes 12582912 | tf_op jit(solution)/shard_map/reduce_scatter | solution.py:329
  773.2 126.7 %collective-permute-start.51 = (bf16[640,1024]{1,0:T(8,128)(2,1)}, bf16[640,1024]{1,0:T(8,128)(2,1)S(1)}, u32[]{:S(2)}, u32[]{:S(2)}) collective-permute-start(bf16[640,1024]{1,0:T(8,128)(2,1)} %convolution_convert_fusion.7), channel_id=1, source_target_pairs={{0,16},{8,24},{16,0},{24,8},{1,17},{9,25},{17,1},{25,9},{2,18},{10... | collective-permute-start | bytes 3932168 | tf_op jit(solution)/shard_map/ppermute | solution.py:315
  777.7 92.9 %all-to-all-start.10 = ((bf16[4,256,256]{2,1,0:T(8,128)(2,1)}), bf16[4,256,256]{2,1,0:T(8,128)(2,1)S(1)}, u32[]{:S(2)}, u32[]{:S(2)}) async-start(bf16[4,256,256]{2,1,0:T(8,128)(2,1)} %bitcast.393), calls=%async_computation.10 | async-start | bytes 1048576 | tf_op jit(solution)/shard_map/all_to_all | solution.py:181
  871.4 81.7 %all-to-all-start.5 = ((bf16[8,40,1024]{2,1,0:T(8,128)(2,1)}), bf16[8,40,1024]{2,1,0:T(8,128)(2,1)S(1)}, u32[]{:S(2)}, u32[]{:S(2)}) async-start(bf16[8,40,1024]{2,1,0:T(8,128)(2,1)} %bitcast.44), calls=%async_computation.5 | async-start | bytes 1310720 | tf_op jit(solution)/shard_map/all_to_all | solution.py:187
  874.9 304.2 %reduce-scatter.8.cloned.1.call-start = ((), (), s32[]{:S(2)}) async-start(), calls=%async_computation.22 | async-start | bytes 12582912 | tf_op jit(solution)/shard_map/reduce_scatter | solution.py:329
  983.8 55.3 %all-to-all-start.11 = ((bf16[4,256,768]{1,2,0:T(8,128)(2,1)}), bf16[4,256,768]{1,2,0:T(8,128)(2,1)}, u32[]{:S(2)}, u32[]{:S(2)}) async-start(bf16[4,256,768]{1,2,0:T(8,128)(2,1)} %copy.59), calls=%async_computation.11 | async-start | bytes 3145728 | tf_op jit(solution)/shard_map/all_to_all | solution.py:181
  1052.0 57.8 %collective-permute-start.53 = (bf16[4,2,2,128,1024]{4,3,2,1,0:T(8,128)(2,1)}, bf16[4,2,2,128,1024]{4,3,2,1,0:T(8,128)(2,1)}, u32[]{:S(2)}, u32[]{:S(2)}) collective-permute-start(bf16[4,2,2,128,1024]{4,3,2,1,0:T(8,128)(2,1)} %dynamic-slice_bitcast_fusion.1), channel_id=1, source_target_pairs={{0,1},{1,0},{2,3},{3,2},{4,5},{5,4},{6,7},{7,6},{8,9},{9,8},{10,11... | collective-permute-start | bytes 12582920 | tf_op jit(solution)/shard_map/ppermute | solution.py:50
  1117.9 51.6 %collective-permute-start.66 = (bf16[4,2,128,1024]{3,2,1,0:T(8,128)(2,1)}, bf16[4,2,128,1024]{3,2,1,0:T(8,128)(2,1)S(1)}, u32[]{:S(2)}, u32[]{:S(2)}) collective-permute-start(bf16[4,2,128,1024]{3,2,1,0:T(8,128)(2,1)} %dynamic-slice_bitcast_fusion.2), channel_id=1, source_target_pairs={{0,2},{1,3},{2,0},{3,1},{4,6},{5,7},{6,4},{7,5},{8,10},{9,11},{10,... | collective-permute-start | bytes 6291464 | tf_op jit(solution)/shard_map/ppermute | solution.py:50
  1163.8 119.6 %reduce-scatter.14.cloned.1.call-start = ((), (), s32[]{:S(2)}) async-start(), calls=%async_computation.25 | async-start | bytes 1310720 | tf_op jit(solution)/shard_map/reduce_scatter | solution.py:169
  1177.7 59.8 %collective-permute-start.65 = (bf16[4,32,4096]{2,1,0:T(8,128)(2,1)}, bf16[4,32,4096]{2,1,0:T(8,128)(2,1)}, u32[]{:S(2)}, u32[]{:S(2)}) collective-permute-start(bf16[4,32,4096]{2,1,0:T(8,128)(2,1)} %dynamic-slice_bitcast_fusion.7), channel_id=1, source_target_pairs={{0,2},{1,3},{2,0},{3,1},{4,6},{5,7},{6,4},{7,5},{8,10},{9,11},{10,... | collective-permute-start | bytes 3145736 | tf_op jit(solution)/shard_map/ppermute | solution.py:50
  1220.7 51.4 %collective-permute-start.68 = (f32[2,1024]{1,0:T(2,128)S(1)}, f32[2,1024]{1,0:T(2,128)S(1)}, u32[]{:S(2)}, u32[]{:S(2)}) collective-permute-start(f32[2,1024]{1,0:T(2,128)S(1)} %maximum_add_fusion), channel_id=1, source_target_pairs={{0,8},{8,16},{16,24},{24,0},{1,9},{9,17},{17,25},{25,1},{2,10},{10... | collective-permute-start | bytes 24584 | tf_op jit(solution)/shard_map/ppermute | solution.py:55
  1225.5 59.8 %reduce-scatter.12.cloned.1.call-start = ((), (), s32[]{:S(2)}) async-start(), calls=%async_computation.24 | async-start | bytes 1310720 | tf_op jit(solution)/shard_map/reduce_scatter | solution.py:169
  1240.6 67.4 %reduce-scatter.10.cloned.1.call-start = ((), (), s32[]{:S(2)}) async-start(), calls=%async_computation.23 | async-start | bytes 1310720 | tf_op jit(solution)/shard_map/reduce_scatter | solution.py:169
  (268 other events, 5379.2 us)
Sparse Core Ops, SparseCore 0:
  9.6 40.9 all-gather.12
  52.2 28.1 all-gather.14
  81.9 81.3 all-gather.16
  164.7 79.1 all-gather.20
  245.3 76.2 all-gather.18
  323.0 114.0 all-gather.22
  759.0 147.0 reduce-scatter.5
  945.8 124.0 reduce-scatter.7
  1225.6 26.3 reduce-scatter.13
  1254.1 25.7 reduce-scatter.11
  1282.2 25.7 reduce-scatter.9
